TPU v7x, 32 devices: a whole 2x2x4 slice. The times are simulated.
32 devices in a mesh: tower: 2 (over core), batch: 16 (over z, y, x).
Axes of the slice: x: 2, y: 2, z: 4, core: 2. Of those that a mesh axis runs over, the one named last changes fastest.
Arguments:
- tokens: bfloat16 [2, 32768, 768], P('tower', 'batch'), may hold values from -6 to 6
- lengths: int32 [2, 64], P('tower', 'batch'), may hold values from 64 to 512, as said below
- prefixes: int32 [2, 64], P('tower', 'batch'), may hold values from 1 to 32
- positives: int32 [64], replicated, may hold values from 0 to 63, each once
- gain_attention: float32 [768], replicated, may hold values from 0.5 to 1.5
- query_weight: bfloat16 [768, 768], replicated, may hold values from -0.02734375 to 0.02734375
- key_weight: bfloat16 [768, 768], replicated, may hold values from -0.21875 to 0.21875
- value_weight: bfloat16 [768, 768], replicated, may hold values from -0.21875 to 0.21875
- output_weight: bfloat16 [768, 768], replicated, may hold values from -1.75 to 1.75
- bucket_bias: float32 [32, 12], replicated, may hold values from -4 to 4
- gain_feedforward: float32 [768], replicated, may hold values from 0.5 to 1.5
- widen_weight: bfloat16 [768, 3072], replicated, may hold values from -0.21875 to 0.21875
- narrow_weight: bfloat16 [3072, 768], replicated, may hold values from -0.109375 to 0.109375
- gain_final: float32 [768], replicated, may hold values from 0.5 to 1.5
Outputs:
- contrast_loss: float32 [], replicated
- score_gradient: float32 [64, 64], P('batch')
- token_gradient: bfloat16 [2, 32768, 768], P('tower', 'batch')
- grad_attention: float32 [768], replicated
- grad_query: float32 [768, 768], replicated
- grad_key: float32 [768, 768], replicated
- grad_value: float32 [768, 768], replicated
- grad_output: float32 [768, 768], replicated
- grad_bucket: float32 [32, 12], replicated
- grad_feedforward: float32 [768], replicated
- grad_widen: float32 [768, 3072], replicated
- grad_narrow: float32 [3072, 768], replicated
- grad_final: float32 [768], replicated
Inputs may be any that keep to these rules, and one draw needn't show every extreme that they name: `lengths`: sequence 0 of each side uses all 512 positions. `positives`: every document is the positive of exactly one query.
All inputs are finite; a program needn't handle non-finite values.
Results may differ from a plain program's by a relative error of at most 0.025.
The roundings to bfloat16 on the way count: a program that leaves them out, or rounds other values in their place, can miss the bound.
Values sent between devices are 32-bit elements; how exact they have to be, the bound alone decides.
A program may use at most 320 MiB of HBM per device.

v0:
```python
import jax
import jax.numpy as jnp
from jax import lax
from jax.sharding import PartitionSpec as P

epsilon = 1e-06
masked_score = -1000000000.0
score_scale = 100.0
far_steps = (12, 16, 23, 32, 46, 64, 91)
highest = lax.Precision.HIGHEST


def bucket_onehot(slot_len, bucket_count):
    places = jnp.arange(slot_len, dtype=jnp.int32)
    offset = places[None, :] - places[:, None]
    spread = jnp.abs(offset)
    far_bucket = 8 + sum(((spread >= step).astype(jnp.int32) for step in far_steps))
    bucket = jnp.where(spread < 8, spread, far_bucket) + jnp.where(
        offset > 0, bucket_count // 2, 0
    ).astype(jnp.int32)
    labels = jnp.arange(bucket_count, dtype=jnp.int32)
    return (bucket[:, :, None] == labels[None, None, :]).astype(jnp.float32)


def norm_forward(values, scale_vec):
    inverse = lax.rsqrt(jnp.mean(values * values, axis=-1, keepdims=True) + epsilon)
    return (values * inverse * scale_vec, inverse)


def norm_backward(values, inverse, scale_vec, upstream):
    scaled = upstream * scale_vec
    inner_mean = jnp.mean(scaled * values, axis=-1, keepdims=True)
    grad_values = inverse * scaled - values * (inverse * inverse * inverse) * inner_mean
    grad_scale = jnp.sum(upstream * values * inverse, axis=0)
    return (grad_values, grad_scale)


def local(
    tokens,
    lengths,
    prefixes,
    positives,
    gain_attention,
    query_weight,
    key_weight,
    value_weight,
    output_weight,
    bucket_bias,
    gain_feedforward,
    widen_weight,
    narrow_weight,
    gain_final,
):
    seqs = lengths.shape[1]
    rows = tokens.shape[1]
    slot_len = rows // seqs
    width = tokens.shape[2]
    heads = bucket_bias.shape[1]
    head_dim = query_weight.shape[1] // heads
    inner = heads * head_dim
    tokens_f = tokens[0].astype(jnp.float32)
    seq_lengths = lengths[0]
    seq_prefix = prefixes[0]
    onehot = bucket_onehot(slot_len, bucket_bias.shape[0])
    bias = jnp.einsum("ijb,bh->hij", onehot, bucket_bias, precision=highest)
    normed_f, inverse_first = norm_forward(tokens_f, gain_attention)
    normed = normed_f.astype(jnp.bfloat16)

    def project(matrix):
        projected = jnp.dot(normed, matrix, preferred_element_type=jnp.float32).astype(jnp.bfloat16)
        return projected.reshape(seqs, slot_len, heads, head_dim)

    query_all = project(query_weight)
    key_all = project(key_weight)
    value_all = project(value_weight)
    places = jnp.arange(slot_len, dtype=jnp.int32)
    valid = places[None, :] < seq_lengths[:, None]

    def score_block(query_rows, key_rows, valid_keys):
        raw_scores = jnp.einsum(
            "ihd,jhd->hij", query_rows, key_rows, preferred_element_type=jnp.float32
        )
        return jnp.where(valid_keys[None, None, :], raw_scores + bias, masked_score)

    def attend_forward(parts):
        query_rows, key_rows, value_rows, valid_keys = parts
        scores = score_block(query_rows, key_rows, valid_keys)
        row_peak = jnp.max(scores, axis=-1, keepdims=True)
        raised = jnp.exp(scores - row_peak)
        totals = jnp.sum(raised, axis=-1, keepdims=True)
        soft_low = (raised / totals).astype(jnp.bfloat16)
        context = jnp.einsum(
            "hij,jhd->ihd", soft_low, value_rows, preferred_element_type=jnp.float32
        )
        return (context.astype(jnp.bfloat16), (row_peak + jnp.log(totals))[:, :, 0])

    context, log_totals = lax.map(attend_forward, (query_all, key_all, value_all, valid))
    context_flat = context.reshape(rows, inner)
    mixed = tokens_f + jnp.dot(context_flat, output_weight, preferred_element_type=jnp.float32)
    ffn_in_f, inverse_second = norm_forward(mixed, gain_feedforward)
    ffn_in = ffn_in_f.astype(jnp.bfloat16)
    pre_act = jnp.dot(ffn_in, widen_weight, preferred_element_type=jnp.float32)
    hidden = jnp.where(pre_act > 0, pre_act, 0.0).astype(jnp.bfloat16)
    output = mixed + jnp.dot(hidden, narrow_weight, preferred_element_type=jnp.float32)
    final, inverse_third = norm_forward(output, gain_final)
    pool_mask = ((places[None, :] >= seq_prefix[:, None]) & valid).astype(jnp.float32)
    pool_weight = pool_mask / jnp.sum(pool_mask, axis=1, keepdims=True)
    pooled = jnp.sum(final.reshape(seqs, slot_len, width) * pool_weight[:, :, None], axis=1)
    inverse_pool = lax.rsqrt(jnp.sum(pooled * pooled, axis=-1, keepdims=True) + epsilon)
    unit = pooled * inverse_pool
    gathered = lax.all_gather(unit, ("tower", "batch"), axis=0, tiled=True)
    total_seqs = gathered.shape[0] // 2
    query_units = gathered[:total_seqs]
    doc_units = gathered[total_seqs:]
    scores = score_scale * jnp.dot(query_units, doc_units.T, precision=highest)
    labels = jnp.arange(total_seqs, dtype=jnp.int32)
    target = (positives[:, None] == labels[None, :]).astype(jnp.float32)
    row_peak = jnp.max(scores, axis=1, keepdims=True)
    row_raised = jnp.exp(scores - row_peak)
    row_sum = jnp.sum(row_raised, axis=1, keepdims=True)
    col_peak = jnp.max(scores, axis=0, keepdims=True)
    col_raised = jnp.exp(scores - col_peak)
    col_sum = jnp.sum(col_raised, axis=0, keepdims=True)
    loss_value = (
        0.5 * jnp.sum(row_peak[:, 0] + jnp.log(row_sum[:, 0]))
        + 0.5 * jnp.sum(col_peak[0] + jnp.log(col_sum[0]))
        - jnp.sum(target * scores)
    )
    score_grad = 0.5 * row_raised / row_sum + 0.5 * col_raised / col_sum - target
    tower = lax.axis_index("tower")
    first_row = lax.axis_index("batch") * seqs
    my_rows = lax.dynamic_slice_in_dim(score_grad, first_row, seqs, 0)
    my_cols = lax.dynamic_slice_in_dim(score_grad, first_row, seqs, 1)
    grad_as_query = score_scale * jnp.dot(my_rows, doc_units, precision=highest)
    grad_as_doc = score_scale * jnp.dot(my_cols.T, query_units, precision=highest)
    grad_unit = jnp.where(tower == 0, grad_as_query, grad_as_doc)
    cubed = inverse_pool * inverse_pool * inverse_pool
    grad_pooled = inverse_pool * grad_unit - pooled * cubed * jnp.sum(
        grad_unit * pooled, axis=-1, keepdims=True
    )
    grad_fin = (pool_weight[:, :, None] * grad_pooled[:, None, :]).reshape(rows, width)
    grad_out, grad_final = norm_backward(output, inverse_third, gain_final, grad_fin)
    grad_branch = grad_out.astype(jnp.bfloat16)
    grad_narrow = jnp.einsum("tf,td->fd", hidden, grad_branch, preferred_element_type=jnp.float32)
    grad_hidden = jnp.einsum(
        "td,fd->tf", grad_branch, narrow_weight, preferred_element_type=jnp.float32
    )
    grad_pre = jnp.where(pre_act > 0, grad_hidden, 0.0).astype(jnp.bfloat16)
    grad_widen = jnp.einsum("td,tf->df", ffn_in, grad_pre, preferred_element_type=jnp.float32)
    grad_ffn_in = jnp.einsum(
        "tf,df->td", grad_pre, widen_weight, preferred_element_type=jnp.float32
    )
    grad_mixed_norm, grad_feedforward = norm_backward(
        mixed, inverse_second, gain_feedforward, grad_ffn_in
    )
    grad_mixed = grad_out + grad_mixed_norm
    grad_attn = grad_mixed.astype(jnp.bfloat16)
    grad_output = jnp.einsum(
        "ti,td->id", context_flat, grad_attn, preferred_element_type=jnp.float32
    )
    grad_context = jnp.einsum(
        "td,id->ti", grad_attn, output_weight, preferred_element_type=jnp.float32
    )
    grad_context = grad_context.astype(jnp.bfloat16).reshape(seqs, slot_len, heads, head_dim)

    def attend_backward(bias_total, parts):
        query_rows, key_rows, value_rows, valid_keys, log_rows, context_grad = parts
        scores_here = score_block(query_rows, key_rows, valid_keys)
        soft = jnp.exp(scores_here - log_rows[:, :, None])
        soft_low = soft.astype(jnp.bfloat16)
        value_part = jnp.einsum(
            "hij,ihd->jhd", soft_low, context_grad, preferred_element_type=jnp.float32
        )
        grad_soft = jnp.einsum(
            "ihd,jhd->hij", context_grad, value_rows, preferred_element_type=jnp.float32
        )
        grad_scores = soft * (grad_soft - jnp.sum(grad_soft * soft, axis=-1, keepdims=True))
        scores_low = grad_scores.astype(jnp.bfloat16)
        query_part = jnp.einsum(
            "hij,jhd->ihd", scores_low, key_rows, preferred_element_type=jnp.float32
        )
        key_part = jnp.einsum(
            "hij,ihd->jhd", scores_low, query_rows, preferred_element_type=jnp.float32
        )
        return (
            bias_total + grad_scores,
            (
                query_part.astype(jnp.bfloat16),
                key_part.astype(jnp.bfloat16),
                value_part.astype(jnp.bfloat16),
            ),
        )

    bias_total, (query_grads, key_grads, value_grads) = lax.scan(
        attend_backward,
        jnp.zeros(bias.shape, jnp.float32),
        (query_all, key_all, value_all, valid, log_totals, grad_context),
    )
    query_grads = query_grads.reshape(rows, inner)
    key_grads = key_grads.reshape(rows, inner)
    value_grads = value_grads.reshape(rows, inner)
    grad_bucket = jnp.einsum("ijb,hij->bh", onehot, bias_total, precision=highest)
    grad_query = jnp.einsum("td,ti->di", normed, query_grads, preferred_element_type=jnp.float32)
    grad_key = jnp.einsum("td,ti->di", normed, key_grads, preferred_element_type=jnp.float32)
    grad_value = jnp.einsum("td,ti->di", normed, value_grads, preferred_element_type=jnp.float32)
    grad_normed = (
        jnp.einsum("ti,di->td", query_grads, query_weight, preferred_element_type=jnp.float32)
        + jnp.einsum("ti,di->td", key_grads, key_weight, preferred_element_type=jnp.float32)
        + jnp.einsum("ti,di->td", value_grads, value_weight, preferred_element_type=jnp.float32)
    )
    grad_tokens_norm, grad_attention = norm_backward(
        tokens_f, inverse_first, gain_attention, grad_normed
    )
    token_gradient = (grad_mixed + grad_tokens_norm).astype(jnp.bfloat16)[None]
    (
        sum_attention,
        sum_query,
        sum_key,
        sum_value,
        sum_output,
        sum_bucket,
        sum_feedforward,
        sum_widen,
        sum_narrow,
        sum_final,
    ) = lax.psum(
        (
            grad_attention,
            grad_query,
            grad_key,
            grad_value,
            grad_output,
            grad_bucket,
            grad_feedforward,
            grad_widen,
            grad_narrow,
            grad_final,
        ),
        ("tower", "batch"),
    )
    return (
        loss_value,
        my_rows,
        token_gradient,
        sum_attention,
        sum_query,
        sum_key,
        sum_value,
        sum_output,
        sum_bucket,
        sum_feedforward,
        sum_widen,
        sum_narrow,
        sum_final,
    )


def solution(mesh):
    placed = (
        P("tower", "batch", None),
        P("tower", "batch"),
        P("tower", "batch"),
        P(),
        P(),
        P(),
        P(),
        P(),
        P(),
        P(),
        P(),
        P(),
        P(),
        P(),
    )
    return jax.shard_map(
        local,
        mesh=mesh,
        in_specs=placed,
        out_specs=(
            P(),
            P("batch", None),
            P("tower", "batch", None),
            P(),
            P(),
            P(),
            P(),
            P(),
            P(),
            P(),
            P(),
            P(),
            P(),
        ),
        check_vma=False,
    )
```

profile of v0, /device:TPU:0, one launch (start us, length us, event | category | flops | bytes accessed | tf_op | source)
XLA Modules:
  0.0 1078.6 jit_solution(5208512605683882147)
XLA Ops:
  74.6 13.7 %fusion.55 = f32[12,512,512]{2,0,1:T(8,128)} fusion(s32[512,512]{1,0:T(8,128)S(1)} %fusion.93, f32[32,12]{0,1:T(8,128)S(1)} %copy-done.36), kind=kOutput, calls=%fused_computation.65 | convolution fusion | flops 1216348160 | bytes 13633024 | tf_op jit(solution)/shard_map/ijb,bh->hij/dot_general | solution.py:65
  88.2 17.3 %copy.73 = f32[12,512,512]{1,2,0:T(8,128)} copy(f32[12,512,512]{2,0,1:T(8,128)} %fusion.55) | data formatting | bytes 25165824 | tf_op jit(solution)/shard_map/while | solution.py:97
  107.6 59.8 %while.29 = (s32[]{:T(128)}, bf16[4,512,12,64]{1,3,2,0:T(8,128)(2,1)}, f32[4,12,512]{2,1,0:T(8,128)}, bf16[4,512,12,64]{1,3,2,0:T(8,128)(2,1)}, pred[4,512]{1,0:...) while((s32[]{:T(128)}, ...), condition=%wide.region_4.5_spmd, body=%wide.region_1.4_spmd.sunk | while | flops 830859264 | bytes 53685868 | solution.py:97
  108.2 8.0 fusion.177
  123.0 8.0 fusion.177
  137.7 8.0 fusion.177
  152.5 8.0 fusion.177
  179.0 13.7 %fusion.113 = f32[2048,3072]{1,0:T(8,128)} fusion(bf16[768,3072]{1,0:T(8,128)(2,1)S(1)} %bitcast.270, f32[2048,768]{1,0:T(8,128)S(1)} %get-tuple-element.306, f32[768]{0:T(1024)S(1)} %copy-done.46, f32[2048]{0:T(1024)S(1)} %get-tuple-element.298), kind=kOutput, calls=%fused_computation.170 | convolution fusion | flops 9668395008 | bytes 36187136 | tf_op jit(solution)/shard_map/dot_general | solution.py:102
  192.7 19.2 %multiply_reduce_fusion.4 = (f32[2048]{0:T(1024)S(1)}, f32[2048,768]{1,0:T(8,128)}) fusion(f32[2048,768]{1,0:T(8,128)} %copy-done.16, bf16[3072,768]{1,0:T(8,128)(2,1)} %param.30, f32[2048,3072]{1,0:T(8,128)} %fusion.113), kind=kOutput, calls=%fused_computation.101 | convolution fusion | flops 9687267328 | bytes 42475520 | tf_op jit(solution)/shard_map/dot_general | solution.py:104
  215.5 72.1 %all-gather = f32[32,4,768]{2,1,0:T(4,128)S(1)} all-gather(f32[1,4,768]{2,1,0:T(4,128)S(1)} %multiply_bitcast_fusion), channel_id=1, replica_groups=mesh['tower'=2,'batch'=16] {'tower','batch'}, dimensions={0}, use_global_device_ids=true | all-gather | bytes 405504 | tf_op jit(solution)/shard_map/all_gather | solution.py:111
  300.3 18.3 %fusion.83 = f32[3072,768]{1,0:T(8,128)} fusion(bf16[2048,768]{1,0:T(8,128)(2,1)} %fusion.82, f32[2048,3072]{1,0:T(8,128)} %fusion.113), kind=kOutput, calls=%fused_computation.110 | convolution fusion | flops 9682550784 | bytes 37748736 | tf_op jit(solution)/shard_map/tf,td->fd/dot_general | solution.py:144
  318.5 20.8 %fusion.52 = bf16[2048,3072]{1,0:T(8,128)(2,1)} fusion(f32[2048,3072]{1,0:T(8,128)} %fusion.113, bf16[2048,768]{1,0:T(8,128)(2,1)} %fusion.82, bf16[3072,768]{1,0:T(8,128)(2,1)} %param.30), kind=kOutput, calls=%fused_computation.62 | convolution fusion | flops 9682550784 | bytes 45613056 | tf_op jit(solution)/shard_map/td,fd->tf/dot_general | solution.py:145
  339.4 17.4 %multiply_reduce_fusion.1 = (f32[768]{0:T(1024)}, f32[2048]{0:T(1024)S(1)}, f32[2048,768]{1,0:T(8,128)}) fusion(f32[2048,768]{1,0:T(8,128)S(1)} %bitcast.254, f32[2048]{0:T(1024)S(1)} %get-tuple-element.298, f32[768]{0:T(1024)S(1)} %copy-done.46, bf16[2048,3072]{1,0:T(8,128)(2,1)} %fusion.52, bf16[768,3072]{1,0:T(8,128)(2,1)} %param.29), kind=kOutput, calls=%fused_computation.95 | convolution fusion | flops 9673110528 | bytes 29906944 | tf_op jit(solution)/shard_map/tf,df->td/dot_general | solution.py:150
  356.8 15.6 %fusion.112 = f32[768,3072]{1,0:T(8,128)} fusion(bf16[2048,3072]{1,0:T(8,128)(2,1)} %fusion.52, f32[2048,768]{1,0:T(8,128)S(1)} %bitcast.254, f32[768]{0:T(1024)S(1)} %copy-done.46, f32[2048]{0:T(1024)S(1)} %get-tuple-element.298), kind=kOutput, calls=%fused_computation.169 | convolution fusion | flops 9668395008 | bytes 28322816 | tf_op jit(solution)/shard_map/td,tf->df/dot_general | solution.py:149
  405.7 183.0 %while.30 = (s32[]{:T(128)}, f32[12,512,512]{1,2,0:T(8,128)}, bf16[4,512,12,64]{1,3,2,0:T(8,128)(2,1)}, bf16[4,512,12,64]{1,3,2,0:T(8,128)(2,1)}, bf16[4,512,12,...) while((s32[]{:T(128)}, f32[12,512,512]{1,2,0:T(8,128)}, ...), condition=%wide.region_22.23_spmd.clone, body=%wide.region_20.22_spmd.clone.sunk | while | flops 2049042432 | bytes 177863392 | solution.py:194
  406.5 8.8 subtract_exponential_fusion.5
  425.8 13.5 %fusion.188 = (bf16[12,512,512]{1,2,0:T(8,128)(2,1)}, f32[12,512,512]{1,2,0:T(8,128)}) fusion(f32[12,512,512]{1,2,0:T(8,128)S(1)} %subtract_exponential_fusion.5, f32[12,512,512]{1,2,0:T(8,128)} %get-tuple-element.446, f32[12,512]{1,0:T(8,128)S(1)} %get-tuple-element.447, f32[12,512,512]{1,2,0:T(8,128)} %get-tuple-element.492, pred[]{:T(512)S(6)} %compare.3), kind=kLoop, calls=%fused_computation.24.clone.1 | loop fusion | flops 15728640 | bytes 56647680 | tf_op jit(solution)/shard_map/while/body/eval_jaxpr/convert_element_type | solution.py:178
  449.3 8.8 subtract_exponential_fusion.5
  468.6 17.4 %fusion.188 = (bf16[12,512,512]{1,2,0:T(8,128)(2,1)}, f32[12,512,512]{1,2,0:T(8,128)}) fusion(f32[12,512,512]{1,2,0:T(8,128)S(1)} %subtract_exponential_fusion.5, f32[12,512,512]{1,2,0:T(8,128)} %get-tuple-element.446, f32[12,512]{1,0:T(8,128)S(1)} %get-tuple-element.447, f32[12,512,512]{1,2,0:T(8,128)} %get-tuple-element.492, pred[]{:T(512)S(6)} %compare.3), kind=kLoop, calls=%fused_computation.24.clone.1 | loop fusion | flops 15728640 | bytes 56647680 | tf_op jit(solution)/shard_map/while/body/eval_jaxpr/convert_element_type | solution.py:178
  496.0 8.8 subtract_exponential_fusion.5
  515.3 17.4 %fusion.188 = (bf16[12,512,512]{1,2,0:T(8,128)(2,1)}, f32[12,512,512]{1,2,0:T(8,128)}) fusion(f32[12,512,512]{1,2,0:T(8,128)S(1)} %subtract_exponential_fusion.5, f32[12,512,512]{1,2,0:T(8,128)} %get-tuple-element.446, f32[12,512]{1,0:T(8,128)S(1)} %get-tuple-element.447, f32[12,512,512]{1,2,0:T(8,128)} %get-tuple-element.492, pred[]{:T(512)S(6)} %compare.3), kind=kLoop, calls=%fused_computation.24.clone.1 | loop fusion | flops 15728640 | bytes 56647680 | tf_op jit(solution)/shard_map/while/body/eval_jaxpr/convert_element_type | solution.py:178
  542.6 8.8 subtract_exponential_fusion.5
  561.9 17.4 %fusion.188 = (bf16[12,512,512]{1,2,0:T(8,128)(2,1)}, f32[12,512,512]{1,2,0:T(8,128)}) fusion(f32[12,512,512]{1,2,0:T(8,128)S(1)} %subtract_exponential_fusion.5, f32[12,512,512]{1,2,0:T(8,128)} %get-tuple-element.446, f32[12,512]{1,0:T(8,128)S(1)} %get-tuple-element.447, f32[12,512,512]{1,2,0:T(8,128)} %get-tuple-element.492, pred[]{:T(512)S(6)} %compare.3), kind=kLoop, calls=%fused_computation.24.clone.1 | loop fusion | flops 15728640 | bytes 56647680 | tf_op jit(solution)/shard_map/while/body/eval_jaxpr/convert_element_type | solution.py:178
  617.3 18.7 %copy.84 = f32[12,512,512]{2,0,1:T(8,128)} copy(f32[12,512,512]{1,2,0:T(8,128)} %get-tuple-element.126) | data formatting | bytes 25165824 | tf_op jit(solution)/shard_map/while | solution.py:194
  638.6 8.1 fusion.126
  646.6 7.9 fusion.127
  654.5 17.5 %fusion.92 = f32[32,12]{0,1:T(8,128)S(1)} fusion(f32[12,512,512]{2,0,1:T(8,128)S(1)} %copy-done.2, s32[512,512]{1,0:T(8,128)S(1)} %copy-done.11), kind=kOutput, calls=%fused_computation.121 | convolution fusion | flops 1216348160 | bytes 13633024 | tf_op jit(solution)/shard_map/ijb,hij->bh/dot_general | solution.py:202
  672.1 9.1 fusion.71
  681.2 39.6 %all-reduce = (f32[768]{0:T(1024)}, f32[32,12]{0,1:T(8,128)}, f32[768]{0:T(1024)}, f32[768]{0:T(1024)}) all-reduce(f32[768]{0:T(1024)S(1)} %get-tuple-element.228, f32[32,12]{0,1:T(8,128)S(1)} %fusion.92, f32[768]{0:T(1024)S(1)} %copy-done.47, f32[768]{0:T(1024)S(1)} %copy-done.33), channel_id=1, replica_groups=mesh['tower'=2,'batch'=16] {'tower','batch'}, use_global_device_ids=true, to_apply=%region_25.26 | all-reduce | flops 2688 | bytes 21504 | tf_op jit(solution)/shard_map/psum | solution.py:226
  720.8 8.3 fusion.87
  729.1 320.5 %all-reduce.4.cloned.1.call-done = (f32[768,768]{1,0:T(8,128)}, f32[768,768]{1,0:T(8,128)}, f32[768,768]{1,0:T(8,128)}, f32[768,768]{1,0:T(8,128)}, f32[768,3072]{1,0:T(8,128)}, /*index=5*/f32[3072,768]{1,0:T(8,128)}) async-done(((f32[768,768]{1,0:T(8,128)}, f32[768,768]{1,0:T(8,128)}, f32[768,768]{1,0:T(8,128)}, f32[768,768]{1,0:T(8,128)}, f32[768,3072]{1,0:T(8,128)}, /*index=5*/f32[3072,768]{1,0:T(8,128)}), ...) | async-done | bytes 28311568 | tf_op jit(solution)/shard_map/psum | solution.py:226
  1057.3 9.3 copy.133
  (252 shorter events, 279.7 us)
Async XLA Ops:
  7.2 48.2 %copy-start = (bf16[768,768]{1,0:T(8,128)(2,1)S(1)}, bf16[768,768]{1,0:T(8,128)(2,1)}, u32[]{:S(2)}) copy-start(bf16[768,768]{1,0:T(8,128)(2,1)} %param.25) | copy-start | bytes 3538948
  7.2 1042.5 %all-reduce.4.cloned.1.call-start = ((), (), s32[]{:S(2)}) async-start(), calls=%async_computation | async-start | bytes 56623104 | tf_op jit(solution)/shard_map/psum | solution.py:226
  7.7 66.9 %copy-start.10 = (s32[512,512]{1,0:T(8,128)}, s32[512,512]{1,0:T(8,128)S(1)}, u32[]{:S(2)}) copy-start(s32[512,512]{1,0:T(8,128)S(1)} %fusion.93) | copy-start | bytes 3145732
  12.5 42.9 %copy-start.27 = (f32[2048]{0:T(1024)}, f32[2048]{0:T(1024)S(1)}, u32[]{:S(2)}) copy-start(f32[2048]{0:T(1024)S(1)} %get-tuple-element.296) | copy-start | bytes 24580
  25.4 10.7 copy-start.34
  25.4 10.7 copy-start.52
  64.1 10.5 copy-start.36
  192.7 19.2 %copy-start.29 = (f32[768]{0:T(1024)S(1)}, f32[768]{0:T(1024)}, u32[]{:S(2)}) copy-start(f32[768]{0:T(1024)} %param.31) | copy-start | bytes 9220
  192.7 19.2 %copy-start.31 = (f32[4,512]{1,0:T(4,128)S(1)}, f32[4,512]{1,0:T(4,128)}, u32[]{:S(2)}) copy-start(f32[4,512]{1,0:T(4,128)} %get-tuple-element.302) | copy-start | bytes 24580
  211.9 76.4 %copy-start.48 = (s32[64]{0:T(128)S(1)}, s32[64]{0:T(128)}, u32[]{:S(2)}) copy-start(s32[64]{0:T(128)} %param.21) | copy-start | bytes 772
  211.9 78.2 %copy-start.32 = (f32[1,4,4,128]{3,2,1,0:T(4,128)S(1)}, f32[1,4,4,128]{3,2,1,0:T(4,128)}, u32[]{:S(2)}) copy-start(f32[1,4,4,128]{3,2,1,0:T(4,128)} %get-tuple-element.301) | copy-start | bytes 24580
  295.3 44.0 %slice-start.5 = ((s8[6291456]{0:T(1024)(128)(4,1)}), s8[4194304]{0:T(1024)(128)(4,1)S(1)}, s32[]{:S(2)}) async-start(s8[6291456]{0:T(1024)(128)(4,1)} %bitcast.253), calls=%async_computation.6 | async-start | bytes 8388608
  300.3 39.1 %slice-start.6 = ((s8[6291456]{0:T(1024)(128)(4,1)}), s8[2097152]{0:T(1024)(128)(4,1)S(1)}, s32[]{:S(2)}) async-start(s8[6291456]{0:T(1024)(128)(4,1)} %bitcast.253), calls=%async_computation.7 | async-start | bytes 4194304
  318.5 53.8 %slice-start = ((s8[6291456]{0:T(1024)(128)(4,1)}), s8[2097152]{0:T(1024)(128)(4,1)S(1)}, s32[]{:S(2)}) async-start(s8[6291456]{0:T(1024)(128)(4,1)} %bitcast.243), calls=%async_computation.1 | async-start | bytes 4194304
  339.4 33.0 %slice-start.1 = ((s8[6291456]{0:T(1024)(128)(4,1)}), s8[4194304]{0:T(1024)(128)(4,1)S(1)}, s32[]{:S(2)}) async-start(s8[6291456]{0:T(1024)(128)(4,1)} %bitcast.243), calls=%async_computation.2 | async-start | bytes 8388608
  356.8 15.6 %copy-start.17 = (f32[2048,768]{1,0:T(8,128)S(1)}, f32[2048,768]{1,0:T(8,128)}, u32[]{:S(2)}) copy-start(f32[2048,768]{1,0:T(8,128)} %get-tuple-element.312) | copy-start | bytes 18874372
  406.5 8.8 copy-start.3
  449.3 8.8 copy-start.3
  617.2 18.7 %copy-start.38 = (f32[64]{0:T(128)S(1)}, f32[64]{0:T(128)}, u32[]{:S(2)}) copy-start(f32[64]{0:T(128)} %copy-done.37) | copy-start | bytes 772
  617.2 18.7 %copy-start.40 = (f32[64]{0:T(128)S(1)}, f32[64]{0:T(128)}, u32[]{:S(2)}) copy-start(f32[64]{0:T(128)} %copy-done.39) | copy-start | bytes 772
  617.3 18.7 %copy-start.43 = (f32[64]{0:T(128)S(1)}, f32[64]{0:T(128)}, u32[]{:S(2)}) copy-start(f32[64]{0:T(128)} %copy-done.42) | copy-start | bytes 772
  617.3 18.7 %copy-start.45 = (f32[64]{0:T(128)S(1)}, f32[64]{0:T(128)}, u32[]{:S(2)}) copy-start(f32[64]{0:T(128)} %copy-done.44) | copy-start | bytes 772
  617.3 21.3 %copy-start.51 = (bf16[768,768]{1,0:T(8,128)(2,1)S(1)}, bf16[768,768]{1,0:T(8,128)(2,1)}, u32[]{:S(2)}) copy-start(bf16[768,768]{1,0:T(8,128)(2,1)} %param.23) | copy-start | bytes 3538948
  638.5 16.0 %copy-start.2 = (f32[12,512,512]{2,0,1:T(8,128)S(1)}, f32[12,512,512]{2,0,1:T(8,128)}, u32[]{:S(2)}) copy-start(f32[12,512,512]{2,0,1:T(8,128)} %copy.84) | copy-start | bytes 37748740
  654.5 17.5 %copy-start.8 = (bf16[1,2048,768]{2,1,0:T(8,128)(2,1)S(1)}, bf16[1,2048,768]{2,1,0:T(8,128)(2,1)}, u32[]{:S(2)}) copy-start(bf16[1,2048,768]{2,1,0:T(8,128)(2,1)} %param.18) | copy-start | bytes 9437188
  654.5 17.5 %copy-start.15 = (bf16[96,8,4,512]{3,1,2,0:T(8,128)(2,1)S(1)}, bf16[96,8,4,512]{3,1,2,0:T(8,128)(2,1)}, u32[]{:S(2)}) copy-start(bf16[96,8,4,512]{3,1,2,0:T(8,128)(2,1)} %copy-done.14) | copy-start | bytes 9437188
  672.1 9.1 copy-start.33
  672.1 9.1 copy-start.47
  672.1 48.7 %copy-start.30 = (f32[2048]{0:T(1024)S(1)}, f32[2048]{0:T(1024)}, u32[]{:S(2)}) copy-start(f32[2048]{0:T(1024)} %get-tuple-element.295) | copy-start | bytes 24580
  1055.9 10.7 slice-start.2
  1057.3 9.3 slice-start.3
  1057.3 9.3 slice-start.4
  (37 other events, 191.2 us)
Sparse Core Ops, SparseCore 0:
  617.4 432.2 all-reduce.3
where the time goes:
time: 1080 us
  matrix products  366 us (34%)
  waiting for transfers between devices  321 us (30%)
  local copies, waits for them, and re-layouts  153 us (14%)
  blocking collectives  112 us (10%)
  other arithmetic  109 us (10%)
  between operations  18 us (2%)
    psum x1, waiting for transfers between devices, local(): lax.psum((grad_attention, grad_query, grad_key, grad_value, grad_output,...  321 us
    all_gather x1, blocking collectives, local(): gathered = lax.all_gather(unit, ('tower', 'batch'), axis=0, tiled=True)  72.1 us
    dot_general x8, matrix products, score_block(): jnp.einsum('ihd,jhd->hij', query_rows, key_rows, preferred_element_type=j...  67.1 us
    convert_element_type x4, other arithmetic, attend_backward(): scores_low = grad_scores.astype(jnp.bfloat16)  65.7 us
    psum x1, blocking collectives, local(): lax.psum((grad_attention, grad_query, grad_key, grad_value, grad_output,...  39.6 us
    while x5, local copies, waits for them, and re-layouts, local(): lax.map(attend_forward, (query_all, key_all, value_all, valid))  35 us
    unnamed x132, local copies, waits for them, and re-layouts  34.2 us
    dot_general x4, matrix products, attend_backward(): jnp.einsum('ihd,jhd->hij', context_grad, value_rows, preferred_element_ty...  30 us
  transfers between devices with their start and end apart: 1, of which 1 were waited for; matrix products, arithmetic and copies ran while one was open for 7% of the time, Pallas kernels for 0%

commit v1 on v0

--- a/solution.py
+++ b/solution.py
@@ -1,6 +1,10 @@
+import functools
+
 import jax
 import jax.numpy as jnp
 from jax import lax
+from jax.experimental import pallas as pl
+from jax.experimental.pallas import tpu as pltpu
 from jax.sharding import PartitionSpec as P
 
 epsilon = 1e-06
@@ -8,6 +12,397 @@
 score_scale = 100.0
 far_steps = (12, 16, 23, 32, 46, 64, 91)
 highest = lax.Precision.HIGHEST
+
+MESH = pl.DeviceIdType.MESH
+job_rows = 384
+unit_rows = 128
+
+
+def batch_dims(size):
+    sizes = {16: (2, 2, 4), 64: (4, 4, 4)}[size]
+    strides = (1, sizes[0], sizes[0] * sizes[1])
+    return dict(zip("xyz", zip(strides, sizes)))
+
+
+def place():
+    return lax.axis_index("tower"), lax.axis_index("batch")
+
+
+def gather_kernel(groups, block_ref, out_ref, slots, send_sem, recv_sem, mate_sem):
+    tower, batch = place()
+    barrier = pltpu.get_barrier_semaphore()
+    mate = (1 - tower, batch)
+
+    def peer(step):
+        return tower, lax.rem(batch + step, groups)
+
+    def greet(step, carry):
+        pl.semaphore_signal(barrier, 1, device_id=peer(step), device_id_type=MESH)
+        return carry
+
+    lax.fori_loop(1, groups, greet, 0)
+    pl.semaphore_signal(barrier, 1, device_id=mate, device_id_type=MESH)
+    slots[tower, batch] = block_ref[...]
+    pl.semaphore_wait(barrier, groups)
+
+    def copy(step, owner):
+        return pltpu.make_async_remote_copy(
+            src_ref=block_ref,
+            dst_ref=slots.at[tower, owner],
+            send_sem=send_sem.at[step],
+            recv_sem=recv_sem.at[owner],
+            device_id=peer(step),
+            device_id_type=MESH,
+        )
+
+    def begin(step, carry):
+        copy(step, batch).start()
+        return carry
+
+    def finish(step, carry):
+        copy(step, batch).wait_send()
+        copy(step, peer(step)[1]).wait_recv()
+        return carry
+
+    lax.fori_loop(1, groups, begin, 0)
+    lax.fori_loop(1, groups, finish, 0)
+    side = pltpu.make_async_remote_copy(
+        src_ref=slots.at[tower],
+        dst_ref=slots.at[tower],
+        send_sem=mate_sem.at[0],
+        recv_sem=mate_sem.at[1],
+        device_id=mate,
+        device_id_type=MESH,
+    )
+    side.start()
+    side.wait()
+    out_ref[...] = slots[...]
+
+
+def gather_blocks(block, groups, collective):
+    whole = (2, groups) + block.shape
+    return pl.pallas_call(
+        functools.partial(gather_kernel, groups),
+        out_shape=jax.ShapeDtypeStruct(whole, jnp.float32),
+        in_specs=[pl.BlockSpec(memory_space=pltpu.VMEM)],
+        out_specs=pl.BlockSpec(memory_space=pltpu.VMEM),
+        scratch_shapes=[
+            pltpu.VMEM(whole, jnp.float32),
+            pltpu.SemaphoreType.DMA((groups,)),
+            pltpu.SemaphoreType.DMA((groups,)),
+            pltpu.SemaphoreType.DMA((2,)),
+        ],
+        compiler_params=pltpu.CompilerParams(collective_id=collective, has_side_effects=True),
+        name="gather_blocks",
+    )(block)
+
+
+def both(first, second):
+    if first is None:
+        return second
+    if second is None:
+        return first
+    return jnp.logical_and(first, second)
+
+
+def guarded(condition, action):
+    if condition is None:
+        action()
+    else:
+        pl.when(condition)(action)
+
+
+def plan_unit(order, dims, batch, rows):
+    add, spread = [], []
+    start, active = 0, None
+    for name in order:
+        stride, size = dims[name]
+        coord = lax.rem(batch // stride, size)
+        if size == 4:
+            inner = jnp.logical_or(coord == 1, coord == 2)
+            outer = jnp.logical_not(inner)
+            mate = batch + stride * (1 - 2 * lax.rem(coord, 2))
+            add.append(
+                dict(rows=rows, send=start, keep=start, peer=mate,
+                     sends=both(active, outer), receives=both(active, inner)))
+            spread.append(
+                dict(rows=rows, send=start, peer=mate,
+                     sends=both(active, inner), receives=both(active, outer)))
+            active = both(active, inner)
+            bit = coord // 2
+            mate = batch + stride * (3 - 2 * coord)
+        else:
+            bit = coord
+            mate = batch + stride * (1 - 2 * coord)
+        rows = rows // 2
+        kept = start + bit * rows
+        add.append(
+            dict(rows=rows, send=start + (1 - bit) * rows, keep=kept, peer=mate,
+                 sends=active, receives=active))
+        spread.append(dict(rows=rows, send=kept, peer=mate, sends=active, receives=active))
+        start = kept
+    return add, spread[::-1]
+
+
+def step_rings(order, dims):
+    one_way = []
+    for name in order:
+        one_way += [True, False] if dims[name][1] == 4 else [False]
+    count = len(one_way)
+    steps = 2 + 2 * count
+    rings = [3] * steps
+    for index, single in enumerate(one_way):
+        if single:
+            first, last = 1 + index, steps - 2 - index
+            rings[first] = rings[last] = last - first + 2
+    return rings
+
+
+def stage_rows(order, dims, rows):
+    result = []
+    for name in order:
+        if dims[name][1] == 4:
+            result.append(rows)
+        rows //= 2
+        result.append(rows)
+    return result
+
+
+orders = ("xyz", "yxz", "zxy")
+
+
+def sums_kernel(dims, jobs, *refs):
+    (hidden, ffn_in, context, normed, branch, pre, attn, dq, dk, dv, small, out, small_out) = refs[:13]
+    (left, right, part, acc, full, mate_in, small_own, small_in) = refs[13:21]
+    rest = refs[21:]
+    counts = [len(stage_rows(order, dims, 8)) for order in orders]
+    inbox, where = [], 0
+    for count in counts:
+        inbox.append(rest[where : where + count])
+        where += count
+    load_sem, send_sem, recv_sem, keep_sem, small_sem = rest[where:]
+    tower, batch = place()
+    half = unit_rows // 2
+    steps = 2 + 2 * counts[0]
+    plans = [plan_unit(order, dims, batch, half) for order in orders]
+    rings = [step_rings(order, dims) for order in orders]
+    held, spread_held = acc.shape[0], full.shape[0]
+
+    barrier = pltpu.get_barrier_semaphore()
+    mate = (1 - tower, batch)
+    mates, turns = [mate], [mate]
+    for stride, size in dims.values():
+        coord = lax.rem(batch // stride, size)
+        near = (tower, batch + stride * (1 - 2 * lax.rem(coord, 2)))
+        mates.append(near)
+        turns.append(near)
+        if size == 4:
+            mates.append((tower, batch + stride * (3 - 2 * coord)))
+            turns.append((tower, batch + stride * (2 - 4 * (coord // 2))))
+            mates.append(turns[-1])
+    for mate in mates:
+        pl.semaphore_signal(barrier, 1, device_id=mate, device_id_type=MESH)
+    pl.semaphore_wait(barrier, len(mates))
+
+    width = out.shape[1]
+
+    def load(job, begin):
+        slot = lax.rem(job, 2)
+
+        def copies(left_ref, left_block, right_ref, right_block):
+            for index, (ref, block, size, target) in enumerate(
+                ((left_ref, left_block, job_rows, left), (right_ref, right_block, width, right))
+            ):
+                columns = pl.ds(pl.multiple_of(block * size, 128), size)
+                copy = pltpu.make_async_copy(
+                    ref.at[:, columns], target.at[slot], load_sem.at[index, slot]
+                )
+                copy.start() if begin else copy.wait()
+
+        if not begin:
+            copies(hidden, 0, branch, 0)
+            return
+        per_narrow = hidden.shape[1] // job_rows
+        per_side = width // job_rows
+        first = 0
+        table = [(hidden, branch, per_narrow)]
+        table.append((ffn_in, pre, per_narrow))
+        table += [(context, attn, per_side), (normed, dq, per_side), (normed, dk, per_side), (normed, dv, per_side)]
+        for index, (left_ref, right_ref, count) in enumerate(table):
+            local = job - first
+
+            def go(local=local, left_ref=left_ref, right_ref=right_ref, index=index):
+                if index == 1:
+                    copies(left_ref, lax.rem(local, per_side), right_ref, local // per_side)
+                else:
+                    copies(left_ref, local, right_ref, 0)
+
+            pl.when(jnp.logical_and(local >= 0, local < count))(go)
+            first += count
+
+    def compute(job):
+        slot = lax.rem(job, 2)
+        load(job, False)
+        pl.when(job + 1 < jobs)(lambda: load(job + 1, True))
+        part[slot] = lax.dot_general(
+            left[slot], right[slot], (((0,), (0,)), ((), ())), preferred_element_type=jnp.float32
+        )
+
+    def remote(unit, step, job):
+        add, spread = plans[unit]
+        turn = lax.rem(job, rings[unit][step])
+        place_in = lax.rem(job, held)
+        sems = dict(
+            send_sem=send_sem.at[unit * steps + step, turn],
+            recv_sem=recv_sem.at[unit * steps + step, turn],
+            device_id_type=MESH,
+        )
+        base = unit * half
+        if step == 0:
+            src = part.at[lax.rem(job, 2), pl.ds(pl.multiple_of(unit * unit_rows + (1 - tower) * half, 8), half)]
+            dst = mate_in.at[turn, pl.ds(base, half)]
+            return pltpu.make_async_remote_copy(src, dst, device_id=(1 - tower, batch), **sems), None, None
+        if step == steps - 1:
+            src = full.at[lax.rem(job, spread_held), pl.ds(base, half)]
+            first = pl.multiple_of(job * job_rows + unit * unit_rows + tower * half, 8)
+            dst = out.at[pl.ds(first, half)]
+            return pltpu.make_async_remote_copy(src, dst, device_id=(1 - tower, batch), **sems), None, None
+        count = counts[unit]
+        item = add[step - 1] if step <= count else spread[step - 1 - count]
+        rows = pl.ds(pl.multiple_of(base + item["send"], 8), item["rows"])
+        if step <= count:
+            src, dst = acc.at[place_in, rows], inbox[unit][step - 1].at[turn]
+        else:
+            src = dst = full.at[lax.rem(job, spread_held), rows]
+        copy = pltpu.make_async_remote_copy(src, dst, device_id=(tower, item["peer"]), **sems)
+        return copy, item["sends"], item["receives"]
+
+    def keep(unit, job):
+        base = unit * half
+        first = pl.multiple_of(job * job_rows + unit * unit_rows + tower * half, 8)
+        return pltpu.make_async_copy(
+            full.at[lax.rem(job, spread_held), pl.ds(base, half)], out.at[pl.ds(first, half)], keep_sem.at[unit, lax.rem(job, 2)]
+        )
+
+    def finish(unit, step, job):
+        copy, sends, receives = remote(unit, step, job)
+        add, _ = plans[unit]
+        base = unit * half
+        guarded(sends, copy.wait_send)
+        turn = lax.rem(job, rings[unit][step])
+        place_in = lax.rem(job, held)
+
+        def arrived():
+            copy.wait_recv()
+            if step == 0:
+                own = pl.ds(pl.multiple_of(unit * unit_rows + tower * half, 8), half)
+                acc[place_in, pl.ds(base, half)] = part[lax.rem(job, 2), own] + mate_in[turn, pl.ds(base, half)]
+            elif step <= counts[unit]:
+                item = add[step - 1]
+                rows = pl.ds(pl.multiple_of(base + item["keep"], 8), item["rows"])
+                total = acc[place_in, rows] + inbox[unit][step - 1][turn]
+                if step == counts[unit]:
+                    full[lax.rem(job, spread_held), rows] = total
+                else:
+                    acc[place_in, rows] = total
+
+        guarded(receives, arrived)
+        if step == steps - 1:
+            keep(unit, job).wait()
+
+    def advance(step, job):
+        for unit in range(len(orders)):
+            if step > 0:
+                finish(unit, step - 1, job)
+            if step < steps:
+                copy, sends, _ = remote(unit, step, job)
+                guarded(sends, copy.start)
+                if step == steps - 1:
+                    keep(unit, job).start()
+
+    def small_copy(turn):
+        return pltpu.make_async_remote_copy(
+            src_ref=small_own.at[turn],
+            dst_ref=small_in.at[turn],
+            send_sem=small_sem.at[0, turn],
+            recv_sem=small_sem.at[1, turn],
+            device_id=turns[turn],
+            device_id_type=MESH,
+        )
+
+    def small_turn(turn):
+        if turn == 0:
+            small_own[0] = small[...]
+        else:
+            small_copy(turn - 1).wait()
+            total = small_own[turn - 1] + small_in[turn - 1]
+            if turn == len(turns):
+                small_out[...] = total
+            else:
+                small_own[turn] = total
+        if turn < len(turns):
+            small_copy(turn).start()
+
+    load(0, True)
+
+    def slot(time, carry):
+        for step in range(steps, -1, -1):
+            job = time - 1 - step
+            pl.when(jnp.logical_and(job >= 0, job < jobs))(functools.partial(advance, step, job))
+        for turn in range(len(turns) + 1):
+            pl.when(time == turn)(functools.partial(small_turn, turn))
+        pl.when(time < jobs)(functools.partial(compute, time))
+        return carry
+
+    lax.fori_loop(0, jobs + steps + 1, slot, 0)
+
+
+def sum_weights(batch_size, collective, *arrays):
+    hidden, normed = arrays[0], arrays[3]
+    tokens, width = normed.shape
+    total = 2 * hidden.shape[1] + 4 * width
+    jobs = total // job_rows
+    dims = batch_dims(batch_size)
+    half = unit_rows // 2
+    rings = [step_rings(order, dims) for order in orders]
+    inboxes = [
+        pltpu.VMEM((rings[unit][1 + index], rows, width), jnp.float32)
+        for unit, order in enumerate(orders)
+        for index, rows in enumerate(stage_rows(order, dims, half))
+    ]
+    steps = len(rings[0])
+    longest = max(max(ring) for ring in rings)
+    turns = 1 + sum(size // 2 for _, size in dims.values())
+    small = arrays[-1]
+    return pl.pallas_call(
+        functools.partial(sums_kernel, dims, jobs),
+        out_shape=(
+            jax.ShapeDtypeStruct((total, width), jnp.float32),
+            jax.ShapeDtypeStruct(small.shape, jnp.float32),
+        ),
+        in_specs=[pl.BlockSpec(memory_space=pl.ANY)] * 10 + [pl.BlockSpec(memory_space=pltpu.VMEM)],
+        out_specs=(pl.BlockSpec(memory_space=pl.ANY), pl.BlockSpec(memory_space=pltpu.VMEM)),
+        scratch_shapes=[
+            pltpu.VMEM((2, tokens, job_rows), jnp.bfloat16),
+            pltpu.VMEM((2, tokens, width), jnp.bfloat16),
+            pltpu.VMEM((2, job_rows, width), jnp.float32),
+            pltpu.VMEM((steps // 2, 3 * half, width), jnp.float32),
+            pltpu.VMEM((steps, 3 * half, width), jnp.float32),
+            pltpu.VMEM((3, 3 * half, width), jnp.float32),
+            pltpu.VMEM((turns,) + small.shape, jnp.float32),
+            pltpu.VMEM((turns,) + small.shape, jnp.float32),
+            *inboxes,
+            pltpu.SemaphoreType.DMA((2, 2)),
+            pltpu.SemaphoreType.DMA((3 * steps, longest)),
+            pltpu.SemaphoreType.DMA((3 * steps, longest)),
+            pltpu.SemaphoreType.DMA((3, 2)),
+            pltpu.SemaphoreType.DMA((2, turns)),
+        ],
+        compiler_params=pltpu.CompilerParams(
+            collective_id=collective, has_side_effects=True, vmem_limit_bytes=56000000
+        ),
+        name="sum_weights",
+    )(*arrays)
 
 
 def bucket_onehot(slot_len, bucket_count):
@@ -36,6 +431,7 @@
 
 
 def local(
+    batch_size,
     tokens,
     lengths,
     prefixes,
@@ -108,7 +504,7 @@
     pooled = jnp.sum(final.reshape(seqs, slot_len, width) * pool_weight[:, :, None], axis=1)
     inverse_pool = lax.rsqrt(jnp.sum(pooled * pooled, axis=-1, keepdims=True) + epsilon)
     unit = pooled * inverse_pool
-    gathered = lax.all_gather(unit, ("tower", "batch"), axis=0, tiled=True)
+    gathered = gather_blocks(unit, batch_size, 0).reshape(2 * batch_size * seqs, width)
     total_seqs = gathered.shape[0] // 2
     query_units = gathered[:total_seqs]
     doc_units = gathered[total_seqs:]
@@ -141,12 +537,10 @@
     grad_fin = (pool_weight[:, :, None] * grad_pooled[:, None, :]).reshape(rows, width)
     grad_out, grad_final = norm_backward(output, inverse_third, gain_final, grad_fin)
     grad_branch = grad_out.astype(jnp.bfloat16)
-    grad_narrow = jnp.einsum("tf,td->fd", hidden, grad_branch, preferred_element_type=jnp.float32)
     grad_hidden = jnp.einsum(
         "td,fd->tf", grad_branch, narrow_weight, preferred_element_type=jnp.float32
     )
     grad_pre = jnp.where(pre_act > 0, grad_hidden, 0.0).astype(jnp.bfloat16)
-    grad_widen = jnp.einsum("td,tf->df", ffn_in, grad_pre, preferred_element_type=jnp.float32)
     grad_ffn_in = jnp.einsum(
         "tf,df->td", grad_pre, widen_weight, preferred_element_type=jnp.float32
     )
@@ -155,9 +549,6 @@
     )
     grad_mixed = grad_out + grad_mixed_norm
     grad_attn = grad_mixed.astype(jnp.bfloat16)
-    grad_output = jnp.einsum(
-        "ti,td->id", context_flat, grad_attn, preferred_element_type=jnp.float32
-    )
     grad_context = jnp.einsum(
         "td,id->ti", grad_attn, output_weight, preferred_element_type=jnp.float32
     )
@@ -200,9 +591,6 @@
     key_grads = key_grads.reshape(rows, inner)
     value_grads = value_grads.reshape(rows, inner)
     grad_bucket = jnp.einsum("ijb,hij->bh", onehot, bias_total, precision=highest)
-    grad_query = jnp.einsum("td,ti->di", normed, query_grads, preferred_element_type=jnp.float32)
-    grad_key = jnp.einsum("td,ti->di", normed, key_grads, preferred_element_type=jnp.float32)
-    grad_value = jnp.einsum("td,ti->di", normed, value_grads, preferred_element_type=jnp.float32)
     grad_normed = (
         jnp.einsum("ti,di->td", query_grads, query_weight, preferred_element_type=jnp.float32)
         + jnp.einsum("ti,di->td", key_grads, key_weight, preferred_element_type=jnp.float32)
@@ -212,31 +600,22 @@
         tokens_f, inverse_first, gain_attention, grad_normed
     )
     token_gradient = (grad_mixed + grad_tokens_norm).astype(jnp.bfloat16)[None]
-    (
-        sum_attention,
-        sum_query,
-        sum_key,
-        sum_value,
-        sum_output,
-        sum_bucket,
-        sum_feedforward,
-        sum_widen,
-        sum_narrow,
-        sum_final,
-    ) = lax.psum(
-        (
-            grad_attention,
-            grad_query,
-            grad_key,
-            grad_value,
-            grad_output,
-            grad_bucket,
-            grad_feedforward,
-            grad_widen,
-            grad_narrow,
-            grad_final,
-        ),
-        ("tower", "batch"),
+    buckets = grad_bucket.reshape(-1)
+    lines = [grad_attention, grad_feedforward, grad_final]
+    lines.append(jnp.pad(buckets, (0, width - buckets.shape[0])))
+    block = jnp.concatenate([jnp.stack(lines), jnp.zeros((4, width), jnp.float32)])
+    weights, sums = sum_weights(
+        batch_size, 1, hidden, ffn_in, context_flat, normed,
+        grad_branch, grad_pre, grad_attn, query_grads, key_grads, value_grads, block,
+    )
+    sum_attention, sum_feedforward, sum_final = sums[0], sums[1], sums[2]
+    sum_bucket = sums[3, : buckets.shape[0]].reshape(grad_bucket.shape)
+    ff = hidden.shape[1]
+    sum_narrow = weights[:ff]
+    sum_widen = weights[ff : 2 * ff].reshape(ff // width, width, width)
+    sum_widen = sum_widen.transpose(1, 0, 2).reshape(width, ff)
+    sum_output, sum_query, sum_key, sum_value = (
+        weights[2 * ff + n * width : 2 * ff + (n + 1) * width] for n in range(4)
     )
     return (
         loss_value,
@@ -273,7 +652,7 @@
         P(),
     )
     return jax.shard_map(
-        local,
+        functools.partial(local, mesh.shape["batch"]),
         mesh=mesh,
         in_specs=placed,
         out_specs=(

time: 1080 us -> 878 us (0.81); the launches traced: 1080 us -> 865 us
  waiting for transfers between devices: 321 us -> 0 us
  Pallas kernels: 0 us -> 255 us
  blocking collectives: 112 us -> 0 us
  matrix products: 366 us -> 315 us
  local copies, waits for them, and re-layouts: 153 us -> 177 us
  between operations: 18 us -> 4.81 us
    psum x1 -> x0, waiting for transfers between devices: 321 us -> none  [local(): lax.psum((grad_attention, grad_query, grad_key, grad_value, grad_output,...]
    pallas_call x0 -> x2, Pallas kernels: none -> 255 us  [the longest x1 242 us: sum_weights(): pl.pallas_call(functools.partial(sums_kernel, dims, jobs), out_shape=(jax...]
    all_gather x1 -> x0, blocking collectives: 72.1 us -> none  [local(): gathered = lax.all_gather(unit, ('tower', 'batch'), axis=0, tiled=True)]
    dot_general x6 -> x0, matrix products: 52.1 us -> none  [the longest x1 18.3 us: local(): jnp.einsum('tf,td->fd', hidden, grad_branch, preferred_element_type=jnp.f...]
    psum x1 -> x0, blocking collectives: 39.6 us -> none  [local(): lax.psum((grad_attention, grad_query, grad_key, grad_value, grad_output,...]
    reshape x0 -> x6, local copies, waits for them, and re-layouts: none -> 23.9 us  [the longest x1 5.17 us: local(): sum_widen = sum_widen.transpose(1, 0, 2).reshape(width, ff)]
    slice x0 -> x4, local copies, waits for them, and re-layouts: none -> 19.2 us  [the longest x1 11 us: local(): sum_narrow = weights[:ff]]
    unnamed x132 -> x85, local copies, waits for them, and re-layouts: 34.2 us -> 16.8 us
  transfers between devices with their start and end apart: 1 -> 0, of which waited for: 1 -> 0; matrix products, arithmetic and copies ran while one was open for 7% -> 0% of each run, Pallas kernels for 0% -> 0%
where the time goes in v1:
time: 878 us; the launch traced here: 865 us
  matrix products  315 us (36%)
  Pallas kernels  255 us (29%)
  local copies, waits for them, and re-layouts  177 us (20%)
  other arithmetic  113 us (13%)
    pallas_call x1, Pallas kernels, sum_weights(): pl.pallas_call(functools.partial(sums_kernel, dims, jobs), out_shape=(jax...  242 us
    convert_element_type x4, other arithmetic, attend_backward(): scores_low = grad_scores.astype(jnp.bfloat16)  72.5 us
    dot_general x8, matrix products, score_block(): jnp.einsum('ihd,jhd->hij', query_rows, key_rows, preferred_element_type=j...  66.6 us
    while x5, local copies, waits for them, and re-layouts, local(): lax.map(attend_forward, (query_all, key_all, value_all, valid))  35.8 us
    dot_general x4, matrix products, attend_backward(): jnp.einsum('ihd,jhd->hij', context_grad, value_rows, preferred_element_ty...  35.5 us
    while x4, local copies, waits for them, and re-layouts, local(): lax.scan(attend_backward, jnp.zeros(bias.shape, jnp.float32), (query_all,...  27.9 us
    dot_general x1, matrix products, local(): jnp.einsum('td,fd->tf', grad_branch, narrow_weight, preferred_element_typ...  20.5 us
    dot_general x1, matrix products, local(): pre_act = jnp.dot(ffn_in, widen_weight, preferred_element_type=jnp.float32)  20.3 us

profile of v1, /device:TPU:0, one launch (start us, length us, event | category | flops | bytes accessed | tf_op | source)
XLA Modules:
  0.0 865.4 jit_solution(8725982954458607212)
XLA Ops:
  70.4 13.6 %fusion.55 = f32[12,512,512]{2,0,1:T(8,128)} fusion(s32[512,512]{1,0:T(8,128)S(1)} %fusion.78, f32[32,12]{0,1:T(8,128)S(1)} %copy-done.29), kind=kOutput, calls=%fused_computation.71 | convolution fusion | flops 1216348160 | bytes 13633024 | tf_op jit(solution)/shard_map/ijb,bh->hij/dot_general | solution.py:461
  84.0 18.0 %copy.57 = f32[12,512,512]{1,2,0:T(8,128)} copy(f32[12,512,512]{2,0,1:T(8,128)} %fusion.55) | data formatting | bytes 25165824 | tf_op jit(solution)/shard_map/while | solution.py:493
  104.1 56.7 %while.29 = (s32[]{:T(128)}, bf16[4,512,12,64]{1,3,2,0:T(8,128)(2,1)}, f32[4,12,512]{2,1,0:T(8,128)S(1)}, bf16[4,512,12,64]{1,3,2,0:T(8,128)(2,1)}, pred[4,512]{...) while((s32[]{:T(128)}, ...), condition=%wide.region_4.5_spmd, body=%wide.region_1.4_spmd.sunk | while | flops 830859264 | bytes 53702252 | solution.py:493
  104.2 8.0 fusion.152
  118.3 8.0 fusion.152
  132.5 8.0 fusion.152
  146.7 8.0 fusion.152
  172.3 20.3 %fusion.51 = (bf16[2048,3072]{1,0:T(8,128)(2,1)}, f32[2048,3072]{1,0:T(8,128)}) fusion(bf16[2048,768]{1,0:T(8,128)(2,1)} %multiply_convert_fusion.refs_1_, bf16[768,3072]{1,0:T(8,128)(2,1)} %param.29), kind=kOutput, calls=%fused_computation.61 | convolution fusion | flops 9682550784 | bytes 45613056 | tf_op jit(solution)/shard_map/dot_general | solution.py:498
  192.6 14.9 %multiply_reduce_fusion.4 = (f32[2048]{0:T(1024)S(1)}, f32[2048,768]{1,0:T(8,128)S(1)}) fusion(f32[2048,768]{1,0:T(8,128)S(1)} %get-tuple-element.317, bf16[2048,3072]{1,0:T(8,128)(2,1)} %get-tuple-element.318.refs_0_, bf16[3072,768]{1,0:T(8,128)(2,1)} %param.30), kind=kOutput, calls=%fused_computation.97 | convolution fusion | flops 9668392960 | bytes 29892608 | tf_op jit(solution)/shard_map/dot_general | solution.py:500
  212.0 13.3 %gather_blocks.1 = f32[2,16,4,768]{3,2,1,0:T(4,128)} custom-call(f32[4,768]{1,0:T(4,128)} %broadcast_multiply_fusion.block_ref), custom_call_target="tpu_custom_call" | custom-call | tf_op jit(solution)/shard_map/gather_blocks/pallas_call | solution.py:84
  237.8 20.5 %fusion.52.refs_5_ = bf16[2048,3072]{1,0:T(8,128)(2,1)} fusion(f32[2048,3072]{1,0:T(8,128)} %get-tuple-element.319, bf16[2048,768]{1,0:T(8,128)(2,1)S(1)} %fusion.74.refs_4_, bf16[3072,768]{1,0:T(8,128)(2,1)} %param.30), kind=kOutput, calls=%fused_computation.62 | convolution fusion | flops 9682550784 | bytes 45613056 | tf_op jit(solution)/shard_map/td,fd->tf/dot_general | solution.py:540
  258.3 18.2 %multiply_reduce_fusion.1 = (f32[768]{0:T(1024)}, f32[2048]{0:T(1024)S(1)}, f32[2048,768]{1,0:T(8,128)}) fusion(f32[2048,768]{1,0:T(8,128)} %copy-done.8, f32[2048]{0:T(1024)S(1)} %get-tuple-element.309, f32[768]{0:T(1024)S(1)} %copy-done.27, bf16[2048,3072]{1,0:T(8,128)(2,1)} %fusion.52.refs_5_, bf16[768,3072]{1,0:T(8,128)(2,1)} %param.29), kind=kOutput, calls=%fused_computation.91 | convolution fusion | flops 9673110528 | bytes 29906944 | tf_op jit(solution)/shard_map/tf,df->td/dot_general | solution.py:544
  276.4 9.5 %fusion.96 = (bf16[2048,768]{1,0:T(8,128)(2,1)}, f32[2048,768]{1,0:T(8,128)}) fusion(f32[2048]{0:T(1024)S(1)} %broadcast_multiply_fusion.2, f32[2048,768]{1,0:T(8,128)} %copy-done.8, f32[2048]{0:T(1024)S(1)} %get-tuple-element.308, f32[2048,768]{1,0:T(8,128)} %get-tuple-element.325, f32[768]{0:T(1024)S(1)} %copy-done.27, f32[2048]{0:T(1024)S(1)} %get-tuple-element.309, ...), kind=kLoop, calls=%fused_computation.163 | loop fusion | flops 20447232 | bytes 28387328 | tf_op jit(solution)/shard_map/convert_element_type | solution.py:551
  313.2 191.9 %while.30 = (s32[]{:T(128)}, f32[12,512,512]{1,2,0:T(8,128)}, bf16[4,512,12,64]{1,3,2,0:T(8,128)(2,1)}, bf16[4,512,12,64]{1,3,2,0:T(8,128)(2,1)}, bf16[4,512,12,...) while((s32[]{:T(128)}, f32[12,512,512]{1,2,0:T(8,128)}, ...), condition=%wide.region_22.23_spmd.clone, body=%wide.region_20.22_spmd.clone.sunk | while | flops 2049042432 | bytes 240777952 | solution.py:585
  313.7 8.7 %subtract_exponential_fusion.5 = f32[12,512,512]{1,2,0:T(8,128)S(1)} fusion(f32[12,512,512]{1,2,0:T(8,128)} %get-tuple-element.526, f32[12,512]{1,0:T(8,128)S(1)} %dynamic-slice_bitcast_fusion.2, pred[512]{0:T(512)(128)(4,1)S(1)} %dynamic-slice_reduce_fusion.5, bf16[4,512,12,64]{1,3,2,0:T(8,128)(2,1)} %get-tuple-element.525, s32[]{:T(128)S(6)} %copy.107, ...), kind=kOutput, calls=%fused_computation.21.clone.1 | convolution fusion | flops 412090368 | bytes 26764800 | tf_op jit(solution)/shard_map/while/body/eval_jaxpr/ihd,jhd->hij/dot_general | solution.py:476
  322.4 8.9 %multiply_reduce_fusion.9 = (f32[12,512]{1,0:T(8,128)S(1)}, f32[12,512,512]{1,2,0:T(8,128)}) fusion(f32[12,512,512]{1,2,0:T(8,128)S(1)} %subtract_exponential_fusion.5, bf16[4,512,12,64]{1,3,2,0:T(8,128)(2,1)} %get-tuple-element.529, s32[]{:T(128)S(6)} %copy.107, bf16[4,512,12,64]{1,3,2,0:T(8,128)(2,1)} %get-tuple-element.528), kind=kOutput, calls=%fused_computation.20.clone.1 | convolution fusion | flops 408938496 | bytes 26764288 | tf_op jit(solution)/shard_map/while/body/eval_jaxpr/ihd,jhd->hij/dot_general | solution.py:565
  331.2 15.9 %fusion.163 = (bf16[12,512,512]{1,2,0:T(8,128)(2,1)S(1)}, f32[12,512,512]{1,2,0:T(8,128)}) fusion(f32[12,512,512]{1,2,0:T(8,128)} %copy-done.1, f32[12,512,512]{1,2,0:T(8,128)} %get-tuple-element.459, f32[12,512]{1,0:T(8,128)S(1)} %get-tuple-element.460, f32[12,512,512]{1,2,0:T(8,128)} %get-tuple-element.505, pred[]{:T(512)S(6)} %compare.4), kind=kLoop, calls=%fused_computation.24.clone.1 | loop fusion | flops 15728640 | bytes 56647680 | tf_op jit(solution)/shard_map/while/body/eval_jaxpr/convert_element_type | solution.py:569
  359.3 8.7 %subtract_exponential_fusion.5 = f32[12,512,512]{1,2,0:T(8,128)S(1)} fusion(f32[12,512,512]{1,2,0:T(8,128)} %get-tuple-element.526, f32[12,512]{1,0:T(8,128)S(1)} %dynamic-slice_bitcast_fusion.2, pred[512]{0:T(512)(128)(4,1)S(1)} %dynamic-slice_reduce_fusion.5, bf16[4,512,12,64]{1,3,2,0:T(8,128)(2,1)} %get-tuple-element.525, s32[]{:T(128)S(6)} %copy.107, ...), kind=kOutput, calls=%fused_computation.21.clone.1 | convolution fusion | flops 412090368 | bytes 26764800 | tf_op jit(solution)/shard_map/while/body/eval_jaxpr/ihd,jhd->hij/dot_general | solution.py:476
  368.0 8.9 %multiply_reduce_fusion.9 = (f32[12,512]{1,0:T(8,128)S(1)}, f32[12,512,512]{1,2,0:T(8,128)}) fusion(f32[12,512,512]{1,2,0:T(8,128)S(1)} %subtract_exponential_fusion.5, bf16[4,512,12,64]{1,3,2,0:T(8,128)(2,1)} %get-tuple-element.529, s32[]{:T(128)S(6)} %copy.107, bf16[4,512,12,64]{1,3,2,0:T(8,128)(2,1)} %get-tuple-element.528), kind=kOutput, calls=%fused_computation.20.clone.1 | convolution fusion | flops 408938496 | bytes 26764288 | tf_op jit(solution)/shard_map/while/body/eval_jaxpr/ihd,jhd->hij/dot_general | solution.py:565
  376.8 18.9 %fusion.163 = (bf16[12,512,512]{1,2,0:T(8,128)(2,1)S(1)}, f32[12,512,512]{1,2,0:T(8,128)}) fusion(f32[12,512,512]{1,2,0:T(8,128)} %copy-done.1, f32[12,512,512]{1,2,0:T(8,128)} %get-tuple-element.459, f32[12,512]{1,0:T(8,128)S(1)} %get-tuple-element.460, f32[12,512,512]{1,2,0:T(8,128)} %get-tuple-element.505, pred[]{:T(512)S(6)} %compare.4), kind=kLoop, calls=%fused_computation.24.clone.1 | loop fusion | flops 15728640 | bytes 56647680 | tf_op jit(solution)/shard_map/while/body/eval_jaxpr/convert_element_type | solution.py:569
  407.8 8.7 %subtract_exponential_fusion.5 = f32[12,512,512]{1,2,0:T(8,128)S(1)} fusion(f32[12,512,512]{1,2,0:T(8,128)} %get-tuple-element.526, f32[12,512]{1,0:T(8,128)S(1)} %dynamic-slice_bitcast_fusion.2, pred[512]{0:T(512)(128)(4,1)S(1)} %dynamic-slice_reduce_fusion.5, bf16[4,512,12,64]{1,3,2,0:T(8,128)(2,1)} %get-tuple-element.525, s32[]{:T(128)S(6)} %copy.107, ...), kind=kOutput, calls=%fused_computation.21.clone.1 | convolution fusion | flops 412090368 | bytes 26764800 | tf_op jit(solution)/shard_map/while/body/eval_jaxpr/ihd,jhd->hij/dot_general | solution.py:476
  416.5 8.9 %multiply_reduce_fusion.9 = (f32[12,512]{1,0:T(8,128)S(1)}, f32[12,512,512]{1,2,0:T(8,128)}) fusion(f32[12,512,512]{1,2,0:T(8,128)S(1)} %subtract_exponential_fusion.5, bf16[4,512,12,64]{1,3,2,0:T(8,128)(2,1)} %get-tuple-element.529, s32[]{:T(128)S(6)} %copy.107, bf16[4,512,12,64]{1,3,2,0:T(8,128)(2,1)} %get-tuple-element.528), kind=kOutput, calls=%fused_computation.20.clone.1 | convolution fusion | flops 408938496 | bytes 26764288 | tf_op jit(solution)/shard_map/while/body/eval_jaxpr/ihd,jhd->hij/dot_general | solution.py:565
  425.4 18.9 %fusion.163 = (bf16[12,512,512]{1,2,0:T(8,128)(2,1)S(1)}, f32[12,512,512]{1,2,0:T(8,128)}) fusion(f32[12,512,512]{1,2,0:T(8,128)} %copy-done.1, f32[12,512,512]{1,2,0:T(8,128)} %get-tuple-element.459, f32[12,512]{1,0:T(8,128)S(1)} %get-tuple-element.460, f32[12,512,512]{1,2,0:T(8,128)} %get-tuple-element.505, pred[]{:T(512)S(6)} %compare.4), kind=kLoop, calls=%fused_computation.24.clone.1 | loop fusion | flops 15728640 | bytes 56647680 | tf_op jit(solution)/shard_map/while/body/eval_jaxpr/convert_element_type | solution.py:569
  456.4 8.7 %subtract_exponential_fusion.5 = f32[12,512,512]{1,2,0:T(8,128)S(1)} fusion(f32[12,512,512]{1,2,0:T(8,128)} %get-tuple-element.526, f32[12,512]{1,0:T(8,128)S(1)} %dynamic-slice_bitcast_fusion.2, pred[512]{0:T(512)(128)(4,1)S(1)} %dynamic-slice_reduce_fusion.5, bf16[4,512,12,64]{1,3,2,0:T(8,128)(2,1)} %get-tuple-element.525, s32[]{:T(128)S(6)} %copy.107, ...), kind=kOutput, calls=%fused_computation.21.clone.1 | convolution fusion | flops 412090368 | bytes 26764800 | tf_op jit(solution)/shard_map/while/body/eval_jaxpr/ihd,jhd->hij/dot_general | solution.py:476
  465.1 8.9 %multiply_reduce_fusion.9 = (f32[12,512]{1,0:T(8,128)S(1)}, f32[12,512,512]{1,2,0:T(8,128)}) fusion(f32[12,512,512]{1,2,0:T(8,128)S(1)} %subtract_exponential_fusion.5, bf16[4,512,12,64]{1,3,2,0:T(8,128)(2,1)} %get-tuple-element.529, s32[]{:T(128)S(6)} %copy.107, bf16[4,512,12,64]{1,3,2,0:T(8,128)(2,1)} %get-tuple-element.528), kind=kOutput, calls=%fused_computation.20.clone.1 | convolution fusion | flops 408938496 | bytes 26764288 | tf_op jit(solution)/shard_map/while/body/eval_jaxpr/ihd,jhd->hij/dot_general | solution.py:565
  474.0 18.9 %fusion.163 = (bf16[12,512,512]{1,2,0:T(8,128)(2,1)S(1)}, f32[12,512,512]{1,2,0:T(8,128)}) fusion(f32[12,512,512]{1,2,0:T(8,128)} %copy-done.1, f32[12,512,512]{1,2,0:T(8,128)} %get-tuple-element.459, f32[12,512]{1,0:T(8,128)S(1)} %get-tuple-element.460, f32[12,512,512]{1,2,0:T(8,128)} %get-tuple-element.505, pred[]{:T(512)S(6)} %compare.4), kind=kLoop, calls=%fused_computation.24.clone.1 | loop fusion | flops 15728640 | bytes 56647680 | tf_op jit(solution)/shard_map/while/body/eval_jaxpr/convert_element_type | solution.py:569
  528.9 7.4 fusion.65
  557.8 18.6 %copy.68 = f32[12,512,512]{2,0,1:T(8,128)} copy(f32[12,512,512]{1,2,0:T(8,128)} %get-tuple-element.128) | data formatting | bytes 25165824 | tf_op jit(solution)/shard_map/while | solution.py:585
  576.4 20.3 %fusion.76 = f32[32,12]{1,0:T(8,128)S(1)} fusion(f32[12,512,512]{2,0,1:T(8,128)} %copy.68, s32[512,512]{1,0:T(8,128)S(1)} %copy-done.10), kind=kOutput, calls=%fused_computation.109 | convolution fusion | flops 1216348160 | bytes 13633024 | tf_op jit(solution)/shard_map/ijb,hij->bh/dot_general | solution.py:593
  596.8 241.8 %sum_weights.1 = (f32[9216,768]{1,0:T(8,128)}, f32[8,768]{1,0:T(8,128)S(1)}) custom-call(bf16[2048,3072]{1,0:T(8,128)(2,1)} %get-tuple-element.318.refs_0_, bf16[2048,768]{1,0:T(8,128)(2,1)} %multiply_convert_fusion.refs_1_, bf16[2048,768]{1,0:T(8,128)(2,1)} %copy.70.refs_2_, bf16[2048,768]{1,0:T(8,128)(2,1)} %copy-done.11, bf16[2048,768]{1,0:T(8,128)(2,1)} %copy-done.15, ...), custom_call_target="tpu_custom_call" | custom-call | tf_op jit(solution)/shard_map/sum_weights/pallas_call | solution.py:377
  839.3 7.6 fusion.99
  847.7 11.0 %fusion.98 = (f32[3072,768]{1,0:T(8,128)}, f32[3072,768]{1,0:T(8,128)S(1)}) fusion(f32[9216,768]{1,0:T(8,128)} %get-tuple-element.130), kind=kLoop, calls=%fused_computation.165 | loop fusion | bytes 37748736 | tf_op jit(solution)/shard_map/slice | solution.py:614
  (213 shorter events, 250.5 us)
Async XLA Ops:
  0.6 10.6 %copy-start = (bf16[768,768]{1,0:T(8,128)(2,1)S(1)}, bf16[768,768]{1,0:T(8,128)(2,1)}, u32[]{:S(2)}) copy-start(bf16[768,768]{1,0:T(8,128)(2,1)} %param.25) | copy-start | bytes 3538948
  19.8 10.7 %copy-start.33 = (s32[1,4]{1,0:T(1,128)S(1)}, s32[1,4]{1,0:T(1,128)}, u32[]{:S(2)}) copy-start(s32[1,4]{1,0:T(1,128)} %param.19) | copy-start | bytes 52
  19.8 10.8 %copy-start.35 = (bf16[768,768]{1,0:T(8,128)(2,1)S(1)}, bf16[768,768]{1,0:T(8,128)(2,1)}, u32[]{:S(2)}) copy-start(bf16[768,768]{1,0:T(8,128)(2,1)} %param.23) | copy-start | bytes 3538948
  39.2 10.8 %copy-start.37 = (bf16[768,768]{1,0:T(8,128)(2,1)S(1)}, bf16[768,768]{1,0:T(8,128)(2,1)}, u32[]{:S(2)}) copy-start(bf16[768,768]{1,0:T(8,128)(2,1)} %param.24) | copy-start | bytes 3538948
  58.6 11.8 %copy-start.29 = (f32[32,12]{0,1:T(8,128)S(1)}, f32[32,12]{0,1:T(8,128)}, u32[]{:S(2)}) copy-start(f32[32,12]{0,1:T(8,128)} %param.27) | copy-start | bytes 4612
  160.8 5.5 copy-start.5
  160.9 5.5 copy-start.34
  169.7 23.0 %copy-start.8 = (f32[2048,768]{1,0:T(8,128)}, f32[2048,768]{1,0:T(8,128)S(1)}, u32[]{:S(2)}) copy-start(f32[2048,768]{1,0:T(8,128)S(1)} %get-tuple-element.317) | copy-start | bytes 18874372
  192.6 17.6 %copy-start.22 = (f32[768]{0:T(1024)S(1)}, f32[768]{0:T(1024)}, u32[]{:S(2)}) copy-start(f32[768]{0:T(1024)} %param.31) | copy-start | bytes 9220
  192.6 17.6 %copy-start.25 = (f32[4,512]{1,0:T(4,128)S(1)}, f32[4,512]{1,0:T(4,128)}, u32[]{:S(2)}) copy-start(f32[4,512]{1,0:T(4,128)} %get-tuple-element.313) | copy-start | bytes 24580
  207.5 19.5 %copy-start.32 = (s32[64]{0:T(128)S(1)}, s32[64]{0:T(128)}, u32[]{:S(2)}) copy-start(s32[64]{0:T(128)} %param.21) | copy-start | bytes 772
  207.5 23.6 %copy-start.26 = (f32[1,4,4,128]{3,2,1,0:T(4,128)S(1)}, f32[1,4,4,128]{3,2,1,0:T(4,128)}, u32[]{:S(2)}) copy-start(f32[1,4,4,128]{3,2,1,0:T(4,128)} %get-tuple-element.312) | copy-start | bytes 24580
  230.4 7.4 copy-start.30
  230.7 5.5 copy-start.4
  237.8 20.5 %copy-start.15 = (bf16[2048,768]{1,0:T(8,128)(2,1)}, bf16[2048,768]{1,0:T(8,128)(2,1)S(1)}, u32[]{:S(2)}) copy-start(bf16[2048,768]{1,0:T(8,128)(2,1)S(1)} %fusion.74.refs_4_) | copy-start | bytes 9437188
  322.3 8.9 %copy-start.1 = (f32[12,512,512]{1,2,0:T(8,128)}, f32[12,512,512]{1,2,0:T(8,128)S(1)}, u32[]{:S(2)}) copy-start(f32[12,512,512]{1,2,0:T(8,128)S(1)} %subtract_exponential_fusion.5) | copy-start | bytes 37748740 | tf_op jit(solution)/shard_map/while
  347.1 8.1 copy-start.2
  367.9 8.9 %copy-start.1 = (f32[12,512,512]{1,2,0:T(8,128)}, f32[12,512,512]{1,2,0:T(8,128)S(1)}, u32[]{:S(2)}) copy-start(f32[12,512,512]{1,2,0:T(8,128)S(1)} %subtract_exponential_fusion.5) | copy-start | bytes 37748740 | tf_op jit(solution)/shard_map/while
  395.7 8.1 copy-start.2
  416.5 8.9 %copy-start.1 = (f32[12,512,512]{1,2,0:T(8,128)}, f32[12,512,512]{1,2,0:T(8,128)S(1)}, u32[]{:S(2)}) copy-start(f32[12,512,512]{1,2,0:T(8,128)S(1)} %subtract_exponential_fusion.5) | copy-start | bytes 37748740 | tf_op jit(solution)/shard_map/while
  444.3 8.1 copy-start.2
  465.1 8.9 %copy-start.1 = (f32[12,512,512]{1,2,0:T(8,128)}, f32[12,512,512]{1,2,0:T(8,128)S(1)}, u32[]{:S(2)}) copy-start(f32[12,512,512]{1,2,0:T(8,128)S(1)} %subtract_exponential_fusion.5) | copy-start | bytes 37748740 | tf_op jit(solution)/shard_map/while
  492.9 8.1 copy-start.2
  505.2 5.5 copy-start.18
  510.7 18.1 %copy-start.7 = (bf16[96,8,4,512]{3,1,2,0:T(8,128)(2,1)}, bf16[96,8,4,512]{3,1,2,0:T(8,128)(2,1)S(1)}, u32[]{:S(2)}) copy-start(bf16[96,8,4,512]{3,1,2,0:T(8,128)(2,1)S(1)} %copy.87) | copy-start | bytes 9437188
  519.1 5.1 copy-start.38
  524.2 12.1 %slice-start = ((s8[6291456]{0:T(1024)(128)(4,1)}), s8[4194304]{0:T(1024)(128)(4,1)S(1)}, s32[]{:S(2)}) async-start(s8[6291456]{0:T(1024)(128)(4,1)} %bitcast.214), calls=%async_computation | async-start | bytes 8388608
  528.8 7.4 slice-start.1
  528.9 7.4 copy-start.24
  548.4 9.4 %copy-start.31 = (f32[768]{0:T(1024)S(1)}, f32[768]{0:T(1024)}, u32[]{:S(2)}) copy-start(f32[768]{0:T(1024)} %get-tuple-element.236) | copy-start | bytes 9220
  548.4 9.4 %copy-start.28 = (f32[768]{0:T(1024)S(1)}, f32[768]{0:T(1024)}, u32[]{:S(2)}) copy-start(f32[768]{0:T(1024)} %get-tuple-element.240) | copy-start | bytes 9220
  557.8 18.6 %copy-start.10 = (s32[512,512]{1,0:T(8,128)S(1)}, s32[512,512]{1,0:T(8,128)}, u32[]{:S(2)}) copy-start(s32[512,512]{1,0:T(8,128)} %copy-done.9) | copy-start | bytes 3145732
  (15 other events, 50.6 us)

commit v2 on v1

--- a/solution.py
+++ b/solution.py
@@ -12,6 +12,7 @@
 score_scale = 100.0
 far_steps = (12, 16, 23, 32, 46, 64, 91)
 highest = lax.Precision.HIGHEST
+
 
 MESH = pl.DeviceIdType.MESH
 job_rows = 384
@@ -405,29 +406,427 @@
     )(*arrays)
 
 
-def bucket_onehot(slot_len, bucket_count):
-    places = jnp.arange(slot_len, dtype=jnp.int32)
-    offset = places[None, :] - places[:, None]
+tile = 128
+near = 3 * tile
+
+
+def bias_lines(bucket_bias, mirrored):
+    buckets, heads = bucket_bias.shape
+    spots = jnp.arange(4 * tile, dtype=jnp.int32)
+    moved = jnp.where(spots >= near, spots - 4 * tile, spots)
+    offset = tile - moved if mirrored else moved - tile
+    onehot = offset_onehot(offset, buckets)
+    lines = jnp.dot(bucket_bias.T, onehot.T, precision=highest)
+    return jnp.pad(lines, ((0, 16 - heads), (0, 0)))
+
+
+def offset_onehot(offset, buckets):
     spread = jnp.abs(offset)
     far_bucket = 8 + sum(((spread >= step).astype(jnp.int32) for step in far_steps))
-    bucket = jnp.where(spread < 8, spread, far_bucket) + jnp.where(
-        offset > 0, bucket_count // 2, 0
-    ).astype(jnp.int32)
-    labels = jnp.arange(bucket_count, dtype=jnp.int32)
-    return (bucket[:, :, None] == labels[None, None, :]).astype(jnp.float32)
-
-
-def norm_forward(values, scale_vec):
-    inverse = lax.rsqrt(jnp.mean(values * values, axis=-1, keepdims=True) + epsilon)
-    return (values * inverse * scale_vec, inverse)
-
-
-def norm_backward(values, inverse, scale_vec, upstream):
-    scaled = upstream * scale_vec
-    inner_mean = jnp.mean(scaled * values, axis=-1, keepdims=True)
-    grad_values = inverse * scaled - values * (inverse * inverse * inverse) * inner_mean
-    grad_scale = jnp.sum(upstream * values * inverse, axis=0)
-    return (grad_values, grad_scale)
+    bucket = jnp.where(spread < 8, spread, far_bucket) + jnp.where(offset > 0, buckets // 2, 0)
+    return (bucket[:, None] == jnp.arange(buckets, dtype=jnp.int32)[None, :]).astype(jnp.float32)
+
+
+def spread_bias(lines_ref, near_ref, heads):
+    for head in range(heads):
+        line = jnp.broadcast_to(lines_ref[head : head + 1, :], (tile, 4 * tile))
+        near_ref[head] = pltpu.roll(line, 0, 1, stride=1, stride_axis=0)[:, :near]
+
+
+def bias_row(near_ref, head, block, blocks, low_far, high_far, mirrored):
+    parts = []
+    for other in range(blocks):
+        ahead = block - other if mirrored else other - block
+        if abs(ahead) <= 1:
+            spot = 1 - ahead if mirrored else 1 + ahead
+            parts.append(near_ref[head, :, spot * tile : (spot + 1) * tile])
+        else:
+            parts.append(jnp.full((tile, tile), high_far if ahead > 0 else low_far, jnp.float32))
+    return jnp.concatenate(parts, axis=1)
+
+
+def unit_scale(values):
+    return lax.rsqrt(jnp.mean(values * values, axis=-1, keepdims=True) + epsilon)
+
+
+def low_dot(left, right):
+    return jnp.dot(left, right, preferred_element_type=jnp.float32)
+
+
+def dot_across(left, right):
+    return lax.dot_general(left, right, (((1,), (1,)), ((), ())), preferred_element_type=jnp.float32)
+
+
+def forward_kernel(
+    lengths, prefixes, far, x_ref, lines_ref, gain_a, wq, wk, wv, wo, gain_f, widen, narrow, gain_z,
+    normed_ref, q_ref, k_ref, v_ref, lse_ref, context_ref, mixed_ref, ffn_ref, hidden_ref, output_ref, pooled_ref,
+    near_ref, lse_cols,
+):
+    seq = pl.program_id(0)
+    heads = far.shape[1]
+    slot_len, width = x_ref.shape
+    blocks = slot_len // tile
+    pair = 2 * width // heads
+    length = lengths[seq]
+    pl.when(seq == 0)(lambda: spread_bias(lines_ref, near_ref, heads))
+    tokens = x_ref[...].astype(jnp.float32)
+    normed = (tokens * unit_scale(tokens) * gain_a[...]).astype(jnp.bfloat16)
+    normed_ref[...] = normed
+    q_ref[...] = low_dot(normed, wq[...]).astype(jnp.bfloat16)
+    k_ref[...] = low_dot(normed, wk[...]).astype(jnp.bfloat16)
+    v_ref[...] = low_dot(normed, wv[...]).astype(jnp.bfloat16)
+    lanes = lax.broadcasted_iota(jnp.int32, (1, pair), 1)
+    valid = lax.broadcasted_iota(jnp.int32, (1, slot_len), 1) < length
+    columns = lax.broadcasted_iota(jnp.int32, (tile, tile), 1)
+
+    def attend(index, carry):
+        span = pl.ds(pl.multiple_of(index * pair, pair), pair)
+        keys = k_ref[:, span]
+        queries = q_ref[:, span]
+        values = v_ref[:, span]
+        total = None
+        for side in range(2):
+            head = 2 * index + side
+            mine = (lanes // (pair // 2) == side).astype(jnp.bfloat16)
+            raw = dot_across(queries * mine, keys)
+            rows = []
+            for block in range(blocks):
+                part = slice(block * tile, (block + 1) * tile)
+                bias = bias_row(near_ref, head, block, blocks, far[0, head], far[1, head], False)
+                scores = jnp.where(valid, raw[part] + bias, masked_score)
+                peak = jnp.max(scores, axis=-1, keepdims=True)
+                raised = jnp.exp(scores - peak)
+                total_raised = jnp.sum(raised, axis=-1, keepdims=True)
+                rows.append((raised * (1.0 / total_raised)).astype(jnp.bfloat16))
+                lse_cols[part] = jnp.where(columns == head, peak + jnp.log(total_raised), lse_cols[part])
+            soft_low = jnp.concatenate(rows, axis=0)
+            piece = low_dot(soft_low, values * mine)
+            total = piece if total is None else total + piece
+        context_ref[:, span] = total.astype(jnp.bfloat16)
+        return carry
+
+    lax.fori_loop(0, heads // 2, attend, 0)
+    lse_ref[0] = lse_cols[...].T[: lse_ref.shape[1]]
+    mixed = tokens + low_dot(context_ref[...], wo[...])
+    mixed_ref[...] = mixed
+    ffn_in = (mixed * unit_scale(mixed) * gain_f[...]).astype(jnp.bfloat16)
+    ffn_ref[...] = ffn_in
+    output_ref[...] = mixed
+
+    def feed(index, carry):
+        span = pl.ds(pl.multiple_of(index * width, 128), width)
+        pre_act = low_dot(ffn_ref[...], widen[:, span])
+        hidden = jnp.where(pre_act > 0, pre_act, 0.0).astype(jnp.bfloat16)
+        hidden_ref[:, span] = hidden
+        output_ref[...] += low_dot(hidden, narrow[span, :])
+        return carry
+
+    lax.fori_loop(0, widen.shape[1] // width, feed, 0)
+    output = output_ref[...]
+    places = lax.broadcasted_iota(jnp.int32, (slot_len, 1), 0)
+    mask = jnp.logical_and(places >= prefixes[seq], places < length).astype(jnp.float32)
+    count = (length - prefixes[seq]).astype(jnp.float32)
+    final = output * unit_scale(output) * gain_z[...]
+    pooled_ref[0] = jnp.sum(final * (mask / count), axis=0, keepdims=True)
+
+
+def run_forward(tokens, lengths, prefixes, far, lines, gains, weights):
+    rows, width = tokens.shape
+    seqs = lengths.shape[0]
+    slot_len = rows // seqs
+    heads = far.shape[1]
+    wq, wk, wv, wo, widen, narrow = weights
+    gain_a, gain_f, gain_z = gains
+    ff = widen.shape[1]
+
+    def whole(shape):
+        return pl.BlockSpec(shape, lambda n, *_: (0,) * len(shape), pipeline_mode=pl.Buffered(1))
+
+    def block(columns):
+        return pl.BlockSpec((slot_len, columns), lambda n, *_: (n, 0))
+
+    square = whole((width, width))
+    line = whole((1, width))
+    low, full = jnp.bfloat16, jnp.float32
+
+    def shape(columns, kind):
+        return jax.ShapeDtypeStruct((rows, columns), kind)
+
+    return pl.pallas_call(
+        forward_kernel,
+        grid_spec=pltpu.PrefetchScalarGridSpec(
+            num_scalar_prefetch=3,
+            grid=(seqs,),
+            in_specs=[
+                block(width), whole((16, 4 * tile)), line, square, square, square, square,
+                line, whole((width, ff)), whole((ff, width)), line,
+            ],
+            out_specs=[
+                block(width), block(width), block(width), block(width),
+                pl.BlockSpec((1, 16, slot_len), lambda n, *_: (n, 0, 0)),
+                block(width), block(width), block(width), block(ff), block(width),
+                pl.BlockSpec((1, 1, width), lambda n, *_: (n, 0, 0)),
+            ],
+            scratch_shapes=[
+                pltpu.VMEM((heads, tile, near), jnp.float32),
+                pltpu.VMEM((slot_len, tile), jnp.float32),
+            ],
+        ),
+        out_shape=(
+            shape(width, low), shape(width, low), shape(width, low), shape(width, low),
+            jax.ShapeDtypeStruct((seqs, 16, slot_len), full),
+            shape(width, low), shape(width, full), shape(width, low), shape(ff, low), shape(width, full),
+            jax.ShapeDtypeStruct((seqs, 1, width), full),
+        ),
+        compiler_params=pltpu.CompilerParams(vmem_limit_bytes=60000000),
+        name="forward",
+    )(lengths, prefixes, far, tokens, lines, gain_a[None], wq, wk, wv, wo, gain_f[None], widen, narrow, gain_z[None])
+
+
+def norm_back(values, gain, upstream):
+    inverse = unit_scale(values)
+    scaled = upstream * gain
+    inner = jnp.mean(scaled * values, axis=-1, keepdims=True)
+    by_values = inverse * scaled - values * (inverse * inverse * inverse) * inner
+    return by_values, jnp.sum(upstream * values * inverse, axis=0, keepdims=True)
+
+
+def feed_back_kernel(
+    lengths, prefixes, wo, gain_f, widen, narrow, gain_z, mixed_ref, hidden_ref, output_ref, pooled_ref,
+    branch_ref, pre_ref, attn_ref, context_ref, mixed_grad, gains_ref, feed_grad,
+):
+    seq = pl.program_id(0)
+    slot_len, width = mixed_ref.shape
+    length = lengths[seq]
+
+    def clear():
+        gains_ref[...] = jnp.zeros_like(gains_ref)
+
+    pl.when(seq == 0)(clear)
+    places = lax.broadcasted_iota(jnp.int32, (slot_len, 1), 0)
+    mask = jnp.logical_and(places >= prefixes[seq], places < length).astype(jnp.float32)
+    count = (length - prefixes[seq]).astype(jnp.float32)
+    final_grad = (mask / count) * pooled_ref[0]
+    output_grad, final_gain = norm_back(output_ref[...], gain_z[...], final_grad)
+    gains_ref[2:3] += final_gain
+    mixed_grad[...] = output_grad
+    branch_ref[...] = output_grad.astype(jnp.bfloat16)
+    feed_grad[...] = jnp.zeros_like(feed_grad)
+
+    def feed(index, carry):
+        span = pl.ds(pl.multiple_of(index * width, 128), width)
+        hidden_grad = dot_across(branch_ref[...], narrow[span, :])
+        pre_grad = jnp.where(hidden_ref[:, span] > 0, hidden_grad, 0.0).astype(jnp.bfloat16)
+        pre_ref[:, span] = pre_grad
+        feed_grad[...] += dot_across(pre_grad, widen[:, span])
+        return carry
+
+    lax.fori_loop(0, widen.shape[1] // width, feed, 0)
+    by_mixed, feed_gain = norm_back(mixed_ref[...], gain_f[...], feed_grad[...])
+    gains_ref[1:2] += feed_gain
+    total_grad = mixed_grad[...] + by_mixed
+    mixed_grad[...] = total_grad
+    attn_low = total_grad.astype(jnp.bfloat16)
+    attn_ref[...] = attn_low
+    context_ref[...] = dot_across(attn_low, wo[...]).astype(jnp.bfloat16)
+
+
+def attend_back_kernel(
+    lengths, far, x_ref, lines_ref, gain_a, wq, wk, wv, q_ref, k_ref, v_ref, lse_ref, context_grad, mixed_grad,
+    dq_ref, dk_ref, dv_ref, token_ref, gains_ref, sums_ref,
+    near_ref, far_sums, near_sums, soft_ref,
+):
+    seq = pl.program_id(0)
+    heads = far.shape[1]
+    slot_len, width = x_ref.shape
+    blocks = slot_len // tile
+    pair = 2 * width // heads
+    length = lengths[seq]
+
+    def clear():
+        spread_bias(lines_ref, near_ref, heads)
+        near_sums[...] = jnp.zeros_like(near_sums)
+        far_sums[...] = jnp.zeros_like(far_sums)
+        gains_ref[...] = jnp.zeros_like(gains_ref)
+
+    pl.when(seq == 0)(clear)
+    places = lax.broadcasted_iota(jnp.int32, (slot_len, 1), 0)
+    lanes = lax.broadcasted_iota(jnp.int32, (1, pair), 1)
+
+    def attend(index, carry):
+        span = pl.ds(pl.multiple_of(index * pair, pair), pair)
+        keys = k_ref[:, span]
+        queries = q_ref[:, span]
+        values = v_ref[:, span]
+        upstream = context_grad[:, span]
+        by_query = by_key = by_value = None
+        for side in range(2):
+            head = 2 * index + side
+            mine = (lanes // (pair // 2) == side).astype(jnp.bfloat16)
+            my_queries, my_upstream = queries * mine, upstream * mine
+            raw = dot_across(keys, my_queries)
+            soft_grad = dot_across(values, my_upstream)
+            totals = lse_ref[0, pl.ds(head, 1), :]
+            inner = jnp.zeros((1, slot_len), jnp.float32)
+            low_rows = []
+            for block in range(blocks):
+                part = slice(block * tile, (block + 1) * tile)
+                bias = bias_row(near_ref, head, block, blocks, far[0, head], far[1, head], True)
+                scores = jnp.where(places[part] < length, raw[part] + bias, masked_score)
+                soft = jnp.exp(scores - totals)
+                soft_ref[part] = soft
+                low_rows.append(soft.astype(jnp.bfloat16))
+                inner += jnp.sum(soft * soft_grad[part], axis=0, keepdims=True)
+            soft_low = jnp.concatenate(low_rows, axis=0)
+            grad_rows = []
+            near_total = [None] * 3
+            far_total = [None] * 2
+            for block in range(blocks):
+                part = slice(block * tile, (block + 1) * tile)
+                grads = soft_ref[part] * (soft_grad[part] - inner)
+                grad_rows.append(grads.astype(jnp.bfloat16))
+                for other in range(blocks):
+                    piece = grads[:, other * tile : (other + 1) * tile]
+                    ahead = block - other
+                    group, spot = (near_total, 1 - ahead) if abs(ahead) <= 1 else (far_total, int(ahead > 0))
+                    group[spot] = piece if group[spot] is None else group[spot] + piece
+            for spot in range(3):
+                if near_total[spot] is not None:
+                    near_sums[head, :, spot * tile : (spot + 1) * tile] += near_total[spot]
+            for spot in range(2):
+                if far_total[spot] is not None:
+                    far_sums[spot, pl.ds(head, 1), :] += jnp.sum(far_total[spot], axis=0, keepdims=True)
+            grads_low = jnp.concatenate(grad_rows, axis=0)
+            pieces = (
+                lax.dot_general(grads_low, keys * mine, (((0,), (0,)), ((), ())), preferred_element_type=jnp.float32),
+                low_dot(grads_low, my_queries),
+                low_dot(soft_low, my_upstream),
+            )
+            if side == 0:
+                by_query, by_key, by_value = pieces
+            else:
+                by_query, by_key, by_value = by_query + pieces[0], by_key + pieces[1], by_value + pieces[2]
+        dq_ref[:, span] = by_query.astype(jnp.bfloat16)
+        dk_ref[:, span] = by_key.astype(jnp.bfloat16)
+        dv_ref[:, span] = by_value.astype(jnp.bfloat16)
+        return carry
+
+    lax.fori_loop(0, heads // 2, attend, 0)
+    normed_grad = dot_across(dq_ref[...], wq[...]) + dot_across(dk_ref[...], wk[...])
+    normed_grad += dot_across(dv_ref[...], wv[...])
+    by_tokens, token_gain = norm_back(x_ref[...].astype(jnp.float32), gain_a[...], normed_grad)
+    gains_ref[0:1] += token_gain
+    token_ref[...] = (mixed_grad[...] + by_tokens).astype(jnp.bfloat16)
+
+    def close():
+        for head in range(heads):
+            turned = jnp.concatenate([near_sums[head], jnp.zeros((tile, tile), jnp.float32)], axis=1)
+            count = tile // 2
+            while count:
+                upper = turned[count : 2 * count]
+                turned = turned[:count] + pltpu.roll(upper, 4 * tile - count, 1)
+                count //= 2
+            line = turned
+            sums_ref[head : head + 1, :] = line
+        sums_ref[:, 2 * tile : 3 * tile] += far_sums[0]
+        sums_ref[:, 3 * tile : 4 * tile] += far_sums[1]
+
+    sums_ref[...] = jnp.zeros_like(sums_ref)
+    pl.when(seq == pl.num_programs(0) - 1)(close)
+
+
+def whole(shape):
+    return pl.BlockSpec(shape, lambda n, *_: (0,) * len(shape), pipeline_mode=pl.Buffered(1))
+
+
+def run_feed_back(lengths, prefixes, gains, weights, mixed, hidden, output, pooled_grad):
+    rows, width = mixed.shape
+    seqs = lengths.shape[0]
+    slot_len = rows // seqs
+    wo, widen, narrow = weights
+    ff = widen.shape[1]
+
+    def block(columns):
+        return pl.BlockSpec((slot_len, columns), lambda n, *_: (n, 0))
+
+    def shape(columns, kind):
+        return jax.ShapeDtypeStruct((rows, columns), kind)
+
+    low, full = jnp.bfloat16, jnp.float32
+    return pl.pallas_call(
+        feed_back_kernel,
+        grid_spec=pltpu.PrefetchScalarGridSpec(
+            num_scalar_prefetch=2,
+            grid=(seqs,),
+            in_specs=[
+                whole((width, width)), whole((1, width)), whole((width, ff)), whole((ff, width)), whole((1, width)),
+                block(width), block(ff), block(width),
+                pl.BlockSpec((1, 1, width), lambda n, *_: (n, 0, 0)),
+            ],
+            out_specs=[
+                block(width), block(ff), block(width), block(width), block(width),
+                pl.BlockSpec((8, width), lambda n, *_: (0, 0)),
+            ],
+            scratch_shapes=[pltpu.VMEM((slot_len, width), jnp.float32)],
+        ),
+        out_shape=(
+            shape(width, low), shape(ff, low), shape(width, low), shape(width, low), shape(width, full),
+            jax.ShapeDtypeStruct((8, width), full),
+        ),
+        compiler_params=pltpu.CompilerParams(vmem_limit_bytes=60000000),
+        name="feed_back",
+    )(lengths, prefixes, wo, gains[0][None], widen, narrow, gains[1][None], mixed, hidden, output, pooled_grad)
+
+
+def run_attend_back(tokens, lengths, far, lines, gain, weights, saved, context_grad, mixed_grad):
+    rows, width = tokens.shape
+    seqs = lengths.shape[0]
+    slot_len = rows // seqs
+    heads = far.shape[1]
+
+    def block(columns):
+        return pl.BlockSpec((slot_len, columns), lambda n, *_: (n, 0))
+
+    square = whole((width, width))
+    low, full = jnp.bfloat16, jnp.float32
+    return pl.pallas_call(
+        attend_back_kernel,
+        grid_spec=pltpu.PrefetchScalarGridSpec(
+            num_scalar_prefetch=2,
+            grid=(seqs,),
+            in_specs=[
+                block(width), whole((16, 4 * tile)), whole((1, width)), square, square, square,
+                block(width), block(width), block(width),
+                pl.BlockSpec((1, 16, slot_len), lambda n, *_: (n, 0, 0)),
+                block(width), block(width),
+            ],
+            out_specs=[
+                block(width), block(width), block(width), block(width),
+                pl.BlockSpec((8, width), lambda n, *_: (0, 0)),
+                pl.BlockSpec((16, 4 * tile), lambda n, *_: (0, 0)),
+            ],
+            scratch_shapes=[
+                pltpu.VMEM((heads, tile, near), full),
+                pltpu.VMEM((2, 16, tile), full),
+                pltpu.VMEM((heads, tile, near), full),
+                pltpu.VMEM((slot_len, slot_len), full),
+            ],
+        ),
+        out_shape=(
+            *(jax.ShapeDtypeStruct((rows, width), low) for _ in range(4)),
+            jax.ShapeDtypeStruct((8, width), full),
+            jax.ShapeDtypeStruct((16, 4 * tile), full),
+        ),
+        compiler_params=pltpu.CompilerParams(vmem_limit_bytes=60000000),
+        name="attend_back",
+    )(lengths, far, tokens, lines, gain[None], *weights, *saved, context_grad, mixed_grad)
+
+
+def bucket_sums(offset_sums, shape):
+    spots = jnp.arange(4 * tile, dtype=jnp.int32)
+    moved = jnp.where(spots >= near, spots - 4 * tile, spots)
+    onehot = offset_onehot(tile - moved, shape[0])
+    return jnp.dot(onehot.T, offset_sums[: shape[1]].T, precision=highest)
 
 
 def local(
@@ -448,60 +847,15 @@
     gain_final,
 ):
     seqs = lengths.shape[1]
-    rows = tokens.shape[1]
-    slot_len = rows // seqs
     width = tokens.shape[2]
-    heads = bucket_bias.shape[1]
-    head_dim = query_weight.shape[1] // heads
-    inner = heads * head_dim
-    tokens_f = tokens[0].astype(jnp.float32)
-    seq_lengths = lengths[0]
-    seq_prefix = prefixes[0]
-    onehot = bucket_onehot(slot_len, bucket_bias.shape[0])
-    bias = jnp.einsum("ijb,bh->hij", onehot, bucket_bias, precision=highest)
-    normed_f, inverse_first = norm_forward(tokens_f, gain_attention)
-    normed = normed_f.astype(jnp.bfloat16)
-
-    def project(matrix):
-        projected = jnp.dot(normed, matrix, preferred_element_type=jnp.float32).astype(jnp.bfloat16)
-        return projected.reshape(seqs, slot_len, heads, head_dim)
-
-    query_all = project(query_weight)
-    key_all = project(key_weight)
-    value_all = project(value_weight)
-    places = jnp.arange(slot_len, dtype=jnp.int32)
-    valid = places[None, :] < seq_lengths[:, None]
-
-    def score_block(query_rows, key_rows, valid_keys):
-        raw_scores = jnp.einsum(
-            "ihd,jhd->hij", query_rows, key_rows, preferred_element_type=jnp.float32
-        )
-        return jnp.where(valid_keys[None, None, :], raw_scores + bias, masked_score)
-
-    def attend_forward(parts):
-        query_rows, key_rows, value_rows, valid_keys = parts
-        scores = score_block(query_rows, key_rows, valid_keys)
-        row_peak = jnp.max(scores, axis=-1, keepdims=True)
-        raised = jnp.exp(scores - row_peak)
-        totals = jnp.sum(raised, axis=-1, keepdims=True)
-        soft_low = (raised / totals).astype(jnp.bfloat16)
-        context = jnp.einsum(
-            "hij,jhd->ihd", soft_low, value_rows, preferred_element_type=jnp.float32
-        )
-        return (context.astype(jnp.bfloat16), (row_peak + jnp.log(totals))[:, :, 0])
-
-    context, log_totals = lax.map(attend_forward, (query_all, key_all, value_all, valid))
-    context_flat = context.reshape(rows, inner)
-    mixed = tokens_f + jnp.dot(context_flat, output_weight, preferred_element_type=jnp.float32)
-    ffn_in_f, inverse_second = norm_forward(mixed, gain_feedforward)
-    ffn_in = ffn_in_f.astype(jnp.bfloat16)
-    pre_act = jnp.dot(ffn_in, widen_weight, preferred_element_type=jnp.float32)
-    hidden = jnp.where(pre_act > 0, pre_act, 0.0).astype(jnp.bfloat16)
-    output = mixed + jnp.dot(hidden, narrow_weight, preferred_element_type=jnp.float32)
-    final, inverse_third = norm_forward(output, gain_final)
-    pool_mask = ((places[None, :] >= seq_prefix[:, None]) & valid).astype(jnp.float32)
-    pool_weight = pool_mask / jnp.sum(pool_mask, axis=1, keepdims=True)
-    pooled = jnp.sum(final.reshape(seqs, slot_len, width) * pool_weight[:, :, None], axis=1)
+    buckets = bucket_bias.shape[0]
+    far = jnp.stack([bucket_bias[buckets // 2 - 1], bucket_bias[buckets - 1]])
+    gains = (gain_attention, gain_feedforward, gain_final)
+    weights = (query_weight, key_weight, value_weight, output_weight, widen_weight, narrow_weight)
+    normed, query, key, value, totals, context, mixed, ffn_in, hidden, output, pooled = run_forward(
+        tokens[0], lengths[0], prefixes[0], far, bias_lines(bucket_bias, False), gains, weights
+    )
+    pooled = pooled[:, 0]
     inverse_pool = lax.rsqrt(jnp.sum(pooled * pooled, axis=-1, keepdims=True) + epsilon)
     unit = pooled * inverse_pool
     gathered = gather_blocks(unit, batch_size, 0).reshape(2 * batch_size * seqs, width)
@@ -534,103 +888,41 @@
     grad_pooled = inverse_pool * grad_unit - pooled * cubed * jnp.sum(
         grad_unit * pooled, axis=-1, keepdims=True
     )
-    grad_fin = (pool_weight[:, :, None] * grad_pooled[:, None, :]).reshape(rows, width)
-    grad_out, grad_final = norm_backward(output, inverse_third, gain_final, grad_fin)
-    grad_branch = grad_out.astype(jnp.bfloat16)
-    grad_hidden = jnp.einsum(
-        "td,fd->tf", grad_branch, narrow_weight, preferred_element_type=jnp.float32
-    )
-    grad_pre = jnp.where(pre_act > 0, grad_hidden, 0.0).astype(jnp.bfloat16)
-    grad_ffn_in = jnp.einsum(
-        "tf,df->td", grad_pre, widen_weight, preferred_element_type=jnp.float32
-    )
-    grad_mixed_norm, grad_feedforward = norm_backward(
-        mixed, inverse_second, gain_feedforward, grad_ffn_in
-    )
-    grad_mixed = grad_out + grad_mixed_norm
-    grad_attn = grad_mixed.astype(jnp.bfloat16)
-    grad_context = jnp.einsum(
-        "td,id->ti", grad_attn, output_weight, preferred_element_type=jnp.float32
-    )
-    grad_context = grad_context.astype(jnp.bfloat16).reshape(seqs, slot_len, heads, head_dim)
-
-    def attend_backward(bias_total, parts):
-        query_rows, key_rows, value_rows, valid_keys, log_rows, context_grad = parts
-        scores_here = score_block(query_rows, key_rows, valid_keys)
-        soft = jnp.exp(scores_here - log_rows[:, :, None])
-        soft_low = soft.astype(jnp.bfloat16)
-        value_part = jnp.einsum(
-            "hij,ihd->jhd", soft_low, context_grad, preferred_element_type=jnp.float32
-        )
-        grad_soft = jnp.einsum(
-            "ihd,jhd->hij", context_grad, value_rows, preferred_element_type=jnp.float32
-        )
-        grad_scores = soft * (grad_soft - jnp.sum(grad_soft * soft, axis=-1, keepdims=True))
-        scores_low = grad_scores.astype(jnp.bfloat16)
-        query_part = jnp.einsum(
-            "hij,jhd->ihd", scores_low, key_rows, preferred_element_type=jnp.float32
-        )
-        key_part = jnp.einsum(
-            "hij,ihd->jhd", scores_low, query_rows, preferred_element_type=jnp.float32
-        )
-        return (
-            bias_total + grad_scores,
-            (
-                query_part.astype(jnp.bfloat16),
-                key_part.astype(jnp.bfloat16),
-                value_part.astype(jnp.bfloat16),
-            ),
-        )
-
-    bias_total, (query_grads, key_grads, value_grads) = lax.scan(
-        attend_backward,
-        jnp.zeros(bias.shape, jnp.float32),
-        (query_all, key_all, value_all, valid, log_totals, grad_context),
-    )
-    query_grads = query_grads.reshape(rows, inner)
-    key_grads = key_grads.reshape(rows, inner)
-    value_grads = value_grads.reshape(rows, inner)
-    grad_bucket = jnp.einsum("ijb,hij->bh", onehot, bias_total, precision=highest)
-    grad_normed = (
-        jnp.einsum("ti,di->td", query_grads, query_weight, preferred_element_type=jnp.float32)
-        + jnp.einsum("ti,di->td", key_grads, key_weight, preferred_element_type=jnp.float32)
-        + jnp.einsum("ti,di->td", value_grads, value_weight, preferred_element_type=jnp.float32)
-    )
-    grad_tokens_norm, grad_attention = norm_backward(
-        tokens_f, inverse_first, gain_attention, grad_normed
-    )
-    token_gradient = (grad_mixed + grad_tokens_norm).astype(jnp.bfloat16)[None]
-    buckets = grad_bucket.reshape(-1)
-    lines = [grad_attention, grad_feedforward, grad_final]
-    lines.append(jnp.pad(buckets, (0, width - buckets.shape[0])))
-    block = jnp.concatenate([jnp.stack(lines), jnp.zeros((4, width), jnp.float32)])
-    weights, sums = sum_weights(
-        batch_size, 1, hidden, ffn_in, context_flat, normed,
-        grad_branch, grad_pre, grad_attn, query_grads, key_grads, value_grads, block,
-    )
-    sum_attention, sum_feedforward, sum_final = sums[0], sums[1], sums[2]
-    sum_bucket = sums[3, : buckets.shape[0]].reshape(grad_bucket.shape)
+    branch, pre, attn, context_grad, mixed_grad, feed_gains = run_feed_back(
+        lengths[0], prefixes[0], gains[1:], weights[3:], mixed, hidden, output, grad_pooled[:, None]
+    )
+    by_query, by_key, by_value, token_gradient, token_gains, offset_sums = run_attend_back(
+        tokens[0], lengths[0], far, bias_lines(bucket_bias, True), gain_attention, weights[:3],
+        (query, key, value, totals), context_grad, mixed_grad,
+    )
+    gain_sums = feed_gains + token_gains
+    grad_bucket = bucket_sums(offset_sums, bucket_bias.shape)
+    flat = grad_bucket.reshape(-1)
+    block = gain_sums.at[3, : flat.shape[0]].set(flat)
+    summed, sums = sum_weights(
+        batch_size, 1, hidden, ffn_in, context, normed, branch, pre, attn, by_query, by_key, by_value, block
+    )
+    sum_bucket = sums[3, : flat.shape[0]].reshape(bucket_bias.shape)
     ff = hidden.shape[1]
-    sum_narrow = weights[:ff]
-    sum_widen = weights[ff : 2 * ff].reshape(ff // width, width, width)
+    sum_widen = summed[ff : 2 * ff].reshape(ff // width, width, width)
     sum_widen = sum_widen.transpose(1, 0, 2).reshape(width, ff)
     sum_output, sum_query, sum_key, sum_value = (
-        weights[2 * ff + n * width : 2 * ff + (n + 1) * width] for n in range(4)
+        summed[2 * ff + n * width : 2 * ff + (n + 1) * width] for n in range(4)
     )
     return (
         loss_value,
         my_rows,
-        token_gradient,
-        sum_attention,
+        token_gradient[None],
+        sums[0],
         sum_query,
         sum_key,
         sum_value,
         sum_output,
         sum_bucket,
-        sum_feedforward,
+        sums[1],
         sum_widen,
-        sum_narrow,
-        sum_final,
+        summed[:ff],
+        sums[2],
     )
 
 

time: 878 us -> 519 us (0.59); the launches traced: 865 us -> 518 us
  matrix products: 315 us -> 4.9 us
  Pallas kernels: 255 us -> 470 us
  local copies, waits for them, and re-layouts: 177 us -> 33.5 us
  other arithmetic: 113 us -> 5.75 us
    dot_general x42 -> x3, matrix products: 314 us -> 3.13 us  [the longest x2 2.01 us: bias_lines(): lines = jnp.dot(bucket_bias.T, onehot.T, precision=highest)]
    pallas_call x0 -> x3, Pallas kernels: none -> 215 us  [the longest x1 89.1 us: run_forward(): pl.pallas_call(forward_kernel, grid_spec=pltpu.PrefetchScalarGridSpec(num...]
    convert_element_type x8 -> x0, other arithmetic: 88.8 us -> none  [the longest x4 72.5 us: attend_backward(): scores_low = grad_scores.astype(jnp.bfloat16)]
    while x25 -> x0, local copies, waits for them, and re-layouts: 63.8 us -> none  [the longest x5 35.8 us: local(): lax.map(attend_forward, (query_all, key_all, value_all, valid))]
    reshape x9 -> x0, local copies, waits for them, and re-layouts: 43.5 us -> none  [the longest x3 18.6 us: project(): return projected.reshape(seqs, slot_len, heads, head_dim)]
    convert_element_type x4 -> x0, local copies, waits for them, and re-layouts: 18.5 us -> none  [the longest x3 13.9 us: project(): jnp.dot(normed, matrix, preferred_element_type=jnp.float32)]
    reduce_sum x8 -> x0, other arithmetic: 16.7 us -> none  [the longest x4 7.1 us: attend_forward(): totals = jnp.sum(raised, axis=-1, keepdims=True)]
    unnamed x85 -> x9, local copies, waits for them, and re-layouts: 16.8 us -> 0.88 us
where the time goes in v2:
time: 519 us; the launch traced here: 518 us
  Pallas kernels  470 us (91%)
  local copies, waits for them, and re-layouts  33.5 us (6%)
  other arithmetic  5.75 us (1%)
    pallas_call x1, Pallas kernels, sum_weights(): pl.pallas_call(functools.partial(sums_kernel, dims, jobs), out_shape=(jax...  242 us
    pallas_call x1, Pallas kernels, run_forward(): pl.pallas_call(forward_kernel, grid_spec=pltpu.PrefetchScalarGridSpec(num...  89.1 us
    pallas_call x1, Pallas kernels, run_attend_back(): pl.pallas_call(attend_back_kernel, grid_spec=pltpu.PrefetchScalarGridSpec...  79.4 us
    pallas_call x1, Pallas kernels, run_feed_back(): pl.pallas_call(feed_back_kernel, grid_spec=pltpu.PrefetchScalarGridSpec(n...  46.8 us
    pallas_call x1, Pallas kernels, gather_blocks(): pl.pallas_call(functools.partial(gather_kernel, groups), out_shape=jax.Sh...  13.2 us
    slice x1, local copies, waits for them, and re-layouts, local(): summed[:ff]  11 us

profile of v2, /device:TPU:0, one launch (start us, length us, event | category | flops | bytes accessed | tf_op | source)
XLA Modules:
  0.0 518.1 jit_solution(17582274544149557070)
XLA Ops:
  0.7 1.3 broadcast_in_dim.18.gain_a
  2.0 1.3 broadcast_in_dim.19.gain_f
  3.2 1.3 broadcast_in_dim.20.gain_z
  4.5 0.8 fusion.28
  5.5 0.6 pad_maximum_fusion.far
  6.1 1.0 convolution_bitcast_fusion.1
  7.1 0.6 pad.10.lines_ref
  7.7 1.0 convolution_bitcast_fusion
  8.7 0.6 pad.11.lines_ref
  9.4 89.1 %forward.1 = (bf16[2048,768]{1,0:T(8,128)(2,1)}, bf16[2048,768]{1,0:T(8,128)(2,1)}, bf16[2048,768]{1,0:T(8,128)(2,1)}, bf16[2048,768]{1,0:T(8,128)(2,1)}, f32[4,...) custom-call(s32[4]{0:T(128)} %bitcast.37, ...), custom_call_target="tpu_custom_call" | custom-call | tf_op jit(solution)/shard_map/forward/pallas_call | solution.py:555
  98.5 0.8 fusion.11
  99.3 1.4 bitcast_multiply_fusion.2.block_ref
  100.7 13.2 %gather_blocks.1 = f32[2,16,4,768]{3,2,1,0:T(4,128)} custom-call(f32[4,768]{1,0:T(4,128)} %bitcast_multiply_fusion.2.block_ref), custom_call_target="tpu_custom_call" | custom-call | tf_op jit(solution)/shard_map/gather_blocks/pallas_call | solution.py:85
  113.9 1.1 fusion.27
  115.1 0.4 fusion.24
  115.5 0.7 select_reduce_fusion
  116.3 0.3 convolution_multiply_fusion.1
  116.7 1.0 fusion.14
  117.7 0.6 add_reduce_fusion
  120.3 0.8 fusion.13
  121.1 0.6 broadcast_in_dim.21.pooled_ref
  121.7 46.8 %feed_back.1 = (bf16[2048,768]{1,0:T(8,128)(2,1)}, bf16[2048,3072]{1,0:T(8,128)(2,1)}, bf16[2048,768]{1,0:T(8,128)(2,1)}, bf16[2048,768]{1,0:T(8,128)(2,1)}, f32[2048,768]{1,0:T(8,128)}, /*index=5*/f32[8,768]{1,0:T(8,128)}) custom-call(s32[4]{0:T(128)} %bitcast.38, s32[4]{0:T(128)} %bitcast.41, bf16[768,768]{1,0:T(8,128)(2,1)} %wo.3, ...), custom_call_target="tpu_custom_call" | custom-call | tf_op jit(solution)/shard_map/feed_back/pallas_call | solution.py:756
  168.6 79.4 %attend_back.1 = (bf16[2048,768]{1,0:T(8,128)(2,1)}, bf16[2048,768]{1,0:T(8,128)(2,1)}, bf16[2048,768]{1,0:T(8,128)(2,1)}, bf16[2048,768]{1,0:T(8,128)(2,1)}, f32[8,768]{1,0:T(8,128)}, /*index=5*/f32[16,512]{1,0:T(8,128)}) custom-call(s32[4]{0:T(128)} %bitcast.39, f32[2,12]{1,0:T(2,128)} %pad_maximum_fusion.far, bf16[2048,768]{1,0:T(8,128)(2,1)} %bitcast.35, ...), custom_call_target="tpu_custom_call" | custom-call | tf_op jit(solution)/shard_map/attend_back/pallas_call | solution.py:792
  248.0 0.7 add.208
  248.8 1.1 fusion.2
  250.0 0.3 scatter.4.refs_10_
  250.3 241.5 %sum_weights.1 = (f32[9216,768]{1,0:T(8,128)}, f32[8,768]{1,0:T(8,128)S(1)}) custom-call(bf16[2048,3072]{1,0:T(8,128)(2,1)} %get-tuple-element.56.hidden_ref.refs_0_, bf16[2048,768]{1,0:T(8,128)(2,1)} %get-tuple-element.61.refs_1_, bf16[2048,768]{1,0:T(8,128)(2,1)} %get-tuple-element.62.refs_2_, bf16[2048,768]{1,0:T(8,128)(2,1)} %get-tuple-element.63.refs_3_, ...), custom_call_target="tpu_custom_call" | custom-call | tf_op jit(solution)/shard_map/sum_weights/pallas_call | solution.py:378
  491.8 0.6 slice_reduce_fusion
  492.6 0.7 copy.36
  493.3 7.6 %fusion.26 = (f32[768,768]{1,0:T(8,128)}, f32[768,768]{1,0:T(8,128)}, f32[768,768]{1,0:T(8,128)}, f32[768,768]{1,0:T(8,128)}) fusion(f32[9216,768]{1,0:T(8,128)} %get-tuple-element.74), kind=kLoop, calls=%fused_computation.54 | loop fusion | bytes 18874368 | tf_op jit(solution)/shard_map/slice | solution.py:910
  500.8 11.0 %fusion.25 = (f32[3072,768]{1,0:T(8,128)}, f32[3072,768]{1,0:T(8,128)S(1)}) fusion(f32[9216,768]{1,0:T(8,128)} %get-tuple-element.74), kind=kLoop, calls=%fused_computation.53 | loop fusion | bytes 37748736 | tf_op jit(solution)/shard_map/slice | solution.py:924
  511.8 5.2 copy.41
  (18 shorter events, 0.7 us)
Async XLA Ops:
  9.4 106.2 %copy-start.2 = (s32[64]{0:T(128)S(1)}, s32[64]{0:T(128)}, u32[]{:S(2)}) copy-start(s32[64]{0:T(128)} %param.19) | copy-start | bytes 772
  116.7 51.8 %copy-start.1 = (f32[4,64]{1,0:T(4,128)}, f32[4,64]{1,0:T(4,128)S(1)}, u32[]{:S(2)}) copy-start(f32[4,64]{1,0:T(4,128)S(1)} %constant_dynamic-slice_fusion) | copy-start | bytes 3076
  168.5 79.5 %copy-start = (f32[8,768]{1,0:T(8,128)S(1)}, f32[8,768]{1,0:T(8,128)}, u32[]{:S(2)}) copy-start(f32[8,768]{1,0:T(8,128)} %get-tuple-element.70) | copy-start | bytes 73732

commit v3 on v2

--- a/solution.py
+++ b/solution.py
@@ -145,17 +145,21 @@
     return add, spread[::-1]
 
 
+def one_way_steps(order, dims):
+    flags = []
+    for name in order:
+        flags += [True, False] if dims[name][1] == 4 else [False]
+    return flags
+
+
 def step_rings(order, dims):
-    one_way = []
-    for name in order:
-        one_way += [True, False] if dims[name][1] == 4 else [False]
-    count = len(one_way)
-    steps = 2 + 2 * count
+    flags = one_way_steps(order, dims)
+    steps = 2 + 2 * len(flags)
     rings = [3] * steps
-    for index, single in enumerate(one_way):
+    for index, single in enumerate(flags):
         if single:
             first, last = 1 + index, steps - 2 - index
-            rings[first] = rings[last] = last - first + 2
+            rings[last] = last - first + 2
     return rings
 
 
@@ -173,39 +177,49 @@
 
 
 def sums_kernel(dims, jobs, *refs):
-    (hidden, ffn_in, context, normed, branch, pre, attn, dq, dk, dv, small, out, small_out) = refs[:13]
-    (left, right, part, acc, full, mate_in, small_own, small_in) = refs[13:21]
-    rest = refs[21:]
+    (lengths, far, hidden, ffn_in, context, normed, branch, pre, attn, query, key, value, upstream) = refs[:13]
+    (tokens, mixed_grad, small, totals, lines, gain, wq, wk, wv) = refs[13:22]
+    (out, token_out, small_out) = refs[22:25]
+    (left, right, part, acc, full, mate_in, small_own, small_in, heads_in, by_query, by_key, by_value) = refs[25:37]
+    (near_ref, near_sums, far_sums, soft_ref, token_in, mixed_in, token_buffer) = refs[37:44]
+    rest = refs[44:]
     counts = [len(stage_rows(order, dims, 8)) for order in orders]
     inbox, where = [], 0
     for count in counts:
         inbox.append(rest[where : where + count])
         where += count
-    load_sem, send_sem, recv_sem, keep_sem, small_sem = rest[where:]
+    load_sem, send_sem, recv_sem, keep_sem, small_sem, heads_sem, token_sem, credit = rest[where:]
     tower, batch = place()
     half = unit_rows // 2
     steps = 2 + 2 * counts[0]
+    slots = jobs + steps + 1
     plans = [plan_unit(order, dims, batch, half) for order in orders]
     rings = [step_rings(order, dims) for order in orders]
+    single = [one_way_steps(order, dims) for order in orders]
     held, spread_held = acc.shape[0], full.shape[0]
+    width = out.shape[1]
+    heads = far.shape[1]
+    seqs = lengths.shape[0]
+    slot_len = tokens.shape[0] // seqs
+    pair = 2 * width // heads
+    pairs = heads // 2
+    tasks = seqs * pairs
+    blocks = slot_len // tile
 
     barrier = pltpu.get_barrier_semaphore()
     mate = (1 - tower, batch)
     mates, turns = [mate], [mate]
     for stride, size in dims.values():
         coord = lax.rem(batch // stride, size)
-        near = (tower, batch + stride * (1 - 2 * lax.rem(coord, 2)))
-        mates.append(near)
-        turns.append(near)
+        near_mate = (tower, batch + stride * (1 - 2 * lax.rem(coord, 2)))
+        mates.append(near_mate)
+        turns.append(near_mate)
         if size == 4:
             mates.append((tower, batch + stride * (3 - 2 * coord)))
             turns.append((tower, batch + stride * (2 - 4 * (coord // 2))))
             mates.append(turns[-1])
-    for mate in mates:
-        pl.semaphore_signal(barrier, 1, device_id=mate, device_id_type=MESH)
-    pl.semaphore_wait(barrier, len(mates))
-
-    width = out.shape[1]
+    for other in mates:
+        pl.semaphore_signal(barrier, 1, device_id=other, device_id_type=MESH)
 
     def load(job, begin):
         slot = lax.rem(job, 2)
@@ -228,7 +242,10 @@
         first = 0
         table = [(hidden, branch, per_narrow)]
         table.append((ffn_in, pre, per_narrow))
-        table += [(context, attn, per_side), (normed, dq, per_side), (normed, dk, per_side), (normed, dv, per_side)]
+        table += [
+            (context, attn, per_side), (normed, by_query, per_side),
+            (normed, by_key, per_side), (normed, by_value, per_side),
+        ]
         for index, (left_ref, right_ref, count) in enumerate(table):
             local = job - first
 
@@ -282,8 +299,12 @@
         base = unit * half
         first = pl.multiple_of(job * job_rows + unit * unit_rows + tower * half, 8)
         return pltpu.make_async_copy(
-            full.at[lax.rem(job, spread_held), pl.ds(base, half)], out.at[pl.ds(first, half)], keep_sem.at[unit, lax.rem(job, 2)]
+            full.at[lax.rem(job, spread_held), pl.ds(base, half)], out.at[pl.ds(first, half)],
+            keep_sem.at[unit, lax.rem(job, 2)],
         )
+
+    def one_way(unit, step):
+        return 1 <= step <= counts[unit] and single[unit][step - 1]
 
     def finish(unit, step, job):
         copy, sends, receives = remote(unit, step, job)
@@ -306,6 +327,13 @@
                     full[lax.rem(job, spread_held), rows] = total
                 else:
                     acc[place_in, rows] = total
+                if one_way(unit, step):
+                    pl.when(job + rings[unit][step] < jobs)(
+                        lambda: pl.semaphore_signal(
+                            credit.at[unit * steps + step], 1,
+                            device_id=(tower, item["peer"]), device_id_type=MESH,
+                        )
+                    )
 
         guarded(receives, arrived)
         if step == steps - 1:
@@ -317,7 +345,15 @@
                 finish(unit, step - 1, job)
             if step < steps:
                 copy, sends, _ = remote(unit, step, job)
-                guarded(sends, copy.start)
+
+                def begin(copy=copy, unit=unit):
+                    if one_way(unit, step):
+                        pl.when(job >= rings[unit][step])(
+                            lambda: pl.semaphore_wait(credit.at[unit * steps + step], 1)
+                        )
+                    copy.start()
+
+                guarded(sends, begin)
                 if step == steps - 1:
                     keep(unit, job).start()
 
@@ -332,9 +368,7 @@
         )
 
     def small_turn(turn):
-        if turn == 0:
-            small_own[0] = small[...]
-        else:
+        if turn > 0:
             small_copy(turn - 1).wait()
             total = small_own[turn - 1] + small_in[turn - 1]
             if turn == len(turns):
@@ -344,23 +378,150 @@
         if turn < len(turns):
             small_copy(turn).start()
 
+    def heads_load(task, begin):
+        rows = pl.ds(pl.multiple_of(task // pairs * slot_len, slot_len), slot_len)
+        columns = pl.ds(pl.multiple_of(lax.rem(task, pairs) * pair, pair), pair)
+        slot = lax.rem(task, 2)
+        for index, ref in enumerate((query, key, value, upstream)):
+            copy = pltpu.make_async_copy(
+                ref.at[rows, columns], heads_in.at[slot, index], heads_sem.at[slot, index]
+            )
+            copy.start() if begin else copy.wait()
+
+    places = lax.broadcasted_iota(jnp.int32, (slot_len, 1), 0)
+    lanes = lax.broadcasted_iota(jnp.int32, (1, pair), 1)
+
+    def attend(task, carry):
+        seq, index = task // pairs, lax.rem(task, pairs)
+        slot = lax.rem(task, 2)
+        heads_load(task, False)
+        pl.when(task + 1 < tasks)(lambda: heads_load(task + 1, True))
+        queries, keys, values, upper = (heads_in[slot, n] for n in range(4))
+        length = lengths[seq]
+        grads_out = [None] * 3
+        for side in range(2):
+            head = 2 * index + side
+            mine = (lanes // (pair // 2) == side).astype(jnp.bfloat16)
+            my_queries, my_upper = queries * mine, upper * mine
+            raw = dot_across(keys, my_queries)
+            soft_grad = dot_across(values, my_upper)
+            line = totals[seq, pl.ds(head, 1), :]
+            inner = jnp.zeros((1, slot_len), jnp.float32)
+            low_rows = []
+            for block in range(blocks):
+                span = slice(block * tile, (block + 1) * tile)
+                bias = bias_row(near_ref, head, block, blocks, far[0, head], far[1, head], True)
+                scores = jnp.where(places[span] < length, raw[span] + bias, masked_score)
+                soft = jnp.exp(scores - line)
+                soft_ref[span] = soft
+                low_rows.append(soft.astype(jnp.bfloat16))
+                inner += jnp.sum(soft * soft_grad[span], axis=0, keepdims=True)
+            soft_low = jnp.concatenate(low_rows, axis=0)
+            grad_rows = []
+            near_total = [None] * 3
+            far_total = [None] * 2
+            for block in range(blocks):
+                span = slice(block * tile, (block + 1) * tile)
+                grads = soft_ref[span] * (soft_grad[span] - inner)
+                grad_rows.append(grads.astype(jnp.bfloat16))
+                for other in range(blocks):
+                    piece = grads[:, other * tile : (other + 1) * tile]
+                    ahead = block - other
+                    group, spot = (near_total, 1 - ahead) if abs(ahead) <= 1 else (far_total, int(ahead > 0))
+                    group[spot] = piece if group[spot] is None else group[spot] + piece
+            for spot in range(3):
+                if near_total[spot] is not None:
+                    near_sums[head, :, spot * tile : (spot + 1) * tile] += near_total[spot]
+            for spot in range(2):
+                if far_total[spot] is not None:
+                    far_sums[spot, pl.ds(head, 1), :] += jnp.sum(far_total[spot], axis=0, keepdims=True)
+            grads_low = jnp.concatenate(grad_rows, axis=0)
+            pieces = (
+                lax.dot_general(grads_low, keys * mine, (((0,), (0,)), ((), ())), preferred_element_type=jnp.float32),
+                low_dot(grads_low, my_queries),
+                low_dot(soft_low, my_upper),
+            )
+            grads_out = [new if old is None else old + new for old, new in zip(grads_out, pieces)]
+        rows = pl.ds(pl.multiple_of(seq * slot_len, slot_len), slot_len)
+        columns = pl.ds(pl.multiple_of(index * pair, pair), pair)
+        for ref, grads in zip((by_query, by_key, by_value), grads_out):
+            ref[rows, columns] = grads.astype(jnp.bfloat16)
+        return carry
+
+    def token_load(seq, begin):
+        rows = pl.ds(pl.multiple_of(seq * slot_len, slot_len), slot_len)
+        for index, (ref, target) in enumerate(((tokens, token_in), (mixed_grad, mixed_in))):
+            copy = pltpu.make_async_copy(ref.at[rows], target, token_sem.at[index])
+            copy.start() if begin else copy.wait()
+
+    def token_store(seq):
+        rows = pl.ds(pl.multiple_of(seq * slot_len, slot_len), slot_len)
+        return pltpu.make_async_copy(token_buffer, token_out.at[rows], token_sem.at[2])
+
+    def token_task(seq):
+        rows = pl.ds(pl.multiple_of(seq * slot_len, slot_len), slot_len)
+        token_load(seq, False)
+        normed_grad = dot_across(by_query[rows, :], wq[...]) + dot_across(by_key[rows, :], wk[...])
+        normed_grad += dot_across(by_value[rows, :], wv[...])
+        by_tokens, token_gain = norm_back(token_in[...].astype(jnp.float32), gain[...], normed_grad)
+        small_own[0, 0:1] += token_gain
+        pl.when(seq > 0)(lambda: token_store(seq - 1).wait())
+        token_buffer[...] = (mixed_in[...] + by_tokens).astype(jnp.bfloat16)
+        token_store(seq).start()
+        pl.when(seq + 1 < seqs)(lambda: token_load(seq + 1, True))
+
+    def close():
+        token_store(seqs - 1).wait()
+        small_own[0, 8:24, :] = jnp.zeros((16, width), jnp.float32)
+        for head in range(heads):
+            turned = jnp.concatenate([near_sums[head], jnp.zeros((tile, tile), jnp.float32)], axis=1)
+            count = tile // 2
+            while count:
+                upper = turned[count : 2 * count]
+                turned = turned[:count] + pltpu.roll(upper, 4 * tile - count, 1)
+                count //= 2
+            small_own[0, 8 + head : 9 + head, : 4 * tile] = turned
+        small_own[0, 8:24, 2 * tile : 3 * tile] += far_sums[0]
+        small_own[0, 8:24, 3 * tile : 4 * tile] += far_sums[1]
+
     load(0, True)
+    heads_load(0, True)
+    token_load(0, True)
+    spread_bias(lines, near_ref, heads)
+    near_sums[...] = jnp.zeros_like(near_sums)
+    far_sums[...] = jnp.zeros_like(far_sums)
+    small_own[0, 0:8, :] = small[...]
+    pl.semaphore_wait(barrier, len(mates))
+
+    last_attend = jobs - 3 * (width // job_rows)
+    first_small = slots - 1 - len(turns)
+    first_token = first_small - 1 - seqs
 
     def slot(time, carry):
         for step in range(steps, -1, -1):
             job = time - 1 - step
             pl.when(jnp.logical_and(job >= 0, job < jobs))(functools.partial(advance, step, job))
         for turn in range(len(turns) + 1):
-            pl.when(time == turn)(functools.partial(small_turn, turn))
+            pl.when(time == first_small + turn)(functools.partial(small_turn, turn))
+        begin = jnp.minimum(time * tasks // last_attend, tasks)
+        end = jnp.minimum((time + 1) * tasks // last_attend, tasks)
+        lax.fori_loop(begin, end, attend, 0)
         pl.when(time < jobs)(functools.partial(compute, time))
+        seq = time - first_token
+        pl.when(jnp.logical_and(seq >= 0, seq < seqs))(functools.partial(token_task, seq))
+        pl.when(time == first_small - 1)(close)
         return carry
 
-    lax.fori_loop(0, jobs + steps + 1, slot, 0)
-
-
-def sum_weights(batch_size, collective, *arrays):
-    hidden, normed = arrays[0], arrays[3]
+    lax.fori_loop(0, slots, slot, 0)
+
+
+def sum_weights(batch_size, collective, lengths, far, streamed, small, resident):
+    hidden, normed = streamed[0], streamed[3]
     tokens, width = normed.shape
+    seqs = lengths.shape[0]
+    heads = far.shape[1]
+    slot_len = tokens // seqs
+    pair = 2 * width // heads
     total = 2 * hidden.shape[1] + 4 * width
     jobs = total // job_rows
     dims = batch_dims(batch_size)
@@ -374,36 +535,55 @@
     steps = len(rings[0])
     longest = max(max(ring) for ring in rings)
     turns = 1 + sum(size // 2 for _, size in dims.values())
-    small = arrays[-1]
+    lines = 24
+    low, full = jnp.bfloat16, jnp.float32
+    in_vmem = pl.BlockSpec(memory_space=pltpu.VMEM)
+    in_smem = pl.BlockSpec(memory_space=pltpu.SMEM)
+    anywhere = pl.BlockSpec(memory_space=pl.ANY)
     return pl.pallas_call(
         functools.partial(sums_kernel, dims, jobs),
         out_shape=(
-            jax.ShapeDtypeStruct((total, width), jnp.float32),
-            jax.ShapeDtypeStruct(small.shape, jnp.float32),
+            jax.ShapeDtypeStruct((total, width), full),
+            jax.ShapeDtypeStruct((tokens, width), low),
+            jax.ShapeDtypeStruct((lines, width), full),
         ),
-        in_specs=[pl.BlockSpec(memory_space=pl.ANY)] * 10 + [pl.BlockSpec(memory_space=pltpu.VMEM)],
-        out_specs=(pl.BlockSpec(memory_space=pl.ANY), pl.BlockSpec(memory_space=pltpu.VMEM)),
+        in_specs=[in_smem] * 2 + [anywhere] * len(streamed) + [in_vmem] * (1 + len(resident)),
+        out_specs=(anywhere, anywhere, in_vmem),
         scratch_shapes=[
-            pltpu.VMEM((2, tokens, job_rows), jnp.bfloat16),
-            pltpu.VMEM((2, tokens, width), jnp.bfloat16),
-            pltpu.VMEM((2, job_rows, width), jnp.float32),
-            pltpu.VMEM((steps // 2, 3 * half, width), jnp.float32),
-            pltpu.VMEM((steps, 3 * half, width), jnp.float32),
-            pltpu.VMEM((3, 3 * half, width), jnp.float32),
-            pltpu.VMEM((turns,) + small.shape, jnp.float32),
-            pltpu.VMEM((turns,) + small.shape, jnp.float32),
+            pltpu.VMEM((2, tokens, job_rows), low),
+            pltpu.VMEM((2, tokens, width), low),
+            pltpu.VMEM((2, job_rows, width), full),
+            pltpu.VMEM((steps // 2, 3 * half, width), full),
+            pltpu.VMEM((steps, 3 * half, width), full),
+            pltpu.VMEM((3, 3 * half, width), full),
+            pltpu.VMEM((turns, lines, width), full),
+            pltpu.VMEM((turns, lines, width), full),
+            pltpu.VMEM((2, 4, slot_len, pair), low),
+            pltpu.VMEM((tokens, width), low),
+            pltpu.VMEM((tokens, width), low),
+            pltpu.VMEM((tokens, width), low),
+            pltpu.VMEM((heads, tile, near), full),
+            pltpu.VMEM((heads, tile, near), full),
+            pltpu.VMEM((2, 16, tile), full),
+            pltpu.VMEM((slot_len, slot_len), full),
+            pltpu.VMEM((slot_len, width), low),
+            pltpu.VMEM((slot_len, width), full),
+            pltpu.VMEM((slot_len, width), low),
             *inboxes,
             pltpu.SemaphoreType.DMA((2, 2)),
             pltpu.SemaphoreType.DMA((3 * steps, longest)),
             pltpu.SemaphoreType.DMA((3 * steps, longest)),
             pltpu.SemaphoreType.DMA((3, 2)),
             pltpu.SemaphoreType.DMA((2, turns)),
+            pltpu.SemaphoreType.DMA((2, 4)),
+            pltpu.SemaphoreType.DMA((3,)),
+            pltpu.SemaphoreType.REGULAR((3 * steps,)),
         ],
         compiler_params=pltpu.CompilerParams(
-            collective_id=collective, has_side_effects=True, vmem_limit_bytes=56000000
+            collective_id=collective, has_side_effects=True, vmem_limit_bytes=66500000
         ),
         name="sum_weights",
-    )(*arrays)
+    )(lengths, far, *streamed, small, *resident)
 
 
 tile = 128
@@ -631,110 +811,6 @@
     context_ref[...] = dot_across(attn_low, wo[...]).astype(jnp.bfloat16)
 
 
-def attend_back_kernel(
-    lengths, far, x_ref, lines_ref, gain_a, wq, wk, wv, q_ref, k_ref, v_ref, lse_ref, context_grad, mixed_grad,
-    dq_ref, dk_ref, dv_ref, token_ref, gains_ref, sums_ref,
-    near_ref, far_sums, near_sums, soft_ref,
-):
-    seq = pl.program_id(0)
-    heads = far.shape[1]
-    slot_len, width = x_ref.shape
-    blocks = slot_len // tile
-    pair = 2 * width // heads
-    length = lengths[seq]
-
-    def clear():
-        spread_bias(lines_ref, near_ref, heads)
-        near_sums[...] = jnp.zeros_like(near_sums)
-        far_sums[...] = jnp.zeros_like(far_sums)
-        gains_ref[...] = jnp.zeros_like(gains_ref)
-
-    pl.when(seq == 0)(clear)
-    places = lax.broadcasted_iota(jnp.int32, (slot_len, 1), 0)
-    lanes = lax.broadcasted_iota(jnp.int32, (1, pair), 1)
-
-    def attend(index, carry):
-        span = pl.ds(pl.multiple_of(index * pair, pair), pair)
-        keys = k_ref[:, span]
-        queries = q_ref[:, span]
-        values = v_ref[:, span]
-        upstream = context_grad[:, span]
-        by_query = by_key = by_value = None
-        for side in range(2):
-            head = 2 * index + side
-            mine = (lanes // (pair // 2) == side).astype(jnp.bfloat16)
-            my_queries, my_upstream = queries * mine, upstream * mine
-            raw = dot_across(keys, my_queries)
-            soft_grad = dot_across(values, my_upstream)
-            totals = lse_ref[0, pl.ds(head, 1), :]
-            inner = jnp.zeros((1, slot_len), jnp.float32)
-            low_rows = []
-            for block in range(blocks):
-                part = slice(block * tile, (block + 1) * tile)
-                bias = bias_row(near_ref, head, block, blocks, far[0, head], far[1, head], True)
-                scores = jnp.where(places[part] < length, raw[part] + bias, masked_score)
-                soft = jnp.exp(scores - totals)
-                soft_ref[part] = soft
-                low_rows.append(soft.astype(jnp.bfloat16))
-                inner += jnp.sum(soft * soft_grad[part], axis=0, keepdims=True)
-            soft_low = jnp.concatenate(low_rows, axis=0)
-            grad_rows = []
-            near_total = [None] * 3
-            far_total = [None] * 2
-            for block in range(blocks):
-                part = slice(block * tile, (block + 1) * tile)
-                grads = soft_ref[part] * (soft_grad[part] - inner)
-                grad_rows.append(grads.astype(jnp.bfloat16))
-                for other in range(blocks):
-                    piece = grads[:, other * tile : (other + 1) * tile]
-                    ahead = block - other
-                    group, spot = (near_total, 1 - ahead) if abs(ahead) <= 1 else (far_total, int(ahead > 0))
-                    group[spot] = piece if group[spot] is None else group[spot] + piece
-            for spot in range(3):
-                if near_total[spot] is not None:
-                    near_sums[head, :, spot * tile : (spot + 1) * tile] += near_total[spot]
-            for spot in range(2):
-                if far_total[spot] is not None:
-                    far_sums[spot, pl.ds(head, 1), :] += jnp.sum(far_total[spot], axis=0, keepdims=True)
-            grads_low = jnp.concatenate(grad_rows, axis=0)
-            pieces = (
-                lax.dot_general(grads_low, keys * mine, (((0,), (0,)), ((), ())), preferred_element_type=jnp.float32),
-                low_dot(grads_low, my_queries),
-                low_dot(soft_low, my_upstream),
-            )
-            if side == 0:
-                by_query, by_key, by_value = pieces
-            else:
-                by_query, by_key, by_value = by_query + pieces[0], by_key + pieces[1], by_value + pieces[2]
-        dq_ref[:, span] = by_query.astype(jnp.bfloat16)
-        dk_ref[:, span] = by_key.astype(jnp.bfloat16)
-        dv_ref[:, span] = by_value.astype(jnp.bfloat16)
-        return carry
-
-    lax.fori_loop(0, heads // 2, attend, 0)
-    normed_grad = dot_across(dq_ref[...], wq[...]) + dot_across(dk_ref[...], wk[...])
-    normed_grad += dot_across(dv_ref[...], wv[...])
-    by_tokens, token_gain = norm_back(x_ref[...].astype(jnp.float32), gain_a[...], normed_grad)
-    gains_ref[0:1] += token_gain
-    token_ref[...] = (mixed_grad[...] + by_tokens).astype(jnp.bfloat16)
-
-    def close():
-        for head in range(heads):
-            turned = jnp.concatenate([near_sums[head], jnp.zeros((tile, tile), jnp.float32)], axis=1)
-            count = tile // 2
-            while count:
-                upper = turned[count : 2 * count]
-                turned = turned[:count] + pltpu.roll(upper, 4 * tile - count, 1)
-                count //= 2
-            line = turned
-            sums_ref[head : head + 1, :] = line
-        sums_ref[:, 2 * tile : 3 * tile] += far_sums[0]
-        sums_ref[:, 3 * tile : 4 * tile] += far_sums[1]
-
-    sums_ref[...] = jnp.zeros_like(sums_ref)
-    pl.when(seq == pl.num_programs(0) - 1)(close)
-
-
 def whole(shape):
     return pl.BlockSpec(shape, lambda n, *_: (0,) * len(shape), pipeline_mode=pl.Buffered(1))
 
@@ -776,50 +852,6 @@
         compiler_params=pltpu.CompilerParams(vmem_limit_bytes=60000000),
         name="feed_back",
     )(lengths, prefixes, wo, gains[0][None], widen, narrow, gains[1][None], mixed, hidden, output, pooled_grad)
-
-
-def run_attend_back(tokens, lengths, far, lines, gain, weights, saved, context_grad, mixed_grad):
-    rows, width = tokens.shape
-    seqs = lengths.shape[0]
-    slot_len = rows // seqs
-    heads = far.shape[1]
-
-    def block(columns):
-        return pl.BlockSpec((slot_len, columns), lambda n, *_: (n, 0))
-
-    square = whole((width, width))
-    low, full = jnp.bfloat16, jnp.float32
-    return pl.pallas_call(
-        attend_back_kernel,
-        grid_spec=pltpu.PrefetchScalarGridSpec(
-            num_scalar_prefetch=2,
-            grid=(seqs,),
-            in_specs=[
-                block(width), whole((16, 4 * tile)), whole((1, width)), square, square, square,
-                block(width), block(width), block(width),
-                pl.BlockSpec((1, 16, slot_len), lambda n, *_: (n, 0, 0)),
-                block(width), block(width),
-            ],
-            out_specs=[
-                block(width), block(width), block(width), block(width),
-                pl.BlockSpec((8, width), lambda n, *_: (0, 0)),
-                pl.BlockSpec((16, 4 * tile), lambda n, *_: (0, 0)),
-            ],
-            scratch_shapes=[
-                pltpu.VMEM((heads, tile, near), full),
-                pltpu.VMEM((2, 16, tile), full),
-                pltpu.VMEM((heads, tile, near), full),
-                pltpu.VMEM((slot_len, slot_len), full),
-            ],
-        ),
-        out_shape=(
-            *(jax.ShapeDtypeStruct((rows, width), low) for _ in range(4)),
-            jax.ShapeDtypeStruct((8, width), full),
-            jax.ShapeDtypeStruct((16, 4 * tile), full),
-        ),
-        compiler_params=pltpu.CompilerParams(vmem_limit_bytes=60000000),
-        name="attend_back",
-    )(lengths, far, tokens, lines, gain[None], *weights, *saved, context_grad, mixed_grad)
 
 
 def bucket_sums(offset_sums, shape):
@@ -891,18 +923,12 @@
     branch, pre, attn, context_grad, mixed_grad, feed_gains = run_feed_back(
         lengths[0], prefixes[0], gains[1:], weights[3:], mixed, hidden, output, grad_pooled[:, None]
     )
-    by_query, by_key, by_value, token_gradient, token_gains, offset_sums = run_attend_back(
-        tokens[0], lengths[0], far, bias_lines(bucket_bias, True), gain_attention, weights[:3],
-        (query, key, value, totals), context_grad, mixed_grad,
+    streamed = (
+        hidden, ffn_in, context, normed, branch, pre, attn, query, key, value, context_grad, tokens[0], mixed_grad
     )
-    gain_sums = feed_gains + token_gains
-    grad_bucket = bucket_sums(offset_sums, bucket_bias.shape)
-    flat = grad_bucket.reshape(-1)
-    block = gain_sums.at[3, : flat.shape[0]].set(flat)
-    summed, sums = sum_weights(
-        batch_size, 1, hidden, ffn_in, context, normed, branch, pre, attn, by_query, by_key, by_value, block
-    )
-    sum_bucket = sums[3, : flat.shape[0]].reshape(bucket_bias.shape)
+    resident = (totals, bias_lines(bucket_bias, True), gain_attention[None], *weights[:3])
+    summed, token_gradient, sums = sum_weights(batch_size, 1, lengths[0], far, streamed, feed_gains, resident)
+    sum_bucket = bucket_sums(sums[8:, : 4 * tile], bucket_bias.shape)
     ff = hidden.shape[1]
     sum_widen = summed[ff : 2 * ff].reshape(ff // width, width, width)
     sum_widen = sum_widen.transpose(1, 0, 2).reshape(width, ff)

time: 519 us -> 458 us (0.88)
  Pallas kernels: 470 us -> 408 us
    pallas_call x1 -> x0, Pallas kernels: 79.4 us -> none  [run_attend_back(): pl.pallas_call(attend_back_kernel, grid_spec=pltpu.PrefetchScalarGridSpec...]
    pallas_call x1, Pallas kernels: 242 us -> 258 us  [sum_weights(): pl.pallas_call(functools.partial(sums_kernel, dims, jobs), out_shape=(jax...]
where the time goes in v3:
time: 458 us; the launch traced here: 457 us
  Pallas kernels  408 us (89%)
  local copies, waits for them, and re-layouts  34.8 us (8%)
  matrix products  5.43 us (1%)
  other arithmetic  5.04 us (1%)
    pallas_call x1, Pallas kernels, sum_weights(): pl.pallas_call(functools.partial(sums_kernel, dims, jobs), out_shape=(jax...  258 us
    pallas_call x1, Pallas kernels, run_forward(): pl.pallas_call(forward_kernel, grid_spec=pltpu.PrefetchScalarGridSpec(num...  89.1 us
    pallas_call x1, Pallas kernels, run_feed_back(): pl.pallas_call(feed_back_kernel, grid_spec=pltpu.PrefetchScalarGridSpec(n...  46.9 us
    pallas_call x1, Pallas kernels, gather_blocks(): pl.pallas_call(functools.partial(gather_kernel, groups), out_shape=jax.Sh...  13.2 us
    slice x1, local copies, waits for them, and re-layouts, local(): summed[:ff]  11 us

profile of v3, /device:TPU:0, one launch (start us, length us, event | category | flops | bytes accessed | tf_op | source)
XLA Modules:
  0.0 456.7 jit_solution(11849687473358994603)
XLA Ops:
  0.7 1.3 broadcast_in_dim.18.gain_a.refs_18_
  2.0 1.3 broadcast_in_dim.19.gain_f
  3.2 1.3 broadcast_in_dim.20.gain_z
  4.5 0.8 fusion.26
  5.3 0.1 copy.31
  5.4 0.1 copy.32
  5.5 0.6 pad_maximum_fusion.far.refs_1_
  6.1 1.0 convolution_bitcast_fusion.1
  7.1 0.6 pad.7.lines_ref
  7.7 1.0 convolution_bitcast_fusion
  8.7 0.6 pad.8.refs_17_
  9.4 89.1 %forward.1 = (bf16[2048,768]{1,0:T(8,128)(2,1)}, bf16[2048,768]{1,0:T(8,128)(2,1)}, bf16[2048,768]{1,0:T(8,128)(2,1)}, bf16[2048,768]{1,0:T(8,128)(2,1)}, f32[4,...) custom-call(s32[4]{0:T(128)} %bitcast.38, ...), custom_call_target="tpu_custom_call" | custom-call | tf_op jit(solution)/shard_map/forward/pallas_call | solution.py:735
  98.5 0.8 fusion.9
  99.3 1.4 bitcast_multiply_fusion.2.block_ref
  100.7 13.2 %gather_blocks.1 = f32[2,16,4,768]{3,2,1,0:T(4,128)} custom-call(f32[4,768]{1,0:T(4,128)} %bitcast_multiply_fusion.2.block_ref), custom_call_target="tpu_custom_call" | custom-call | tf_op jit(solution)/shard_map/gather_blocks/pallas_call | solution.py:85
  113.9 1.1 fusion.25
  115.1 0.4 fusion.22
  115.6 0.7 select_reduce_fusion
  116.2 0.1 convert_subtract_fusion
  116.3 0.3 convolution_multiply_fusion.1
  116.7 1.0 fusion.12
  117.8 0.6 add_reduce_fusion
  120.3 0.8 fusion.11
  121.1 0.6 broadcast_in_dim.21.pooled_ref
  121.7 46.9 %feed_back.1 = (bf16[2048,768]{1,0:T(8,128)(2,1)}, bf16[2048,3072]{1,0:T(8,128)(2,1)}, bf16[2048,768]{1,0:T(8,128)(2,1)}, bf16[2048,768]{1,0:T(8,128)(2,1)}, f32[2048,768]{1,0:T(8,128)}, /*index=5*/f32[8,768]{1,0:T(8,128)}) custom-call(s32[4]{0:T(128)} %bitcast.39, s32[4]{0:T(128)} %bitcast.42, bf16[768,768]{1,0:T(8,128)(2,1)} %wo.3, ...), custom_call_target="tpu_custom_call" | custom-call | tf_op jit(solution)/shard_map/feed_back/pallas_call | solution.py:832
  168.6 258.4 %sum_weights.1 = (f32[9216,768]{1,0:T(8,128)}, bf16[2048,768]{1,0:T(8,128)(2,1)}, f32[24,768]{1,0:T(8,128)}) custom-call(s32[4]{0:T(128)} %bitcast.40, f32[2,12]{1,0:T(2,128)} %pad_maximum_fusion.far.refs_1_, bf16[2048,3072]{1,0:T(8,128)(2,1)} %get-tuple-element.34.hidden_ref.refs_2_, bf16[2048,768]{1,0:T(8,128)(2,1)} %get-tuple-element.35.refs_3_, ...), custom_call_target="tpu_custom_call" | custom-call | tf_op jit(solution)/shard_map/sum_weights/pallas_call | solution.py:543
  427.0 1.6 fusion.1
  428.7 1.5 slice_reduce_fusion
  430.1 7.6 %fusion.24 = (f32[768,768]{1,0:T(8,128)}, f32[768,768]{1,0:T(8,128)}, f32[768,768]{1,0:T(8,128)}, f32[768,768]{1,0:T(8,128)}) fusion(f32[9216,768]{1,0:T(8,128)} %get-tuple-element.52), kind=kLoop, calls=%fused_computation.52 | loop fusion | bytes 18874368 | tf_op jit(solution)/shard_map/slice | solution.py:936
  437.7 11.0 %fusion.23 = (f32[3072,768]{1,0:T(8,128)}, f32[3072,768]{1,0:T(8,128)S(1)}) fusion(f32[9216,768]{1,0:T(8,128)} %get-tuple-element.52), kind=kLoop, calls=%fused_computation.51 | loop fusion | bytes 37748736 | tf_op jit(solution)/shard_map/slice | solution.py:950
  448.7 5.2 %copy.33 = f32[4,96,8,768]{3,2,0,1:T(8,128)} copy(f32[4,96,8,768]{3,2,1,0:T(8,128)S(1)} %bitcast.33) | data formatting | bytes 18874368 | tf_op jit(solution)/shard_map/reshape | solution.py:934
  453.9 1.7 copy.39
  (12 shorter events, 0.2 us)
Async XLA Ops:
  9.4 106.2 %copy-start.2 = (s32[64]{0:T(128)S(1)}, s32[64]{0:T(128)}, u32[]{:S(2)}) copy-start(s32[64]{0:T(128)} %param.17) | copy-start | bytes 772
  116.7 51.9 %copy-start.1 = (f32[4,64]{1,0:T(4,128)}, f32[4,64]{1,0:T(4,128)S(1)}, u32[]{:S(2)}) copy-start(f32[4,64]{1,0:T(4,128)S(1)} %constant_dynamic-slice_fusion) | copy-start | bytes 3076
  448.7 5.2 %copy-start = (bf16[2048,768]{1,0:T(8,128)(2,1)S(1)}, bf16[2048,768]{1,0:T(8,128)(2,1)}, u32[]{:S(2)}) copy-start(bf16[2048,768]{1,0:T(8,128)(2,1)} %get-tuple-element.50) | copy-start | bytes 9437188

commit v4 on v3

--- a/solution.py
+++ b/solution.py
@@ -113,64 +113,96 @@
         pl.when(condition)(action)
 
 
-def plan_unit(order, dims, batch, rows):
+def hands_back(order, dims, index):
+    return index == 0 and all(dims[name][1] == 2 for name in order[1:])
+
+
+def plan_unit(order, dims, coords, batch, rows):
     add, spread = [], []
-    start, active = 0, None
-    for name in order:
+    start, active, column = 0, None, None
+    for index, name in enumerate(order):
         stride, size = dims[name]
-        coord = lax.rem(batch // stride, size)
+        coord = coords[name]
         if size == 4:
+            low_side = coord < 2
             inner = jnp.logical_or(coord == 1, coord == 2)
             outer = jnp.logical_not(inner)
             mate = batch + stride * (1 - 2 * lax.rem(coord, 2))
+            share = hands_back(order, dims, index)
+            sent = rows * 3 // 4 if share else rows
+            first = start + jnp.where(low_side, rows // 4, 0) if share else start
             add.append(
-                dict(rows=rows, send=start, keep=start, peer=mate,
+                dict(rows=sent, send=first, keep=first, peer=mate, one_way=True,
                      sends=both(active, outer), receives=both(active, inner)))
             spread.append(
-                dict(rows=rows, send=start, peer=mate,
+                dict(rows=sent, send=first, peer=mate,
                      sends=both(active, inner), receives=both(active, outer)))
-            active = both(active, inner)
+            active_inner = both(active, inner)
             bit = coord // 2
-            mate = batch + stride * (3 - 2 * coord)
+            half = rows // 2
+            kept = start + bit * half
+            other = batch + stride * (3 - 2 * coord)
+            add.append(
+                dict(rows=half, send=start + (1 - bit) * half, keep=kept, peer=other, one_way=False,
+                     sends=active_inner, receives=active_inner))
+            spread.append(dict(rows=half, send=kept, peer=other, sends=active_inner, receives=active_inner))
+            if share:
+                quarter = rows // 4
+                last = start + jnp.where(low_side, 0, 3 * quarter)
+                add.append(
+                    dict(rows=quarter, send=last, keep=last, peer=mate, one_way=True,
+                         sends=active_inner, receives=both(active, outer)))
+                spread.append(
+                    dict(rows=quarter, send=last, peer=mate,
+                         sends=both(active, outer), receives=active_inner))
+                start, rows = start + coord * quarter, quarter
+            else:
+                start, rows, active = kept, half, active_inner
+            continue
+        mate = batch + stride * (1 - 2 * coord)
+        if rows > 8:
+            rows = rows // 2
+            kept = start + coord * rows
+            add.append(
+                dict(rows=rows, send=start + (1 - coord) * rows, keep=kept, peer=mate, one_way=False,
+                     sends=active, receives=active))
+            spread.append(dict(rows=rows, send=kept, peer=mate, sends=active, receives=active))
+            start = kept
         else:
-            bit = coord
-            mate = batch + stride * (1 - 2 * coord)
-        rows = rows // 2
-        kept = start + bit * rows
-        add.append(
-            dict(rows=rows, send=start + (1 - bit) * rows, keep=kept, peer=mate,
-                 sends=active, receives=active))
-        spread.append(dict(rows=rows, send=kept, peer=mate, sends=active, receives=active))
-        start = kept
+            add.append(
+                dict(rows=rows, send=start, keep=start, peer=mate, one_way=False, sends=active, receives=active,
+                     send_side=1 - coord, keep_side=coord))
+            spread.append(
+                dict(rows=rows, send=start, peer=mate, sends=active, receives=active, send_side=coord))
     return add, spread[::-1]
 
 
-def one_way_steps(order, dims):
-    flags = []
-    for name in order:
-        flags += [True, False] if dims[name][1] == 4 else [False]
-    return flags
-
-
-def step_rings(order, dims):
-    flags = one_way_steps(order, dims)
-    steps = 2 + 2 * len(flags)
-    rings = [3] * steps
-    for index, single in enumerate(flags):
+def plan_shapes(order, dims, rows):
+    result = []
+    for index, name in enumerate(order):
+        if dims[name][1] == 4:
+            share = hands_back(order, dims, index)
+            result.append((rows * 3 // 4 if share else rows, 1, True))
+            result.append((rows // 2, 1, False))
+            if share:
+                result.append((rows // 4, 1, True))
+            rows = rows // 4 if share else rows // 2
+        elif rows > 8:
+            rows //= 2
+            result.append((rows, 1, False))
+        else:
+            result.append((rows, 2, False))
+    return result
+
+
+def step_rings(shapes):
+    steps = 2 + 2 * len(shapes)
+    rings = [4] * steps
+    for index, (_, _, single) in enumerate(shapes):
         if single:
             first, last = 1 + index, steps - 2 - index
-            rings[last] = last - first + 2
+            rings[last] = last - first + 4
     return rings
-
-
-def stage_rows(order, dims, rows):
-    result = []
-    for name in order:
-        if dims[name][1] == 4:
-            result.append(rows)
-        rows //= 2
-        result.append(rows)
-    return result
 
 
 orders = ("xyz", "yxz", "zxy")
@@ -183,19 +215,43 @@
     (left, right, part, acc, full, mate_in, small_own, small_in, heads_in, by_query, by_key, by_value) = refs[25:37]
     (near_ref, near_sums, far_sums, soft_ref, token_in, mixed_in, token_buffer) = refs[37:44]
     rest = refs[44:]
-    counts = [len(stage_rows(order, dims, 8)) for order in orders]
+    half = unit_rows // 2
+    shapes = [plan_shapes(order, dims, half) for order in orders]
+    counts = [len(shape) for shape in shapes]
     inbox, where = [], 0
     for count in counts:
         inbox.append(rest[where : where + count])
         where += count
-    load_sem, send_sem, recv_sem, keep_sem, small_sem, heads_sem, token_sem, credit = rest[where:]
+    load_sem, right_sem, send_sem, recv_sem, keep_sem, small_sem, heads_sem, token_sem, credit = rest[where:]
     tower, batch = place()
-    half = unit_rows // 2
-    steps = 2 + 2 * counts[0]
-    slots = jobs + steps + 1
-    plans = [plan_unit(order, dims, batch, half) for order in orders]
-    rings = [step_rings(order, dims) for order in orders]
-    single = [one_way_steps(order, dims) for order in orders]
+    steps = [2 + 2 * count for count in counts]
+    longest = max(steps)
+    slots = jobs + longest + 1
+    rings = [step_rings(shape) for shape in shapes]
+    coords = {name: lax.rem(batch // stride, size) for name, (stride, size) in dims.items()}
+    plans = [plan_unit(order, dims, coords, batch, half) for order in orders]
+    turned_dims = dict(dims, x=dims["y"], y=dims["x"])
+    turned_coords = dict(coords, x=coords["y"], y=coords["x"])
+    turned = plan_unit(orders[-1], turned_dims, turned_coords, batch, half)
+
+    def pick(odd, first, second):
+        if isinstance(first, int) and isinstance(second, int) and first == second or first is None:
+            return first
+        if isinstance(first, bool):
+            return first
+        if getattr(first, "dtype", None) == jnp.bool_:
+            return jnp.logical_or(jnp.logical_and(odd, second), jnp.logical_and(jnp.logical_not(odd), first))
+        return jnp.where(odd, second, first)
+
+    def plan(unit, job):
+        if unit < len(orders) - 1:
+            return plans[unit]
+        odd = lax.rem(job, 2) == 1
+        return tuple(
+            [{key: pick(odd, one[key], two[key]) for key in one} for one, two in zip(ones, twos)]
+            for ones, twos in zip(plans[unit], turned)
+        )
+
     held, spread_held = acc.shape[0], full.shape[0]
     width = out.shape[1]
     heads = far.shape[1]
@@ -221,58 +277,76 @@
     for other in mates:
         pl.semaphore_signal(barrier, 1, device_id=other, device_id_type=MESH)
 
-    def load(job, begin):
-        slot = lax.rem(job, 2)
-
-        def copies(left_ref, left_block, right_ref, right_block):
-            for index, (ref, block, size, target) in enumerate(
-                ((left_ref, left_block, job_rows, left), (right_ref, right_block, width, right))
-            ):
-                columns = pl.ds(pl.multiple_of(block * size, 128), size)
-                copy = pltpu.make_async_copy(
-                    ref.at[:, columns], target.at[slot], load_sem.at[index, slot]
-                )
-                copy.start() if begin else copy.wait()
-
-        if not begin:
-            copies(hidden, 0, branch, 0)
-            return
-        per_narrow = hidden.shape[1] // job_rows
-        per_side = width // job_rows
+    per_narrow = hidden.shape[1] // job_rows
+    per_side = width // job_rows
+    sources = [(hidden, branch, per_narrow), (ffn_in, pre, per_narrow), (context, attn, per_side)]
+    sources += [(normed, grads, per_side) for grads in (by_query, by_key, by_value)]
+
+    def right_place(job):
+        past = job - per_narrow
+        group = jnp.where(past < 0, 0, 1 + past // per_side)
+        fresh = jnp.where(past < 0, job == 0, lax.rem(past, per_side) == 0)
+        return lax.rem(group, 2), fresh
+
+    def left_copies(target, job, columns):
+        quarter = target.shape[1] // 4
+        return [
+            pltpu.make_async_copy(
+                columns(pl.ds(n * quarter, quarter)), target.at[lax.rem(job, 2), pl.ds(n * quarter, quarter)],
+                load_sem.at[lax.rem(job, 2), n],
+            )
+            for n in range(4)
+        ]
+
+    def load(job):
+        place_right, fresh = right_place(job)
         first = 0
-        table = [(hidden, branch, per_narrow)]
-        table.append((ffn_in, pre, per_narrow))
-        table += [
-            (context, attn, per_side), (normed, by_query, per_side),
-            (normed, by_key, per_side), (normed, by_value, per_side),
-        ]
-        for index, (left_ref, right_ref, count) in enumerate(table):
+        for index, (left_ref, right_ref, count) in enumerate(sources):
             local = job - first
 
             def go(local=local, left_ref=left_ref, right_ref=right_ref, index=index):
-                if index == 1:
-                    copies(left_ref, lax.rem(local, per_side), right_ref, local // per_side)
-                else:
-                    copies(left_ref, local, right_ref, 0)
+                block = lax.rem(local, per_side) if index == 1 else local
+                span = pl.ds(pl.multiple_of(block * job_rows, 128), job_rows)
+                for copy in left_copies(left, job, lambda rows: left_ref.at[rows, span]):
+                    copy.start()
+
+                def go_right():
+                    block = local // per_side if index == 1 else 0
+                    span = pl.ds(pl.multiple_of(block * width, 128), width)
+                    pltpu.make_async_copy(
+                        right_ref.at[:, span], right.at[place_right], right_sem.at[place_right]
+                    ).start()
+
+                pl.when(fresh)(go_right)
 
             pl.when(jnp.logical_and(local >= 0, local < count))(go)
             first += count
 
     def compute(job):
         slot = lax.rem(job, 2)
-        load(job, False)
-        pl.when(job + 1 < jobs)(lambda: load(job + 1, True))
+        place_right, fresh = right_place(job)
+        for copy in left_copies(left, job, lambda rows: normed.at[rows, pl.ds(0, job_rows)]):
+            copy.wait()
+        pl.when(fresh)(
+            lambda: pltpu.make_async_copy(attn, right.at[place_right], right_sem.at[place_right]).wait()
+        )
+        pl.when(job + 1 < jobs)(lambda: load(job + 1))
         part[slot] = lax.dot_general(
-            left[slot], right[slot], (((0,), (0,)), ((), ())), preferred_element_type=jnp.float32
+            left[slot], right[place_right], (((0,), (0,)), ((), ())), preferred_element_type=jnp.float32
         )
 
+    def side_columns(item, key):
+        if key not in item:
+            return slice(None)
+        return pl.ds(pl.multiple_of(item[key] * (width // 2), 128), width // 2)
+
     def remote(unit, step, job):
-        add, spread = plans[unit]
+        add, spread = plan(unit, job)
         turn = lax.rem(job, rings[unit][step])
         place_in = lax.rem(job, held)
         sems = dict(
-            send_sem=send_sem.at[unit * steps + step, turn],
-            recv_sem=recv_sem.at[unit * steps + step, turn],
+            send_sem=send_sem.at[unit * longest + step, turn],
+            recv_sem=recv_sem.at[unit * longest + step, turn],
             device_id_type=MESH,
         )
         base = unit * half
@@ -280,7 +354,7 @@
             src = part.at[lax.rem(job, 2), pl.ds(pl.multiple_of(unit * unit_rows + (1 - tower) * half, 8), half)]
             dst = mate_in.at[turn, pl.ds(base, half)]
             return pltpu.make_async_remote_copy(src, dst, device_id=(1 - tower, batch), **sems), None, None
-        if step == steps - 1:
+        if step == steps[unit] - 1:
             src = full.at[lax.rem(job, spread_held), pl.ds(base, half)]
             first = pl.multiple_of(job * job_rows + unit * unit_rows + tower * half, 8)
             dst = out.at[pl.ds(first, half)]
@@ -288,10 +362,11 @@
         count = counts[unit]
         item = add[step - 1] if step <= count else spread[step - 1 - count]
         rows = pl.ds(pl.multiple_of(base + item["send"], 8), item["rows"])
+        columns = side_columns(item, "send_side")
         if step <= count:
-            src, dst = acc.at[place_in, rows], inbox[unit][step - 1].at[turn]
+            src, dst = acc.at[place_in, rows, columns], inbox[unit][step - 1].at[turn]
         else:
-            src = dst = full.at[lax.rem(job, spread_held), rows]
+            src = dst = full.at[lax.rem(job, spread_held), rows, columns]
         copy = pltpu.make_async_remote_copy(src, dst, device_id=(tower, item["peer"]), **sems)
         return copy, item["sends"], item["receives"]
 
@@ -304,11 +379,11 @@
         )
 
     def one_way(unit, step):
-        return 1 <= step <= counts[unit] and single[unit][step - 1]
+        return 1 <= step <= counts[unit] and shapes[unit][step - 1][2]
 
     def finish(unit, step, job):
         copy, sends, receives = remote(unit, step, job)
-        add, _ = plans[unit]
+        add, _ = plan(unit, job)
         base = unit * half
         guarded(sends, copy.wait_send)
         turn = lax.rem(job, rings[unit][step])
@@ -322,40 +397,40 @@
             elif step <= counts[unit]:
                 item = add[step - 1]
                 rows = pl.ds(pl.multiple_of(base + item["keep"], 8), item["rows"])
-                total = acc[place_in, rows] + inbox[unit][step - 1][turn]
+                columns = side_columns(item, "keep_side")
+                total = acc[place_in, rows, columns] + inbox[unit][step - 1][turn]
                 if step == counts[unit]:
-                    full[lax.rem(job, spread_held), rows] = total
+                    full[lax.rem(job, spread_held), rows, columns] = total
                 else:
-                    acc[place_in, rows] = total
+                    acc[place_in, rows, columns] = total
                 if one_way(unit, step):
                     pl.when(job + rings[unit][step] < jobs)(
                         lambda: pl.semaphore_signal(
-                            credit.at[unit * steps + step], 1,
+                            credit.at[unit * longest + step], 1,
                             device_id=(tower, item["peer"]), device_id_type=MESH,
                         )
                     )
 
         guarded(receives, arrived)
-        if step == steps - 1:
+        if step == steps[unit] - 1:
             keep(unit, job).wait()
 
-    def advance(step, job):
-        for unit in range(len(orders)):
-            if step > 0:
-                finish(unit, step - 1, job)
-            if step < steps:
-                copy, sends, _ = remote(unit, step, job)
-
-                def begin(copy=copy, unit=unit):
-                    if one_way(unit, step):
-                        pl.when(job >= rings[unit][step])(
-                            lambda: pl.semaphore_wait(credit.at[unit * steps + step], 1)
-                        )
-                    copy.start()
-
-                guarded(sends, begin)
-                if step == steps - 1:
-                    keep(unit, job).start()
+    def advance(unit, step, job):
+        if step > 0:
+            finish(unit, step - 1, job)
+        if step < steps[unit]:
+            copy, sends, _ = remote(unit, step, job)
+
+            def begin():
+                if one_way(unit, step):
+                    pl.when(job >= rings[unit][step])(
+                        lambda: pl.semaphore_wait(credit.at[unit * longest + step], 1)
+                    )
+                copy.start()
+
+            guarded(sends, begin)
+            if step == steps[unit] - 1:
+                keep(unit, job).start()
 
     def small_copy(turn):
         return pltpu.make_async_remote_copy(
@@ -484,7 +559,7 @@
         small_own[0, 8:24, 2 * tile : 3 * tile] += far_sums[0]
         small_own[0, 8:24, 3 * tile : 4 * tile] += far_sums[1]
 
-    load(0, True)
+    load(0)
     heads_load(0, True)
     token_load(0, True)
     spread_bias(lines, near_ref, heads)
@@ -498,9 +573,10 @@
     first_token = first_small - 1 - seqs
 
     def slot(time, carry):
-        for step in range(steps, -1, -1):
-            job = time - 1 - step
-            pl.when(jnp.logical_and(job >= 0, job < jobs))(functools.partial(advance, step, job))
+        for unit in range(len(orders)):
+            for step in range(steps[unit] + 1):
+                job = time - 1 - step
+                pl.when(jnp.logical_and(job >= 0, job < jobs))(functools.partial(advance, unit, step, job))
         for turn in range(len(turns) + 1):
             pl.when(time == first_small + turn)(functools.partial(small_turn, turn))
         begin = jnp.minimum(time * tasks // last_attend, tasks)
@@ -526,13 +602,14 @@
     jobs = total // job_rows
     dims = batch_dims(batch_size)
     half = unit_rows // 2
-    rings = [step_rings(order, dims) for order in orders]
+    shapes = [plan_shapes(order, dims, half) for order in orders]
+    rings = [step_rings(shape) for shape in shapes]
     inboxes = [
-        pltpu.VMEM((rings[unit][1 + index], rows, width), jnp.float32)
-        for unit, order in enumerate(orders)
-        for index, rows in enumerate(stage_rows(order, dims, half))
+        pltpu.VMEM((rings[unit][1 + index], rows, width // parts), jnp.float32)
+        for unit, shape in enumerate(shapes)
+        for index, (rows, parts, _) in enumerate(shape)
     ]
-    steps = len(rings[0])
+    steps = max(len(ring) for ring in rings)
     longest = max(max(ring) for ring in rings)
     turns = 1 + sum(size // 2 for _, size in dims.values())
     lines = 24
@@ -555,7 +632,7 @@
             pltpu.VMEM((2, job_rows, width), full),
             pltpu.VMEM((steps // 2, 3 * half, width), full),
             pltpu.VMEM((steps, 3 * half, width), full),
-            pltpu.VMEM((3, 3 * half, width), full),
+            pltpu.VMEM((4, 3 * half, width), full),
             pltpu.VMEM((turns, lines, width), full),
             pltpu.VMEM((turns, lines, width), full),
             pltpu.VMEM((2, 4, slot_len, pair), low),
@@ -570,7 +647,8 @@
             pltpu.VMEM((slot_len, width), full),
             pltpu.VMEM((slot_len, width), low),
             *inboxes,
-            pltpu.SemaphoreType.DMA((2, 2)),
+            pltpu.SemaphoreType.DMA((2, 4)),
+            pltpu.SemaphoreType.DMA((2,)),
             pltpu.SemaphoreType.DMA((3 * steps, longest)),
             pltpu.SemaphoreType.DMA((3 * steps, longest)),
             pltpu.SemaphoreType.DMA((3, 2)),

time: 458 us -> 443 us (0.967)
  Pallas kernels: 408 us -> 393 us
    pallas_call x1, Pallas kernels: 258 us -> 244 us  [sum_weights(): pl.pallas_call(functools.partial(sums_kernel, dims, jobs), out_shape=(jax...]
where the time goes in v4:
time: 443 us; the launch traced here: 442 us
  Pallas kernels  393 us (89%)
  local copies, waits for them, and re-layouts  34.8 us (8%)
  matrix products  5.43 us (1%)
  other arithmetic  5.04 us (1%)
    pallas_call x1, Pallas kernels, sum_weights(): pl.pallas_call(functools.partial(sums_kernel, dims, jobs), out_shape=(jax...  244 us
    pallas_call x1, Pallas kernels, run_forward(): pl.pallas_call(forward_kernel, grid_spec=pltpu.PrefetchScalarGridSpec(num...  89.1 us
    pallas_call x1, Pallas kernels, run_feed_back(): pl.pallas_call(feed_back_kernel, grid_spec=pltpu.PrefetchScalarGridSpec(n...  46.9 us
    pallas_call x1, Pallas kernels, gather_blocks(): pl.pallas_call(functools.partial(gather_kernel, groups), out_shape=jax.Sh...  13.2 us
    slice x1, local copies, waits for them, and re-layouts, local(): summed[:ff]  11 us

profile of v4, /device:TPU:0, one launch (start us, length us, event | category | flops | bytes accessed | tf_op | source)
XLA Modules:
  0.0 441.8 jit_solution(16105295954807921824)
XLA Ops:
  0.7 1.3 broadcast_in_dim.18.gain_a.refs_18_
  2.0 1.3 broadcast_in_dim.19.gain_f
  3.2 1.3 broadcast_in_dim.20.gain_z
  4.5 0.8 fusion.26
  5.3 0.1 copy.31
  5.4 0.1 copy.32
  5.5 0.6 pad_maximum_fusion.far.refs_1_
  6.1 1.0 convolution_bitcast_fusion.1
  7.1 0.6 pad.7.lines_ref
  7.7 1.0 convolution_bitcast_fusion
  8.7 0.6 pad.8.refs_17_
  9.4 89.1 %forward.1 = (bf16[2048,768]{1,0:T(8,128)(2,1)}, bf16[2048,768]{1,0:T(8,128)(2,1)}, bf16[2048,768]{1,0:T(8,128)(2,1)}, bf16[2048,768]{1,0:T(8,128)(2,1)}, f32[4,...) custom-call(s32[4]{0:T(128)} %bitcast.38, ...), custom_call_target="tpu_custom_call" | custom-call | tf_op jit(solution)/shard_map/forward/pallas_call | solution.py:813
  98.5 0.8 fusion.9
  99.3 1.4 bitcast_multiply_fusion.2.block_ref
  100.7 13.2 %gather_blocks.1 = f32[2,16,4,768]{3,2,1,0:T(4,128)} custom-call(f32[4,768]{1,0:T(4,128)} %bitcast_multiply_fusion.2.block_ref), custom_call_target="tpu_custom_call" | custom-call | tf_op jit(solution)/shard_map/gather_blocks/pallas_call | solution.py:85
  113.9 1.1 fusion.25
  115.1 0.4 fusion.22
  115.6 0.7 select_reduce_fusion
  116.2 0.1 convert_subtract_fusion
  116.3 0.3 convolution_multiply_fusion.1
  116.7 1.0 fusion.12
  117.8 0.6 add_reduce_fusion
  120.3 0.8 fusion.11
  121.1 0.6 broadcast_in_dim.21.pooled_ref
  121.7 46.9 %feed_back.1 = (bf16[2048,768]{1,0:T(8,128)(2,1)}, bf16[2048,3072]{1,0:T(8,128)(2,1)}, bf16[2048,768]{1,0:T(8,128)(2,1)}, bf16[2048,768]{1,0:T(8,128)(2,1)}, f32[2048,768]{1,0:T(8,128)}, /*index=5*/f32[8,768]{1,0:T(8,128)}) custom-call(s32[4]{0:T(128)} %bitcast.39, s32[4]{0:T(128)} %bitcast.42, bf16[768,768]{1,0:T(8,128)(2,1)} %wo.3, ...), custom_call_target="tpu_custom_call" | custom-call | tf_op jit(solution)/shard_map/feed_back/pallas_call | solution.py:910
  168.6 243.5 %sum_weights.1 = (f32[9216,768]{1,0:T(8,128)}, bf16[2048,768]{1,0:T(8,128)(2,1)}, f32[24,768]{1,0:T(8,128)}) custom-call(s32[4]{0:T(128)} %bitcast.40, f32[2,12]{1,0:T(2,128)} %pad_maximum_fusion.far.refs_1_, bf16[2048,3072]{1,0:T(8,128)(2,1)} %get-tuple-element.34.hidden_ref.refs_2_, bf16[2048,768]{1,0:T(8,128)(2,1)} %get-tuple-element.35.refs_3_, ...), custom_call_target="tpu_custom_call" | custom-call | tf_op jit(solution)/shard_map/sum_weights/pallas_call | solution.py:620
  412.1 1.6 fusion.1
  413.8 1.5 slice_reduce_fusion
  415.3 7.6 %fusion.24 = (f32[768,768]{1,0:T(8,128)}, f32[768,768]{1,0:T(8,128)}, f32[768,768]{1,0:T(8,128)}, f32[768,768]{1,0:T(8,128)}) fusion(f32[9216,768]{1,0:T(8,128)} %get-tuple-element.52), kind=kLoop, calls=%fused_computation.52 | loop fusion | bytes 18874368 | tf_op jit(solution)/shard_map/slice | solution.py:1014
  422.9 11.0 %fusion.23 = (f32[3072,768]{1,0:T(8,128)}, f32[3072,768]{1,0:T(8,128)S(1)}) fusion(f32[9216,768]{1,0:T(8,128)} %get-tuple-element.52), kind=kLoop, calls=%fused_computation.51 | loop fusion | bytes 37748736 | tf_op jit(solution)/shard_map/slice | solution.py:1028
  433.8 5.2 %copy.33 = f32[4,96,8,768]{3,2,0,1:T(8,128)} copy(f32[4,96,8,768]{3,2,1,0:T(8,128)S(1)} %bitcast.33) | data formatting | bytes 18874368 | tf_op jit(solution)/shard_map/reshape | solution.py:1012
  439.0 1.7 copy.39
  (12 shorter events, 0.2 us)
Async XLA Ops:
  9.4 106.2 %copy-start.2 = (s32[64]{0:T(128)S(1)}, s32[64]{0:T(128)}, u32[]{:S(2)}) copy-start(s32[64]{0:T(128)} %param.17) | copy-start | bytes 772
  116.7 51.9 %copy-start.1 = (f32[4,64]{1,0:T(4,128)}, f32[4,64]{1,0:T(4,128)S(1)}, u32[]{:S(2)}) copy-start(f32[4,64]{1,0:T(4,128)S(1)} %constant_dynamic-slice_fusion) | copy-start | bytes 3076
  433.8 5.2 %copy-start = (bf16[2048,768]{1,0:T(8,128)(2,1)S(1)}, bf16[2048,768]{1,0:T(8,128)(2,1)}, u32[]{:S(2)}) copy-start(bf16[2048,768]{1,0:T(8,128)(2,1)} %get-tuple-element.50) | copy-start | bytes 9437188

commit v5 on v4

--- a/solution.py
+++ b/solution.py
@@ -211,10 +211,10 @@
 def sums_kernel(dims, jobs, *refs):
     (lengths, far, hidden, ffn_in, context, normed, branch, pre, attn, query, key, value, upstream) = refs[:13]
     (tokens, mixed_grad, small, totals, lines, gain, wq, wk, wv) = refs[13:22]
-    (out, token_out, small_out) = refs[22:25]
-    (left, right, part, acc, full, mate_in, small_own, small_in, heads_in, by_query, by_key, by_value) = refs[25:37]
-    (near_ref, near_sums, far_sums, soft_ref, token_in, mixed_in, token_buffer) = refs[37:44]
-    rest = refs[44:]
+    (narrow_out, widen_out, square_out, token_out, small_out) = refs[22:27]
+    (left, right, part, acc, full, mate_in, small_own, small_in, heads_in, by_query, by_key, by_value) = refs[27:39]
+    (near_ref, near_sums, far_sums, token_in, mixed_in, token_buffer) = refs[39:45]
+    rest = refs[45:]
     half = unit_rows // 2
     shapes = [plan_shapes(order, dims, half) for order in orders]
     counts = [len(shape) for shape in shapes]
@@ -253,7 +253,7 @@
         )
 
     held, spread_held = acc.shape[0], full.shape[0]
-    width = out.shape[1]
+    width = narrow_out.shape[1]
     heads = far.shape[1]
     seqs = lengths.shape[0]
     slot_len = tokens.shape[0] // seqs
@@ -354,11 +354,6 @@
             src = part.at[lax.rem(job, 2), pl.ds(pl.multiple_of(unit * unit_rows + (1 - tower) * half, 8), half)]
             dst = mate_in.at[turn, pl.ds(base, half)]
             return pltpu.make_async_remote_copy(src, dst, device_id=(1 - tower, batch), **sems), None, None
-        if step == steps[unit] - 1:
-            src = full.at[lax.rem(job, spread_held), pl.ds(base, half)]
-            first = pl.multiple_of(job * job_rows + unit * unit_rows + tower * half, 8)
-            dst = out.at[pl.ds(first, half)]
-            return pltpu.make_async_remote_copy(src, dst, device_id=(1 - tower, batch), **sems), None, None
         count = counts[unit]
         item = add[step - 1] if step <= count else spread[step - 1 - count]
         rows = pl.ds(pl.multiple_of(base + item["send"], 8), item["rows"])
@@ -370,13 +365,41 @@
         copy = pltpu.make_async_remote_copy(src, dst, device_id=(tower, item["peer"]), **sems)
         return copy, item["sends"], item["receives"]
 
-    def keep(unit, job):
-        base = unit * half
-        first = pl.multiple_of(job * job_rows + unit * unit_rows + tower * half, 8)
-        return pltpu.make_async_copy(
-            full.at[lax.rem(job, spread_held), pl.ds(base, half)], out.at[pl.ds(first, half)],
-            keep_sem.at[unit, lax.rem(job, 2)],
+    def place_sums(unit, job, action):
+        src = full.at[lax.rem(job, spread_held), pl.ds(unit * half, half)]
+        first = unit * unit_rows + tower * half
+
+        def at(ref, row, *columns):
+            return lambda: action(src, ref.at[(pl.ds(pl.multiple_of(row + first, 8), half), *columns)])
+
+        past = job - per_narrow
+        pl.when(past < 0)(at(narrow_out, job * job_rows))
+        columns = pl.ds(pl.multiple_of(past // per_side * width, 128), width)
+        pl.when(jnp.logical_and(past >= 0, past < per_narrow))(
+            at(widen_out, lax.rem(past, per_side) * job_rows, columns)
         )
+        pl.when(past >= per_narrow)(at(square_out, (past - per_narrow) * job_rows))
+
+    def last_copy(unit, job, src, dst):
+        turn = lax.rem(job, rings[unit][steps[unit] - 1])
+        index = unit * longest + steps[unit] - 1
+        return pltpu.make_async_remote_copy(
+            src, dst, send_sem=send_sem.at[index, turn], recv_sem=recv_sem.at[index, turn],
+            device_id=(1 - tower, batch), device_id_type=MESH,
+        )
+
+    def begin_last(unit, job):
+        def both_ways(src, dst):
+            last_copy(unit, job, src, dst).start()
+            pltpu.make_async_copy(src, dst, keep_sem.at[unit, lax.rem(job, 2)]).start()
+
+        place_sums(unit, job, both_ways)
+
+    def finish_last(unit, job):
+        src = full.at[lax.rem(job, spread_held), pl.ds(unit * half, half)]
+        dst = narrow_out.at[pl.ds(0, half)]
+        last_copy(unit, job, src, dst).wait()
+        pltpu.make_async_copy(src, dst, keep_sem.at[unit, lax.rem(job, 2)]).wait()
 
     def one_way(unit, step):
         return 1 <= step <= counts[unit] and shapes[unit][step - 1][2]
@@ -412,25 +435,26 @@
                     )
 
         guarded(receives, arrived)
-        if step == steps[unit] - 1:
-            keep(unit, job).wait()
 
     def advance(unit, step, job):
+        if step == steps[unit]:
+            finish_last(unit, job)
+            return
         if step > 0:
             finish(unit, step - 1, job)
-        if step < steps[unit]:
-            copy, sends, _ = remote(unit, step, job)
-
-            def begin():
-                if one_way(unit, step):
-                    pl.when(job >= rings[unit][step])(
-                        lambda: pl.semaphore_wait(credit.at[unit * longest + step], 1)
-                    )
-                copy.start()
-
-            guarded(sends, begin)
-            if step == steps[unit] - 1:
-                keep(unit, job).start()
+        if step == steps[unit] - 1:
+            begin_last(unit, job)
+            return
+        copy, sends, _ = remote(unit, step, job)
+
+        def begin():
+            if one_way(unit, step):
+                pl.when(job >= rings[unit][step])(
+                    lambda: pl.semaphore_wait(credit.at[unit * longest + step], 1)
+                )
+            copy.start()
+
+        guarded(sends, begin)
 
     def small_copy(turn):
         return pltpu.make_async_remote_copy(
@@ -473,7 +497,9 @@
         pl.when(task + 1 < tasks)(lambda: heads_load(task + 1, True))
         queries, keys, values, upper = (heads_in[slot, n] for n in range(4))
         length = lengths[seq]
-        grads_out = [None] * 3
+        keys_across = keys.T
+        grads_out = [None] * 2
+        query_rows = []
         for side in range(2):
             head = 2 * index + side
             mine = (lanes // (pair // 2) == side).astype(jnp.bfloat16)
@@ -481,27 +507,24 @@
             raw = dot_across(keys, my_queries)
             soft_grad = dot_across(values, my_upper)
             line = totals[seq, pl.ds(head, 1), :]
-            inner = jnp.zeros((1, slot_len), jnp.float32)
-            low_rows = []
-            for block in range(blocks):
-                span = slice(block * tile, (block + 1) * tile)
-                bias = bias_row(near_ref, head, block, blocks, far[0, head], far[1, head], True)
-                scores = jnp.where(places[span] < length, raw[span] + bias, masked_score)
-                soft = jnp.exp(scores - line)
-                soft_ref[span] = soft
-                low_rows.append(soft.astype(jnp.bfloat16))
-                inner += jnp.sum(soft * soft_grad[span], axis=0, keepdims=True)
-            soft_low = jnp.concatenate(low_rows, axis=0)
-            grad_rows = []
+            soft_columns, grad_columns = [], []
             near_total = [None] * 3
             far_total = [None] * 2
-            for block in range(blocks):
-                span = slice(block * tile, (block + 1) * tile)
-                grads = soft_ref[span] * (soft_grad[span] - inner)
-                grad_rows.append(grads.astype(jnp.bfloat16))
-                for other in range(blocks):
-                    piece = grads[:, other * tile : (other + 1) * tile]
-                    ahead = block - other
+            for column in range(blocks):
+                columns = slice(column * tile, (column + 1) * tile)
+                scores = []
+                for block in range(blocks):
+                    rows = slice(block * tile, (block + 1) * tile)
+                    bias = bias_tile(near_ref, head, block, column, far[0, head], far[1, head])
+                    scores.append(jnp.where(places[rows] < length, raw[rows, columns] + bias, masked_score))
+                soft = jnp.exp(jnp.concatenate(scores, axis=0) - line[:, columns])
+                soft_columns.append(soft.astype(jnp.bfloat16))
+                by_soft = soft_grad[:, columns]
+                grads = soft * (by_soft - jnp.sum(soft * by_soft, axis=0, keepdims=True))
+                grad_columns.append(grads.astype(jnp.bfloat16))
+                for block in range(blocks):
+                    piece = grads[block * tile : (block + 1) * tile]
+                    ahead = block - column
                     group, spot = (near_total, 1 - ahead) if abs(ahead) <= 1 else (far_total, int(ahead > 0))
                     group[spot] = piece if group[spot] is None else group[spot] + piece
             for spot in range(3):
@@ -510,16 +533,16 @@
             for spot in range(2):
                 if far_total[spot] is not None:
                     far_sums[spot, pl.ds(head, 1), :] += jnp.sum(far_total[spot], axis=0, keepdims=True)
-            grads_low = jnp.concatenate(grad_rows, axis=0)
-            pieces = (
-                lax.dot_general(grads_low, keys * mine, (((0,), (0,)), ((), ())), preferred_element_type=jnp.float32),
-                low_dot(grads_low, my_queries),
-                low_dot(soft_low, my_upper),
-            )
+            soft_low = jnp.concatenate(soft_columns, axis=1)
+            grads_low = jnp.concatenate(grad_columns, axis=1)
+            half_rows = slice(side * (pair // 2), (side + 1) * (pair // 2))
+            query_rows.append(low_dot(keys_across[half_rows], grads_low).astype(jnp.bfloat16))
+            pieces = (low_dot(grads_low, my_queries), low_dot(soft_low, my_upper))
             grads_out = [new if old is None else old + new for old, new in zip(grads_out, pieces)]
         rows = pl.ds(pl.multiple_of(seq * slot_len, slot_len), slot_len)
         columns = pl.ds(pl.multiple_of(index * pair, pair), pair)
-        for ref, grads in zip((by_query, by_key, by_value), grads_out):
+        by_query[rows, columns] = jnp.concatenate(query_rows, axis=0).T
+        for ref, grads in zip((by_key, by_value), grads_out):
             ref[rows, columns] = grads.astype(jnp.bfloat16)
         return carry
 
@@ -620,12 +643,14 @@
     return pl.pallas_call(
         functools.partial(sums_kernel, dims, jobs),
         out_shape=(
-            jax.ShapeDtypeStruct((total, width), full),
+            jax.ShapeDtypeStruct((hidden.shape[1], width), full),
+            jax.ShapeDtypeStruct((width, hidden.shape[1]), full),
+            jax.ShapeDtypeStruct((4 * width, width), full),
             jax.ShapeDtypeStruct((tokens, width), low),
             jax.ShapeDtypeStruct((lines, width), full),
         ),
         in_specs=[in_smem] * 2 + [anywhere] * len(streamed) + [in_vmem] * (1 + len(resident)),
-        out_specs=(anywhere, anywhere, in_vmem),
+        out_specs=(anywhere, anywhere, anywhere, anywhere, in_vmem),
         scratch_shapes=[
             pltpu.VMEM((2, tokens, job_rows), low),
             pltpu.VMEM((2, tokens, width), low),
@@ -642,7 +667,6 @@
             pltpu.VMEM((heads, tile, near), full),
             pltpu.VMEM((heads, tile, near), full),
             pltpu.VMEM((2, 16, tile), full),
-            pltpu.VMEM((slot_len, slot_len), full),
             pltpu.VMEM((slot_len, width), low),
             pltpu.VMEM((slot_len, width), full),
             pltpu.VMEM((slot_len, width), low),
@@ -668,12 +692,11 @@
 near = 3 * tile
 
 
-def bias_lines(bucket_bias, mirrored):
+def bias_lines(bucket_bias):
     buckets, heads = bucket_bias.shape
     spots = jnp.arange(4 * tile, dtype=jnp.int32)
     moved = jnp.where(spots >= near, spots - 4 * tile, spots)
-    offset = tile - moved if mirrored else moved - tile
-    onehot = offset_onehot(offset, buckets)
+    onehot = offset_onehot(tile - moved, buckets)
     lines = jnp.dot(bucket_bias.T, onehot.T, precision=highest)
     return jnp.pad(lines, ((0, 16 - heads), (0, 0)))
 
@@ -691,16 +714,12 @@
         near_ref[head] = pltpu.roll(line, 0, 1, stride=1, stride_axis=0)[:, :near]
 
 
-def bias_row(near_ref, head, block, blocks, low_far, high_far, mirrored):
-    parts = []
-    for other in range(blocks):
-        ahead = block - other if mirrored else other - block
-        if abs(ahead) <= 1:
-            spot = 1 - ahead if mirrored else 1 + ahead
-            parts.append(near_ref[head, :, spot * tile : (spot + 1) * tile])
-        else:
-            parts.append(jnp.full((tile, tile), high_far if ahead > 0 else low_far, jnp.float32))
-    return jnp.concatenate(parts, axis=1)
+def bias_tile(near_ref, head, row_block, column_block, low_far, high_far):
+    ahead = row_block - column_block
+    if abs(ahead) <= 1:
+        spot = 1 - ahead
+        return near_ref[head, :, spot * tile : (spot + 1) * tile]
+    return jnp.full((tile, tile), high_far if ahead > 0 else low_far, jnp.float32)
 
 
 def unit_scale(values):
@@ -716,9 +735,9 @@
 
 
 def forward_kernel(
-    lengths, prefixes, far, x_ref, lines_ref, gain_a, wq, wk, wv, wo, gain_f, widen, narrow, gain_z,
+    lengths, prefixes, far, x_ref, lines_ref, gain_a, wq, wk, wv, wo, gain_f, widen_far, narrow_far, gain_z,
     normed_ref, q_ref, k_ref, v_ref, lse_ref, context_ref, mixed_ref, ffn_ref, hidden_ref, output_ref, pooled_ref,
-    near_ref, lse_cols,
+    near_ref, widen, narrow, weight_sem,
 ):
     seq = pl.program_id(0)
     heads = far.shape[1]
@@ -726,7 +745,17 @@
     blocks = slot_len // tile
     pair = 2 * width // heads
     length = lengths[seq]
-    pl.when(seq == 0)(lambda: spread_bias(lines_ref, near_ref, heads))
+    fetches = [
+        pltpu.make_async_copy(widen_far, widen, weight_sem.at[0]),
+        pltpu.make_async_copy(narrow_far, narrow, weight_sem.at[1]),
+    ]
+
+    def first():
+        for fetch in fetches:
+            fetch.start()
+        spread_bias(lines_ref, near_ref, heads)
+
+    pl.when(seq == 0)(first)
     tokens = x_ref[...].astype(jnp.float32)
     normed = (tokens * unit_scale(tokens) * gain_a[...]).astype(jnp.bfloat16)
     normed_ref[...] = normed
@@ -734,42 +763,46 @@
     k_ref[...] = low_dot(normed, wk[...]).astype(jnp.bfloat16)
     v_ref[...] = low_dot(normed, wv[...]).astype(jnp.bfloat16)
     lanes = lax.broadcasted_iota(jnp.int32, (1, pair), 1)
-    valid = lax.broadcasted_iota(jnp.int32, (1, slot_len), 1) < length
-    columns = lax.broadcasted_iota(jnp.int32, (tile, tile), 1)
+    places = lax.broadcasted_iota(jnp.int32, (slot_len, 1), 0)
 
     def attend(index, carry):
         span = pl.ds(pl.multiple_of(index * pair, pair), pair)
         keys = k_ref[:, span]
         queries = q_ref[:, span]
-        values = v_ref[:, span]
-        total = None
+        values_across = v_ref[:, span].T
+        pieces = []
         for side in range(2):
             head = 2 * index + side
             mine = (lanes // (pair // 2) == side).astype(jnp.bfloat16)
-            raw = dot_across(queries * mine, keys)
-            rows = []
-            for block in range(blocks):
-                part = slice(block * tile, (block + 1) * tile)
-                bias = bias_row(near_ref, head, block, blocks, far[0, head], far[1, head], False)
-                scores = jnp.where(valid, raw[part] + bias, masked_score)
-                peak = jnp.max(scores, axis=-1, keepdims=True)
+            raw = dot_across(keys, queries * mine)
+            soft_columns, lines = [], []
+            for column in range(blocks):
+                columns = slice(column * tile, (column + 1) * tile)
+                scores = []
+                for block in range(blocks):
+                    rows = slice(block * tile, (block + 1) * tile)
+                    bias = bias_tile(near_ref, head, block, column, far[0, head], far[1, head])
+                    scores.append(jnp.where(places[rows] < length, raw[rows, columns] + bias, masked_score))
+                scores = jnp.concatenate(scores, axis=0)
+                peak = jnp.max(scores, axis=0, keepdims=True)
                 raised = jnp.exp(scores - peak)
-                total_raised = jnp.sum(raised, axis=-1, keepdims=True)
-                rows.append((raised * (1.0 / total_raised)).astype(jnp.bfloat16))
-                lse_cols[part] = jnp.where(columns == head, peak + jnp.log(total_raised), lse_cols[part])
-            soft_low = jnp.concatenate(rows, axis=0)
-            piece = low_dot(soft_low, values * mine)
-            total = piece if total is None else total + piece
-        context_ref[:, span] = total.astype(jnp.bfloat16)
+                total = jnp.sum(raised, axis=0, keepdims=True)
+                soft_columns.append((raised * (1.0 / total)).astype(jnp.bfloat16))
+                lines.append(peak + jnp.log(total))
+            lse_ref[0, pl.ds(head, 1), :] = jnp.concatenate(lines, axis=1)
+            soft_low = jnp.concatenate(soft_columns, axis=1)
+            rows = slice(side * (pair // 2), (side + 1) * (pair // 2))
+            pieces.append(low_dot(values_across[rows], soft_low).astype(jnp.bfloat16))
+        context_ref[:, span] = jnp.concatenate(pieces, axis=0).T
         return carry
 
     lax.fori_loop(0, heads // 2, attend, 0)
-    lse_ref[0] = lse_cols[...].T[: lse_ref.shape[1]]
     mixed = tokens + low_dot(context_ref[...], wo[...])
     mixed_ref[...] = mixed
     ffn_in = (mixed * unit_scale(mixed) * gain_f[...]).astype(jnp.bfloat16)
     ffn_ref[...] = ffn_in
     output_ref[...] = mixed
+    pl.when(seq == 0)(lambda: [fetch.wait() for fetch in fetches] and None)
 
     def feed(index, carry):
         span = pl.ds(pl.multiple_of(index * width, 128), width)
@@ -781,7 +814,6 @@
 
     lax.fori_loop(0, widen.shape[1] // width, feed, 0)
     output = output_ref[...]
-    places = lax.broadcasted_iota(jnp.int32, (slot_len, 1), 0)
     mask = jnp.logical_and(places >= prefixes[seq], places < length).astype(jnp.float32)
     count = (length - prefixes[seq]).astype(jnp.float32)
     final = output * unit_scale(output) * gain_z[...]
@@ -817,7 +849,7 @@
             grid=(seqs,),
             in_specs=[
                 block(width), whole((16, 4 * tile)), line, square, square, square, square,
-                line, whole((width, ff)), whole((ff, width)), line,
+                line, pl.BlockSpec(memory_space=pl.ANY), pl.BlockSpec(memory_space=pl.ANY), line,
             ],
             out_specs=[
                 block(width), block(width), block(width), block(width),
@@ -827,7 +859,9 @@
             ],
             scratch_shapes=[
                 pltpu.VMEM((heads, tile, near), jnp.float32),
-                pltpu.VMEM((slot_len, tile), jnp.float32),
+                pltpu.VMEM((width, ff), low),
+                pltpu.VMEM((ff, width), low),
+                pltpu.SemaphoreType.DMA((2,)),
             ],
         ),
         out_shape=(
@@ -962,8 +996,9 @@
     far = jnp.stack([bucket_bias[buckets // 2 - 1], bucket_bias[buckets - 1]])
     gains = (gain_attention, gain_feedforward, gain_final)
     weights = (query_weight, key_weight, value_weight, output_weight, widen_weight, narrow_weight)
+    lines = bias_lines(bucket_bias)
     normed, query, key, value, totals, context, mixed, ffn_in, hidden, output, pooled = run_forward(
-        tokens[0], lengths[0], prefixes[0], far, bias_lines(bucket_bias, False), gains, weights
+        tokens[0], lengths[0], prefixes[0], far, lines, gains, weights
     )
     pooled = pooled[:, 0]
     inverse_pool = lax.rsqrt(jnp.sum(pooled * pooled, axis=-1, keepdims=True) + epsilon)
@@ -1004,15 +1039,10 @@
     streamed = (
         hidden, ffn_in, context, normed, branch, pre, attn, query, key, value, context_grad, tokens[0], mixed_grad
     )
-    resident = (totals, bias_lines(bucket_bias, True), gain_attention[None], *weights[:3])
-    summed, token_gradient, sums = sum_weights(batch_size, 1, lengths[0], far, streamed, feed_gains, resident)
+    resident = (totals, lines, gain_attention[None], *weights[:3])
+    sum_narrow, sum_widen, squares, token_gradient, sums = sum_weights(batch_size, 1, lengths[0], far, streamed, feed_gains, resident)
     sum_bucket = bucket_sums(sums[8:, : 4 * tile], bucket_bias.shape)
-    ff = hidden.shape[1]
-    sum_widen = summed[ff : 2 * ff].reshape(ff // width, width, width)
-    sum_widen = sum_widen.transpose(1, 0, 2).reshape(width, ff)
-    sum_output, sum_query, sum_key, sum_value = (
-        summed[2 * ff + n * width : 2 * ff + (n + 1) * width] for n in range(4)
-    )
+    sum_output, sum_query, sum_key, sum_value = (squares[n * width : (n + 1) * width] for n in range(4))
     return (
         loss_value,
         my_rows,
@@ -1025,7 +1055,7 @@
         sum_bucket,
         sums[1],
         sum_widen,
-        summed[:ff],
+        sum_narrow,
         sums[2],
     )
 

time: 443 us -> 426 us (0.962)
  Pallas kernels: 393 us -> 381 us
    unnamed x9 -> x19, local copies, waits for them, and re-layouts: 1.86 us -> 13.2 us
    slice x2 -> x1, local copies, waits for them, and re-layouts: 18.5 us -> 8.7 us  [local(): squares[n * width:(n + 1) * width]]
    pallas_call x1, Pallas kernels: 89.1 us -> 80.2 us  [run_forward(): pl.pallas_call(forward_kernel, grid_spec=pltpu.PrefetchScalarGridSpec(num...]
    reshape x1 -> x0, local copies, waits for them, and re-layouts: 5.17 us -> none  [local(): sum_widen = sum_widen.transpose(1, 0, 2).reshape(width, ff)]
where the time goes in v5:
time: 426 us; the launch traced here: 425 us
  Pallas kernels  381 us (89%)
  local copies, waits for them, and re-layouts  30.5 us (7%)
  other arithmetic  5.02 us (1%)
  matrix products  4.43 us (1%)
    pallas_call x1, Pallas kernels, sum_weights(): pl.pallas_call(functools.partial(sums_kernel, dims, jobs), out_shape=(jax...  240 us
    pallas_call x1, Pallas kernels, run_forward(): pl.pallas_call(forward_kernel, grid_spec=pltpu.PrefetchScalarGridSpec(num...  80.2 us
    pallas_call x1, Pallas kernels, run_feed_back(): pl.pallas_call(feed_back_kernel, grid_spec=pltpu.PrefetchScalarGridSpec(n...  46.9 us
    pallas_call x1, Pallas kernels, gather_blocks(): pl.pallas_call(functools.partial(gather_kernel, groups), out_shape=jax.Sh...  13.3 us
    unnamed x19, local copies, waits for them, and re-layouts  13.2 us
    slice x1, local copies, waits for them, and re-layouts, local(): squares[n * width:(n + 1) * width]  8.7 us

profile of v5, /device:TPU:0, one launch (start us, length us, event | category | flops | bytes accessed | tf_op | source)
XLA Modules:
  0.0 424.6 jit_solution(3300512712777657034)
XLA Ops:
  0.7 1.3 broadcast_in_dim.16.gain_a.refs_18_
  1.9 1.3 broadcast_in_dim.17.gain_f
  3.2 1.3 broadcast_in_dim.18.gain_z
  4.5 0.8 fusion.20
  5.3 0.1 copy.30
  5.5 0.6 pad_maximum_fusion.far.refs_1_
  6.1 1.0 convolution_bitcast_fusion
  7.1 0.6 pad.4.lines_ref.refs_17_
  7.7 80.2 %forward.1 = (bf16[2048,768]{1,0:T(8,128)(2,1)}, bf16[2048,768]{1,0:T(8,128)(2,1)}, bf16[2048,768]{1,0:T(8,128)(2,1)}, bf16[2048,768]{1,0:T(8,128)(2,1)}, f32[4,...) custom-call(s32[4]{0:T(128)} %bitcast.30, ...), custom_call_target="tpu_custom_call" | custom-call | tf_op jit(solution)/shard_map/forward/pallas_call | solution.py:845
  87.9 0.8 fusion.8
  88.8 1.4 bitcast_multiply_fusion.2.block_ref
  90.2 13.3 %gather_blocks.1 = f32[2,16,4,768]{3,2,1,0:T(4,128)} custom-call(f32[4,768]{1,0:T(4,128)} %bitcast_multiply_fusion.2.block_ref), custom_call_target="tpu_custom_call" | custom-call | tf_op jit(solution)/shard_map/gather_blocks/pallas_call | solution.py:85
  103.5 1.1 fusion.19
  104.7 0.4 fusion.17
  105.1 0.7 select_reduce_fusion
  105.8 0.1 convert_subtract_fusion
  105.9 0.3 convolution_multiply_fusion.1
  106.3 1.0 fusion.11
  107.3 0.6 add_reduce_fusion
  109.9 0.8 fusion.10
  110.7 0.6 broadcast_in_dim.19.pooled_ref
  111.3 46.9 %feed_back.1 = (bf16[2048,768]{1,0:T(8,128)(2,1)}, bf16[2048,3072]{1,0:T(8,128)(2,1)}, bf16[2048,768]{1,0:T(8,128)(2,1)}, bf16[2048,768]{1,0:T(8,128)(2,1)}, f32[2048,768]{1,0:T(8,128)}, /*index=5*/f32[8,768]{1,0:T(8,128)}) custom-call(s32[4]{0:T(128)} %bitcast.31, s32[4]{0:T(128)} %bitcast.34, bf16[768,768]{1,0:T(8,128)(2,1)} %wo.3, ...), custom_call_target="tpu_custom_call" | custom-call | tf_op jit(solution)/shard_map/feed_back/pallas_call | solution.py:944
  158.1 240.5 %sum_weights.1 = (f32[3072,768]{1,0:T(8,128)}, f32[768,3072]{1,0:T(8,128)}, f32[3072,768]{1,0:T(8,128)}, bf16[2048,768]{1,0:T(8,128)(2,1)}, f32[24,768]{1,0:T(8,128)}) custom-call(s32[4]{0:T(128)} %bitcast.32, f32[2,12]{1,0:T(2,128)} %pad_maximum_fusion.far.refs_1_, bf16[2048,3072]{1,0:T(8,128)(2,1)} %get-tuple-element.36.hidden_ref.refs_2_, ...), custom_call_target="tpu_custom_call" | custom-call | tf_op jit(solution)/shard_map/sum_weights/pallas_call | solution.py:643
  398.6 1.6 fusion.1
  400.3 1.5 slice_reduce_fusion
  401.8 8.7 %fusion.18 = (f32[768,768]{1,0:T(8,128)}, f32[768,768]{1,0:T(8,128)}, f32[768,768]{1,0:T(8,128)}, f32[768,768]{1,0:T(8,128)}) fusion(f32[3072,768]{1,0:T(8,128)} %get-tuple-element.54), kind=kLoop, calls=%fused_computation.43 | loop fusion | bytes 18874368 | tf_op jit(solution)/shard_map/slice | solution.py:1045
  410.5 1.7 copy.39
  412.1 1.4 copy-done
  413.6 4.8 %copy.40 = f32[768,3072]{1,0:T(8,128)} copy(f32[768,3072]{1,0:T(8,128)S(1)} %copy-done) | data formatting | bytes 18874368
  418.4 1.2 slice-done.1
  419.5 0.2 slice-done.2
  419.7 3.7 copy.41
  (18 shorter events, 0.3 us)
Async XLA Ops:
  7.7 97.4 %copy-start.3 = (s32[64]{0:T(128)S(1)}, s32[64]{0:T(128)}, u32[]{:S(2)}) copy-start(s32[64]{0:T(128)} %param.17) | copy-start | bytes 772
  106.3 51.8 %copy-start.2 = (f32[4,64]{1,0:T(4,128)}, f32[4,64]{1,0:T(4,128)S(1)}, u32[]{:S(2)}) copy-start(f32[4,64]{1,0:T(4,128)S(1)} %constant_dynamic-slice_fusion) | copy-start | bytes 3076
  401.8 8.7 %copy-start.1 = (bf16[2048,768]{1,0:T(8,128)(2,1)S(1)}, bf16[2048,768]{1,0:T(8,128)(2,1)}, u32[]{:S(2)}) copy-start(bf16[2048,768]{1,0:T(8,128)(2,1)} %get-tuple-element.52) | copy-start | bytes 9437188
  401.8 11.8 %copy-start = (f32[768,3072]{1,0:T(8,128)S(1)}, f32[768,3072]{1,0:T(8,128)}, u32[]{:S(2)}) copy-start(f32[768,3072]{1,0:T(8,128)} %get-tuple-element.103) | copy-start | bytes 28311556
  410.5 7.9 %slice-start = ((s8[9437184]{0:T(1024)(128)(4,1)}), s8[4194304]{0:T(1024)(128)(4,1)S(1)}, s32[]{:S(2)}) async-start(s8[9437184]{0:T(1024)(128)(4,1)} %bitcast.27), calls=%async_computation | async-start | bytes 8388608
  413.6 5.9 %slice-start.1 = ((s8[9437184]{0:T(1024)(128)(4,1)}), s8[4194304]{0:T(1024)(128)(4,1)S(1)}, s32[]{:S(2)}) async-start(s8[9437184]{0:T(1024)(128)(4,1)} %bitcast.27), calls=%async_computation.1 | async-start | bytes 8388608
  413.6 6.2 %slice-start.2 = ((s8[9437184]{0:T(1024)(128)(4,1)}), s8[1048576]{0:T(1024)(128)(4,1)S(1)}, s32[]{:S(2)}) async-start(s8[9437184]{0:T(1024)(128)(4,1)} %bitcast.27), calls=%async_computation.2 | async-start | bytes 2097152

commit v6 on v5

--- a/solution.py
+++ b/solution.py
@@ -29,22 +29,27 @@
     return lax.axis_index("tower"), lax.axis_index("batch")
 
 
-def gather_kernel(groups, block_ref, out_ref, slots, send_sem, recv_sem, mate_sem):
+def gather_peer(groups, step):
+    tower, batch = place()
+    return tower, lax.rem(batch + step, groups)
+
+
+def greet_all(groups):
     tower, batch = place()
     barrier = pltpu.get_barrier_semaphore()
-    mate = (1 - tower, batch)
-
-    def peer(step):
-        return tower, lax.rem(batch + step, groups)
 
     def greet(step, carry):
-        pl.semaphore_signal(barrier, 1, device_id=peer(step), device_id_type=MESH)
+        pl.semaphore_signal(barrier, 1, device_id=gather_peer(groups, step), device_id_type=MESH)
         return carry
 
     lax.fori_loop(1, groups, greet, 0)
-    pl.semaphore_signal(barrier, 1, device_id=mate, device_id_type=MESH)
+    pl.semaphore_signal(barrier, 1, device_id=(1 - tower, batch), device_id_type=MESH)
+
+
+def gather_units(groups, block_ref, out_ref, slots, send_sem, recv_sem, mate_sem):
+    tower, batch = place()
     slots[tower, batch] = block_ref[...]
-    pl.semaphore_wait(barrier, groups)
+    pl.semaphore_wait(pltpu.get_barrier_semaphore(), groups)
 
     def copy(step, owner):
         return pltpu.make_async_remote_copy(
@@ -52,7 +57,7 @@
             dst_ref=slots.at[tower, owner],
             send_sem=send_sem.at[step],
             recv_sem=recv_sem.at[owner],
-            device_id=peer(step),
+            device_id=gather_peer(groups, step),
             device_id_type=MESH,
         )
 
@@ -62,7 +67,7 @@
 
     def finish(step, carry):
         copy(step, batch).wait_send()
-        copy(step, peer(step)[1]).wait_recv()
+        copy(step, gather_peer(groups, step)[1]).wait_recv()
         return carry
 
     lax.fori_loop(1, groups, begin, 0)
@@ -72,30 +77,12 @@
         dst_ref=slots.at[tower],
         send_sem=mate_sem.at[0],
         recv_sem=mate_sem.at[1],
-        device_id=mate,
+        device_id=(1 - tower, batch),
         device_id_type=MESH,
     )
     side.start()
     side.wait()
     out_ref[...] = slots[...]
-
-
-def gather_blocks(block, groups, collective):
-    whole = (2, groups) + block.shape
-    return pl.pallas_call(
-        functools.partial(gather_kernel, groups),
-        out_shape=jax.ShapeDtypeStruct(whole, jnp.float32),
-        in_specs=[pl.BlockSpec(memory_space=pltpu.VMEM)],
-        out_specs=pl.BlockSpec(memory_space=pltpu.VMEM),
-        scratch_shapes=[
-            pltpu.VMEM(whole, jnp.float32),
-            pltpu.SemaphoreType.DMA((groups,)),
-            pltpu.SemaphoreType.DMA((groups,)),
-            pltpu.SemaphoreType.DMA((2,)),
-        ],
-        compiler_params=pltpu.CompilerParams(collective_id=collective, has_side_effects=True),
-        name="gather_blocks",
-    )(block)
 
 
 def both(first, second):
@@ -209,8 +196,8 @@
 
 
 def sums_kernel(dims, jobs, *refs):
-    (lengths, far, hidden, ffn_in, context, normed, branch, pre, attn, query, key, value, upstream) = refs[:13]
-    (tokens, mixed_grad, small, totals, lines, gain, wq, wk, wv) = refs[13:22]
+    (lengths, table, hidden, ffn_in, context, normed, branch, pre, attn, query, key, value, upstream) = refs[:13]
+    (tokens, mixed_grad, small, totals, bias_ref, gain, wq, wk, wv) = refs[13:22]
     (narrow_out, widen_out, square_out, token_out, small_out) = refs[22:27]
     (left, right, part, acc, full, mate_in, small_own, small_in, heads_in, by_query, by_key, by_value) = refs[27:39]
     (near_ref, near_sums, far_sums, token_in, mixed_in, token_buffer) = refs[39:45]
@@ -254,11 +241,12 @@
 
     held, spread_held = acc.shape[0], full.shape[0]
     width = narrow_out.shape[1]
-    heads = far.shape[1]
+    heads = table.shape[1]
     seqs = lengths.shape[0]
     slot_len = tokens.shape[0] // seqs
     pair = 2 * width // heads
-    pairs = heads // 2
+    group = heads_in.shape[3]
+    pairs = width // group
     tasks = seqs * pairs
     blocks = slot_len // tile
 
@@ -479,7 +467,7 @@
 
     def heads_load(task, begin):
         rows = pl.ds(pl.multiple_of(task // pairs * slot_len, slot_len), slot_len)
-        columns = pl.ds(pl.multiple_of(lax.rem(task, pairs) * pair, pair), pair)
+        columns = pl.ds(pl.multiple_of(lax.rem(task, pairs) * group, group), group)
         slot = lax.rem(task, 2)
         for index, ref in enumerate((query, key, value, upstream)):
             copy = pltpu.make_async_copy(
@@ -495,7 +483,13 @@
         slot = lax.rem(task, 2)
         heads_load(task, False)
         pl.when(task + 1 < tasks)(lambda: heads_load(task + 1, True))
-        queries, keys, values, upper = (heads_in[slot, n] for n in range(4))
+        for inside in range(group // pair):
+            attend_pair(seq, index * (group // pair) + inside, slot, inside)
+        return carry
+
+    def attend_pair(seq, index, slot, inside):
+        span = slice(inside * pair, (inside + 1) * pair)
+        queries, keys, values, upper = (heads_in[slot, n, :, span] for n in range(4))
         length = lengths[seq]
         keys_across = keys.T
         grads_out = [None] * 2
@@ -515,7 +509,7 @@
                 scores = []
                 for block in range(blocks):
                     rows = slice(block * tile, (block + 1) * tile)
-                    bias = bias_tile(near_ref, head, block, column, far[0, head], far[1, head])
+                    bias = bias_tile(near_ref, head, block, column, *far_bias(table, head))
                     scores.append(jnp.where(places[rows] < length, raw[rows, columns] + bias, masked_score))
                 soft = jnp.exp(jnp.concatenate(scores, axis=0) - line[:, columns])
                 soft_columns.append(soft.astype(jnp.bfloat16))
@@ -544,7 +538,6 @@
         by_query[rows, columns] = jnp.concatenate(query_rows, axis=0).T
         for ref, grads in zip((by_key, by_value), grads_out):
             ref[rows, columns] = grads.astype(jnp.bfloat16)
-        return carry
 
     def token_load(seq, begin):
         rows = pl.ds(pl.multiple_of(seq * slot_len, slot_len), slot_len)
@@ -561,7 +554,7 @@
         token_load(seq, False)
         normed_grad = dot_across(by_query[rows, :], wq[...]) + dot_across(by_key[rows, :], wk[...])
         normed_grad += dot_across(by_value[rows, :], wv[...])
-        by_tokens, token_gain = norm_back(token_in[...].astype(jnp.float32), gain[...], normed_grad)
+        by_tokens, token_gain = norm_back(token_in[...].astype(jnp.float32), gain[...][None], normed_grad)
         small_own[0, 0:1] += token_gain
         pl.when(seq > 0)(lambda: token_store(seq - 1).wait())
         token_buffer[...] = (mixed_in[...] + by_tokens).astype(jnp.bfloat16)
@@ -585,13 +578,13 @@
     load(0)
     heads_load(0, True)
     token_load(0, True)
-    spread_bias(lines, near_ref, heads)
+    spread_bias(bias_ref, near_ref, heads)
     near_sums[...] = jnp.zeros_like(near_sums)
     far_sums[...] = jnp.zeros_like(far_sums)
     small_own[0, 0:8, :] = small[...]
     pl.semaphore_wait(barrier, len(mates))
 
-    last_attend = jobs - 3 * (width // job_rows)
+    last_attend = jobs - 3 * (width // job_rows) - 1
     first_small = slots - 1 - len(turns)
     first_token = first_small - 1 - seqs
 
@@ -604,8 +597,8 @@
             pl.when(time == first_small + turn)(functools.partial(small_turn, turn))
         begin = jnp.minimum(time * tasks // last_attend, tasks)
         end = jnp.minimum((time + 1) * tasks // last_attend, tasks)
+        pl.when(time < jobs)(functools.partial(compute, time))
         lax.fori_loop(begin, end, attend, 0)
-        pl.when(time < jobs)(functools.partial(compute, time))
         seq = time - first_token
         pl.when(jnp.logical_and(seq >= 0, seq < seqs))(functools.partial(token_task, seq))
         pl.when(time == first_small - 1)(close)
@@ -614,11 +607,11 @@
     lax.fori_loop(0, slots, slot, 0)
 
 
-def sum_weights(batch_size, collective, lengths, far, streamed, small, resident):
+def sum_weights(batch_size, collective, lengths, bucket_bias, streamed, small, resident):
     hidden, normed = streamed[0], streamed[3]
     tokens, width = normed.shape
     seqs = lengths.shape[0]
-    heads = far.shape[1]
+    heads = bucket_bias.shape[1]
     slot_len = tokens // seqs
     pair = 2 * width // heads
     total = 2 * hidden.shape[1] + 4 * width
@@ -660,7 +653,7 @@
             pltpu.VMEM((4, 3 * half, width), full),
             pltpu.VMEM((turns, lines, width), full),
             pltpu.VMEM((turns, lines, width), full),
-            pltpu.VMEM((2, 4, slot_len, pair), low),
+            pltpu.VMEM((2, 4, slot_len, 1 * pair), low),
             pltpu.VMEM((tokens, width), low),
             pltpu.VMEM((tokens, width), low),
             pltpu.VMEM((tokens, width), low),
@@ -685,33 +678,36 @@
             collective_id=collective, has_side_effects=True, vmem_limit_bytes=66500000
         ),
         name="sum_weights",
-    )(lengths, far, *streamed, small, *resident)
+    )(lengths, bucket_bias, *streamed, small, *resident)
 
 
 tile = 128
 near = 3 * tile
 
 
-def bias_lines(bucket_bias):
-    buckets, heads = bucket_bias.shape
-    spots = jnp.arange(4 * tile, dtype=jnp.int32)
-    moved = jnp.where(spots >= near, spots - 4 * tile, spots)
-    onehot = offset_onehot(tile - moved, buckets)
-    lines = jnp.dot(bucket_bias.T, onehot.T, precision=highest)
-    return jnp.pad(lines, ((0, 16 - heads), (0, 0)))
-
-
-def offset_onehot(offset, buckets):
+def offset_onehot(buckets):
+    spots = lax.broadcasted_iota(jnp.int32, (buckets, 4 * tile), 1)
+    labels = lax.broadcasted_iota(jnp.int32, (buckets, 4 * tile), 0)
+    offset = tile - jnp.where(spots >= near, spots - 4 * tile, spots)
     spread = jnp.abs(offset)
     far_bucket = 8 + sum(((spread >= step).astype(jnp.int32) for step in far_steps))
     bucket = jnp.where(spread < 8, spread, far_bucket) + jnp.where(offset > 0, buckets // 2, 0)
-    return (bucket[:, None] == jnp.arange(buckets, dtype=jnp.int32)[None, :]).astype(jnp.float32)
-
-
-def spread_bias(lines_ref, near_ref, heads):
+    return (bucket == labels).astype(jnp.float32)
+
+
+def spread_bias(bias_ref, near_ref, heads):
+    lines = lax.dot_general(
+        bias_ref[...], offset_onehot(bias_ref.shape[0]), (((0,), (0,)), ((), ())),
+        precision=highest, preferred_element_type=jnp.float32,
+    )
     for head in range(heads):
-        line = jnp.broadcast_to(lines_ref[head : head + 1, :], (tile, 4 * tile))
+        line = jnp.broadcast_to(lines[head : head + 1, :], (tile, 4 * tile))
         near_ref[head] = pltpu.roll(line, 0, 1, stride=1, stride_axis=0)[:, :near]
+
+
+def far_bias(table, head):
+    buckets = table.shape[0]
+    return table[buckets // 2 - 1, head], table[buckets - 1, head]
 
 
 def bias_tile(near_ref, head, row_block, column_block, low_far, high_far):
@@ -735,12 +731,12 @@
 
 
 def forward_kernel(
-    lengths, prefixes, far, x_ref, lines_ref, gain_a, wq, wk, wv, wo, gain_f, widen_far, narrow_far, gain_z,
-    normed_ref, q_ref, k_ref, v_ref, lse_ref, context_ref, mixed_ref, ffn_ref, hidden_ref, output_ref, pooled_ref,
-    near_ref, widen, narrow, weight_sem,
+    groups, lengths, prefixes, table, x_ref, bias_ref, gain_a, wq, wk, wv, wo, gain_f, widen_far, narrow_far, gain_z,
+    normed_ref, q_ref, k_ref, v_ref, lse_ref, context_ref, mixed_ref, ffn_ref, hidden_ref, output_ref, pooled_ref, units_ref,
+    near_ref, widen, narrow, weight_sem, slots, block_ref, send_sem, recv_sem, mate_sem,
 ):
     seq = pl.program_id(0)
-    heads = far.shape[1]
+    heads = table.shape[1]
     slot_len, width = x_ref.shape
     blocks = slot_len // tile
     pair = 2 * width // heads
@@ -751,13 +747,14 @@
     ]
 
     def first():
+        greet_all(groups)
         for fetch in fetches:
             fetch.start()
-        spread_bias(lines_ref, near_ref, heads)
+        spread_bias(bias_ref, near_ref, heads)
 
     pl.when(seq == 0)(first)
     tokens = x_ref[...].astype(jnp.float32)
-    normed = (tokens * unit_scale(tokens) * gain_a[...]).astype(jnp.bfloat16)
+    normed = (tokens * unit_scale(tokens) * gain_a[...][None]).astype(jnp.bfloat16)
     normed_ref[...] = normed
     q_ref[...] = low_dot(normed, wq[...]).astype(jnp.bfloat16)
     k_ref[...] = low_dot(normed, wk[...]).astype(jnp.bfloat16)
@@ -781,7 +778,7 @@
                 scores = []
                 for block in range(blocks):
                     rows = slice(block * tile, (block + 1) * tile)
-                    bias = bias_tile(near_ref, head, block, column, far[0, head], far[1, head])
+                    bias = bias_tile(near_ref, head, block, column, *far_bias(table, head))
                     scores.append(jnp.where(places[rows] < length, raw[rows, columns] + bias, masked_score))
                 scores = jnp.concatenate(scores, axis=0)
                 peak = jnp.max(scores, axis=0, keepdims=True)
@@ -796,10 +793,10 @@
         context_ref[:, span] = jnp.concatenate(pieces, axis=0).T
         return carry
 
-    lax.fori_loop(0, heads // 2, attend, 0)
+    lax.fori_loop(0, heads // 2, attend, 0, unroll=True)
     mixed = tokens + low_dot(context_ref[...], wo[...])
     mixed_ref[...] = mixed
-    ffn_in = (mixed * unit_scale(mixed) * gain_f[...]).astype(jnp.bfloat16)
+    ffn_in = (mixed * unit_scale(mixed) * gain_f[...][None]).astype(jnp.bfloat16)
     ffn_ref[...] = ffn_in
     output_ref[...] = mixed
     pl.when(seq == 0)(lambda: [fetch.wait() for fetch in fetches] and None)
@@ -812,22 +809,30 @@
         output_ref[...] += low_dot(hidden, narrow[span, :])
         return carry
 
-    lax.fori_loop(0, widen.shape[1] // width, feed, 0)
+    lax.fori_loop(0, widen.shape[1] // width, feed, 0, unroll=True)
     output = output_ref[...]
     mask = jnp.logical_and(places >= prefixes[seq], places < length).astype(jnp.float32)
     count = (length - prefixes[seq]).astype(jnp.float32)
-    final = output * unit_scale(output) * gain_z[...]
-    pooled_ref[0] = jnp.sum(final * (mask / count), axis=0, keepdims=True)
-
-
-def run_forward(tokens, lengths, prefixes, far, lines, gains, weights):
+    final = output * unit_scale(output) * gain_z[...][None]
+    pooled_ref[pl.ds(seq, 1), :] = jnp.sum(final * (mask / count), axis=0, keepdims=True)
+
+    def last():
+        pooled = pooled_ref[...]
+        block_ref[...] = pooled * lax.rsqrt(jnp.sum(pooled * pooled, axis=-1, keepdims=True) + epsilon)
+        gather_units(groups, block_ref, units_ref, slots, send_sem, recv_sem, mate_sem)
+
+    pl.when(seq == pl.num_programs(0) - 1)(last)
+
+
+def run_forward(groups, collective, tokens, lengths, prefixes, bucket_bias, gains, weights):
     rows, width = tokens.shape
     seqs = lengths.shape[0]
     slot_len = rows // seqs
-    heads = far.shape[1]
+    heads = bucket_bias.shape[1]
     wq, wk, wv, wo, widen, narrow = weights
     gain_a, gain_f, gain_z = gains
     ff = widen.shape[1]
+    units = (2, groups, seqs, width)
 
     def whole(shape):
         return pl.BlockSpec(shape, lambda n, *_: (0,) * len(shape), pipeline_mode=pl.Buffered(1))
@@ -836,31 +841,37 @@
         return pl.BlockSpec((slot_len, columns), lambda n, *_: (n, 0))
 
     square = whole((width, width))
-    line = whole((1, width))
+    line = whole((width,))
     low, full = jnp.bfloat16, jnp.float32
 
     def shape(columns, kind):
         return jax.ShapeDtypeStruct((rows, columns), kind)
 
     return pl.pallas_call(
-        forward_kernel,
+        functools.partial(forward_kernel, groups),
         grid_spec=pltpu.PrefetchScalarGridSpec(
             num_scalar_prefetch=3,
             grid=(seqs,),
             in_specs=[
-                block(width), whole((16, 4 * tile)), line, square, square, square, square,
+                block(width), whole(bucket_bias.shape), line, square, square, square, square,
                 line, pl.BlockSpec(memory_space=pl.ANY), pl.BlockSpec(memory_space=pl.ANY), line,
             ],
             out_specs=[
                 block(width), block(width), block(width), block(width),
                 pl.BlockSpec((1, 16, slot_len), lambda n, *_: (n, 0, 0)),
                 block(width), block(width), block(width), block(ff), block(width),
-                pl.BlockSpec((1, 1, width), lambda n, *_: (n, 0, 0)),
+                pl.BlockSpec((seqs, width), lambda n, *_: (0, 0)),
+                pl.BlockSpec(units, lambda n, *_: (0, 0, 0, 0)),
             ],
             scratch_shapes=[
                 pltpu.VMEM((heads, tile, near), jnp.float32),
                 pltpu.VMEM((width, ff), low),
                 pltpu.VMEM((ff, width), low),
+                pltpu.SemaphoreType.DMA((2,)),
+                pltpu.VMEM(units, full),
+                pltpu.VMEM((seqs, width), full),
+                pltpu.SemaphoreType.DMA((groups,)),
+                pltpu.SemaphoreType.DMA((groups,)),
                 pltpu.SemaphoreType.DMA((2,)),
             ],
         ),
@@ -868,11 +879,14 @@
             shape(width, low), shape(width, low), shape(width, low), shape(width, low),
             jax.ShapeDtypeStruct((seqs, 16, slot_len), full),
             shape(width, low), shape(width, full), shape(width, low), shape(ff, low), shape(width, full),
-            jax.ShapeDtypeStruct((seqs, 1, width), full),
+            jax.ShapeDtypeStruct((seqs, width), full),
+            jax.ShapeDtypeStruct(units, full),
         ),
-        compiler_params=pltpu.CompilerParams(vmem_limit_bytes=60000000),
+        compiler_params=pltpu.CompilerParams(
+            collective_id=collective, has_side_effects=True, vmem_limit_bytes=60000000
+        ),
         name="forward",
-    )(lengths, prefixes, far, tokens, lines, gain_a[None], wq, wk, wv, wo, gain_f[None], widen, narrow, gain_z[None])
+    )(lengths, prefixes, bucket_bias, tokens, bucket_bias, gain_a, wq, wk, wv, wo, gain_f, widen, narrow, gain_z)
 
 
 def norm_back(values, gain, upstream):
@@ -883,9 +897,51 @@
     return by_values, jnp.sum(upstream * values * inverse, axis=0, keepdims=True)
 
 
+def exact_dot(left, right, left_dim, right_dim):
+    return lax.dot_general(
+        left, right, (((left_dim,), (right_dim,)), ((), ())),
+        precision=highest, preferred_element_type=jnp.float32,
+    )
+
+
+def contrast(units_ref, pooled_ref, positives_ref, loss_ref, rows_ref, pooled_grad):
+    tower, batch = place()
+    _, groups, seqs, width = units_ref.shape
+    count = groups * seqs
+    queries = units_ref[0].reshape(count, width)
+    docs = units_ref[1].reshape(count, width)
+    scores = score_scale * exact_dot(queries, docs, 1, 1)
+    labels = lax.broadcasted_iota(jnp.int32, (count, count), 1)
+    target = (positives_ref[...] == labels).astype(jnp.float32)
+    row_peak = jnp.max(scores, axis=1, keepdims=True)
+    row_raised = jnp.exp(scores - row_peak)
+    row_sum = jnp.sum(row_raised, axis=1, keepdims=True)
+    column_peak = jnp.max(scores, axis=0, keepdims=True)
+    column_raised = jnp.exp(scores - column_peak)
+    column_sum = jnp.sum(column_raised, axis=0, keepdims=True)
+    loss = 0.5 * jnp.sum(row_peak + jnp.log(row_sum), axis=0, keepdims=True)
+    loss += 0.5 * jnp.sum(column_peak + jnp.log(column_sum), axis=1, keepdims=True)
+    loss_ref[...] = loss - jnp.sum(jnp.sum(target * scores, axis=1, keepdims=True), axis=0, keepdims=True)
+    grad = 0.5 * row_raised / row_sum + 0.5 * column_raised / column_sum - target
+    mine = lax.broadcasted_iota(jnp.int32, (8, count), 0) + batch * seqs
+    spots = lax.broadcasted_iota(jnp.int32, (8, count), 1)
+    select = (mine == spots).astype(jnp.float32)
+    my_rows = exact_dot(select, grad, 1, 0)
+    my_columns = exact_dot(select, grad, 1, 1)
+    rows_ref[...] = my_rows[:seqs]
+    as_query = exact_dot(my_rows, docs, 1, 0)
+    as_doc = exact_dot(my_columns, queries, 1, 0)
+    unit_grad = (score_scale * jnp.where(tower == 0, as_query, as_doc))[:seqs]
+    pooled = pooled_ref[...]
+    inverse = lax.rsqrt(jnp.sum(pooled * pooled, axis=-1, keepdims=True) + epsilon)
+    cubed = inverse * inverse * inverse
+    pooled_grad[:seqs] = inverse * unit_grad - pooled * cubed * jnp.sum(unit_grad * pooled, axis=-1, keepdims=True)
+
+
 def feed_back_kernel(
     lengths, prefixes, wo, gain_f, widen, narrow, gain_z, mixed_ref, hidden_ref, output_ref, pooled_ref,
-    branch_ref, pre_ref, attn_ref, context_ref, mixed_grad, gains_ref, feed_grad,
+    units_ref, positives_ref,
+    branch_ref, pre_ref, attn_ref, context_ref, mixed_grad, gains_ref, loss_ref, rows_ref, feed_grad, pooled_grad,
 ):
     seq = pl.program_id(0)
     slot_len, width = mixed_ref.shape
@@ -893,28 +949,29 @@
 
     def clear():
         gains_ref[...] = jnp.zeros_like(gains_ref)
+        contrast(units_ref, pooled_ref, positives_ref, loss_ref, rows_ref, pooled_grad)
 
     pl.when(seq == 0)(clear)
     places = lax.broadcasted_iota(jnp.int32, (slot_len, 1), 0)
     mask = jnp.logical_and(places >= prefixes[seq], places < length).astype(jnp.float32)
     count = (length - prefixes[seq]).astype(jnp.float32)
-    final_grad = (mask / count) * pooled_ref[0]
-    output_grad, final_gain = norm_back(output_ref[...], gain_z[...], final_grad)
+    final_grad = (mask / count) * pooled_grad[pl.ds(seq, 1), :]
+    output_grad, final_gain = norm_back(output_ref[...], gain_z[...][None], final_grad)
     gains_ref[2:3] += final_gain
     mixed_grad[...] = output_grad
     branch_ref[...] = output_grad.astype(jnp.bfloat16)
     feed_grad[...] = jnp.zeros_like(feed_grad)
 
     def feed(index, carry):
-        span = pl.ds(pl.multiple_of(index * width, 128), width)
+        span = pl.ds(pl.multiple_of(index * 2 * width, 128), 2 * width)
         hidden_grad = dot_across(branch_ref[...], narrow[span, :])
         pre_grad = jnp.where(hidden_ref[:, span] > 0, hidden_grad, 0.0).astype(jnp.bfloat16)
         pre_ref[:, span] = pre_grad
         feed_grad[...] += dot_across(pre_grad, widen[:, span])
         return carry
 
-    lax.fori_loop(0, widen.shape[1] // width, feed, 0)
-    by_mixed, feed_gain = norm_back(mixed_ref[...], gain_f[...], feed_grad[...])
+    lax.fori_loop(0, widen.shape[1] // (2 * width), feed, 0, unroll=True)
+    by_mixed, feed_gain = norm_back(mixed_ref[...], gain_f[...][None], feed_grad[...])
     gains_ref[1:2] += feed_gain
     total_grad = mixed_grad[...] + by_mixed
     mixed_grad[...] = total_grad
@@ -927,12 +984,13 @@
     return pl.BlockSpec(shape, lambda n, *_: (0,) * len(shape), pipeline_mode=pl.Buffered(1))
 
 
-def run_feed_back(lengths, prefixes, gains, weights, mixed, hidden, output, pooled_grad):
+def run_feed_back(lengths, prefixes, gains, weights, mixed, hidden, output, pooled, units, positives):
     rows, width = mixed.shape
     seqs = lengths.shape[0]
     slot_len = rows // seqs
     wo, widen, narrow = weights
     ff = widen.shape[1]
+    count = positives.shape[0]
 
     def block(columns):
         return pl.BlockSpec((slot_len, columns), lambda n, *_: (n, 0))
@@ -947,30 +1005,34 @@
             num_scalar_prefetch=2,
             grid=(seqs,),
             in_specs=[
-                whole((width, width)), whole((1, width)), whole((width, ff)), whole((ff, width)), whole((1, width)),
+                whole((width, width)), whole((width,)), whole((width, ff)), whole((ff, width)), whole((width,)),
                 block(width), block(ff), block(width),
-                pl.BlockSpec((1, 1, width), lambda n, *_: (n, 0, 0)),
+                whole(pooled.shape), whole(units.shape), whole((count, 1)),
             ],
             out_specs=[
                 block(width), block(ff), block(width), block(width), block(width),
                 pl.BlockSpec((8, width), lambda n, *_: (0, 0)),
+                pl.BlockSpec((1, 1), lambda n, *_: (0, 0)),
+                pl.BlockSpec((seqs, count), lambda n, *_: (0, 0)),
             ],
-            scratch_shapes=[pltpu.VMEM((slot_len, width), jnp.float32)],
+            scratch_shapes=[pltpu.VMEM((slot_len, width), jnp.float32), pltpu.VMEM((8, width), jnp.float32)],
         ),
         out_shape=(
             shape(width, low), shape(ff, low), shape(width, low), shape(width, low), shape(width, full),
             jax.ShapeDtypeStruct((8, width), full),
+            jax.ShapeDtypeStruct((1, 1), full),
+            jax.ShapeDtypeStruct((seqs, count), full),
         ),
         compiler_params=pltpu.CompilerParams(vmem_limit_bytes=60000000),
         name="feed_back",
-    )(lengths, prefixes, wo, gains[0][None], widen, narrow, gains[1][None], mixed, hidden, output, pooled_grad)
+    )(
+        lengths, prefixes, wo, gains[0], widen, narrow, gains[1], mixed, hidden, output, pooled, units,
+        positives[:, None],
+    )
 
 
 def bucket_sums(offset_sums, shape):
-    spots = jnp.arange(4 * tile, dtype=jnp.int32)
-    moved = jnp.where(spots >= near, spots - 4 * tile, spots)
-    onehot = offset_onehot(tile - moved, shape[0])
-    return jnp.dot(onehot.T, offset_sums[: shape[1]].T, precision=highest)
+    return jnp.dot(offset_onehot(shape[0]), offset_sums[: shape[1]].T, precision=highest)
 
 
 def local(
@@ -992,59 +1054,23 @@
 ):
     seqs = lengths.shape[1]
     width = tokens.shape[2]
-    buckets = bucket_bias.shape[0]
-    far = jnp.stack([bucket_bias[buckets // 2 - 1], bucket_bias[buckets - 1]])
     gains = (gain_attention, gain_feedforward, gain_final)
     weights = (query_weight, key_weight, value_weight, output_weight, widen_weight, narrow_weight)
-    lines = bias_lines(bucket_bias)
-    normed, query, key, value, totals, context, mixed, ffn_in, hidden, output, pooled = run_forward(
-        tokens[0], lengths[0], prefixes[0], far, lines, gains, weights
+    normed, query, key, value, totals, context, mixed, ffn_in, hidden, output, pooled, units = run_forward(
+        batch_size, 0, tokens[0], lengths[0], prefixes[0], bucket_bias, gains, weights
     )
-    pooled = pooled[:, 0]
-    inverse_pool = lax.rsqrt(jnp.sum(pooled * pooled, axis=-1, keepdims=True) + epsilon)
-    unit = pooled * inverse_pool
-    gathered = gather_blocks(unit, batch_size, 0).reshape(2 * batch_size * seqs, width)
-    total_seqs = gathered.shape[0] // 2
-    query_units = gathered[:total_seqs]
-    doc_units = gathered[total_seqs:]
-    scores = score_scale * jnp.dot(query_units, doc_units.T, precision=highest)
-    labels = jnp.arange(total_seqs, dtype=jnp.int32)
-    target = (positives[:, None] == labels[None, :]).astype(jnp.float32)
-    row_peak = jnp.max(scores, axis=1, keepdims=True)
-    row_raised = jnp.exp(scores - row_peak)
-    row_sum = jnp.sum(row_raised, axis=1, keepdims=True)
-    col_peak = jnp.max(scores, axis=0, keepdims=True)
-    col_raised = jnp.exp(scores - col_peak)
-    col_sum = jnp.sum(col_raised, axis=0, keepdims=True)
-    loss_value = (
-        0.5 * jnp.sum(row_peak[:, 0] + jnp.log(row_sum[:, 0]))
-        + 0.5 * jnp.sum(col_peak[0] + jnp.log(col_sum[0]))
-        - jnp.sum(target * scores)
-    )
-    score_grad = 0.5 * row_raised / row_sum + 0.5 * col_raised / col_sum - target
-    tower = lax.axis_index("tower")
-    first_row = lax.axis_index("batch") * seqs
-    my_rows = lax.dynamic_slice_in_dim(score_grad, first_row, seqs, 0)
-    my_cols = lax.dynamic_slice_in_dim(score_grad, first_row, seqs, 1)
-    grad_as_query = score_scale * jnp.dot(my_rows, doc_units, precision=highest)
-    grad_as_doc = score_scale * jnp.dot(my_cols.T, query_units, precision=highest)
-    grad_unit = jnp.where(tower == 0, grad_as_query, grad_as_doc)
-    cubed = inverse_pool * inverse_pool * inverse_pool
-    grad_pooled = inverse_pool * grad_unit - pooled * cubed * jnp.sum(
-        grad_unit * pooled, axis=-1, keepdims=True
-    )
-    branch, pre, attn, context_grad, mixed_grad, feed_gains = run_feed_back(
-        lengths[0], prefixes[0], gains[1:], weights[3:], mixed, hidden, output, grad_pooled[:, None]
+    branch, pre, attn, context_grad, mixed_grad, feed_gains, loss, my_rows = run_feed_back(
+        lengths[0], prefixes[0], gains[1:], weights[3:], mixed, hidden, output, pooled, units, positives
     )
     streamed = (
         hidden, ffn_in, context, normed, branch, pre, attn, query, key, value, context_grad, tokens[0], mixed_grad
     )
-    resident = (totals, lines, gain_attention[None], *weights[:3])
-    sum_narrow, sum_widen, squares, token_gradient, sums = sum_weights(batch_size, 1, lengths[0], far, streamed, feed_gains, resident)
+    resident = (totals, bucket_bias, gain_attention, *weights[:3])
+    sum_narrow, sum_widen, squares, token_gradient, sums = sum_weights(batch_size, 1, lengths[0], bucket_bias, streamed, feed_gains, resident)
     sum_bucket = bucket_sums(sums[8:, : 4 * tile], bucket_bias.shape)
     sum_output, sum_query, sum_key, sum_value = (squares[n * width : (n + 1) * width] for n in range(4))
     return (
-        loss_value,
+        loss[0, 0],
         my_rows,
         token_gradient[None],
         sums[0],

time: 426 us -> 388 us (0.911)
  Pallas kernels: 381 us -> 360 us
  local copies, waits for them, and re-layouts: 30.5 us -> 24.4 us
  other arithmetic: 5.02 us -> 0.01 us
    pallas_call x2 -> x1, Pallas kernels: 93.6 us -> 81 us  [run_forward(): pl.pallas_call(functools.partial(forward_kernel, groups), grid_spec=pltpu...]
    pallas_call x1, Pallas kernels: 46.9 us -> 40.5 us  [run_feed_back(): pl.pallas_call(feed_back_kernel, grid_spec=pltpu.PrefetchScalarGridSpec(n...]
    unnamed x19 -> x16, local copies, waits for them, and re-layouts: 13.2 us -> 13.5 us
where the time goes in v6:
time: 388 us
  Pallas kernels  360 us (93%)
  local copies, waits for them, and re-layouts  24.4 us (6%)
    pallas_call x1, Pallas kernels, sum_weights(): pl.pallas_call(functools.partial(sums_kernel, dims, jobs), out_shape=(jax...  239 us
    pallas_call x1, Pallas kernels, run_forward(): pl.pallas_call(functools.partial(forward_kernel, groups), grid_spec=pltpu...  81 us
    pallas_call x1, Pallas kernels, run_feed_back(): pl.pallas_call(feed_back_kernel, grid_spec=pltpu.PrefetchScalarGridSpec(n...  40.5 us
    unnamed x16, local copies, waits for them, and re-layouts  13.5 us
    slice x1, local copies, waits for them, and re-layouts, local(): squares[n * width:(n + 1) * width]  8.7 us

profile of v6, /device:TPU:0, one launch (start us, length us, event | category | flops | bytes accessed | tf_op | source)
XLA Modules:
  0.0 387.8 jit_solution(14509024611199536752)
XLA Ops:
  0.6 1.4 copy.27.table.bias_ref.refs_1_.refs_17_
  2.0 0.0 copy-start.2
  2.0 81.0 %forward.1 = (bf16[2048,768]{1,0:T(8,128)(2,1)}, bf16[2048,768]{1,0:T(8,128)(2,1)}, bf16[2048,768]{1,0:T(8,128)(2,1)}, bf16[2048,768]{1,0:T(8,128)(2,1)}, f32[4,...) custom-call(s32[4]{0:T(128)} %bitcast.11, ...), custom_call_target="tpu_custom_call" | custom-call | tf_op jit(solution)/shard_map/forward/pallas_call | solution.py:850
  83.1 0.0 copy-done.2
  83.1 0.7 copy.29.positives_ref
  83.8 40.5 %feed_back.1 = (bf16[2048,768]{1,0:T(8,128)(2,1)}, bf16[2048,3072]{1,0:T(8,128)(2,1)}, bf16[2048,768]{1,0:T(8,128)(2,1)}, bf16[2048,768]{1,0:T(8,128)(2,1)}, f32...) custom-call(s32[4]{0:T(128)} %bitcast.12, s32[4]{0:T(128)} %bitcast.15, ...), custom_call_target="tpu_custom_call" | custom-call | tf_op jit(solution)/shard_map/feed_back/pallas_call | solution.py:1002
  124.3 239.0 %sum_weights.1 = (f32[3072,768]{1,0:T(8,128)}, f32[768,3072]{1,0:T(8,128)}, f32[3072,768]{1,0:T(8,128)}, bf16[2048,768]{1,0:T(8,128)(2,1)}, f32[24,768]{1,0:T(8,128)}) custom-call(s32[4]{0:T(128)} %bitcast.13, f32[32,12]{1,0:T(8,128)} %copy.27.table.bias_ref.refs_1_.refs_17_, bf16[2048,3072]{1,0:T(8,128)(2,1)} %get-tuple-element.39.hidden_ref.refs_2_, ...), custom_call_target="tpu_custom_call" | custom-call | tf_op jit(solution)/shard_map/sum_weights/pallas_call | solution.py:636
  363.2 1.5 slice_reduce_fusion
  364.7 0.0 copy-start.1
  364.7 0.0 copy-start
  364.7 8.7 %fusion.36 = (f32[768,768]{1,0:T(8,128)}, f32[768,768]{1,0:T(8,128)}, f32[768,768]{1,0:T(8,128)}, f32[768,768]{1,0:T(8,128)}) fusion(f32[3072,768]{1,0:T(8,128)} %get-tuple-element.60), kind=kLoop, calls=%fused_computation.42 | loop fusion | bytes 18874368 | tf_op jit(solution)/shard_map/slice | solution.py:1071
  373.4 2.3 fusion.11
  375.7 0.0 copy-done.1
  375.7 0.0 slice-start
  375.7 1.7 copy.35
  377.4 0.0 copy-done
  377.4 0.0 slice-start.1
  377.4 0.0 slice-start.2
  377.4 4.8 %copy.36 = f32[768,3072]{1,0:T(8,128)} copy(f32[768,3072]{1,0:T(8,128)S(1)} %copy-done) | data formatting | bytes 18874368
  382.2 0.0 slice-done
  382.2 1.7 slice-done.1
  383.8 0.2 slice-done.2
  384.1 3.7 copy.37
  (3 shorter events, 0.0 us)
Async XLA Ops:
  2.0 81.0 %copy-start.2 = (s32[64]{0:T(128)S(1)}, s32[64]{0:T(128)}, u32[]{:S(2)}) copy-start(s32[64]{0:T(128)} %param.17) | copy-start | bytes 772
  364.7 11.0 %copy-start.1 = (bf16[2048,768]{1,0:T(8,128)(2,1)S(1)}, bf16[2048,768]{1,0:T(8,128)(2,1)}, u32[]{:S(2)}) copy-start(bf16[2048,768]{1,0:T(8,128)(2,1)} %get-tuple-element.58) | copy-start | bytes 9437188
  364.7 12.7 %copy-start = (f32[768,3072]{1,0:T(8,128)S(1)}, f32[768,3072]{1,0:T(8,128)}, u32[]{:S(2)}) copy-start(f32[768,3072]{1,0:T(8,128)} %get-tuple-element.93) | copy-start | bytes 28311556
  375.7 6.5 %slice-start = ((s8[9437184]{0:T(1024)(128)(4,1)}), s8[4194304]{0:T(1024)(128)(4,1)S(1)}, s32[]{:S(2)}) async-start(s8[9437184]{0:T(1024)(128)(4,1)} %bitcast.8), calls=%async_computation | async-start | bytes 8388608
  377.4 6.5 %slice-start.1 = ((s8[9437184]{0:T(1024)(128)(4,1)}), s8[4194304]{0:T(1024)(128)(4,1)S(1)}, s32[]{:S(2)}) async-start(s8[9437184]{0:T(1024)(128)(4,1)} %bitcast.8), calls=%async_computation.1 | async-start | bytes 8388608
  377.4 6.7 %slice-start.2 = ((s8[9437184]{0:T(1024)(128)(4,1)}), s8[1048576]{0:T(1024)(128)(4,1)S(1)}, s32[]{:S(2)}) async-start(s8[9437184]{0:T(1024)(128)(4,1)} %bitcast.8), calls=%async_computation.2 | async-start | bytes 2097152

commit v7 on v6

--- a/solution.py
+++ b/solution.py
@@ -241,7 +241,7 @@
 
     held, spread_held = acc.shape[0], full.shape[0]
     width = narrow_out.shape[1]
-    heads = table.shape[1]
+    heads = table.shape[0]
     seqs = lengths.shape[0]
     slot_len = tokens.shape[0] // seqs
     pair = 2 * width // heads
@@ -319,7 +319,7 @@
             lambda: pltpu.make_async_copy(attn, right.at[place_right], right_sem.at[place_right]).wait()
         )
         pl.when(job + 1 < jobs)(lambda: load(job + 1))
-        part[slot] = lax.dot_general(
+        part[lax.rem(job, 3)] = lax.dot_general(
             left[slot], right[place_right], (((0,), (0,)), ((), ())), preferred_element_type=jnp.float32
         )
 
@@ -339,7 +339,7 @@
         )
         base = unit * half
         if step == 0:
-            src = part.at[lax.rem(job, 2), pl.ds(pl.multiple_of(unit * unit_rows + (1 - tower) * half, 8), half)]
+            src = part.at[lax.rem(job, 3), pl.ds(pl.multiple_of(unit * unit_rows + (1 - tower) * half, 8), half)]
             dst = mate_in.at[turn, pl.ds(base, half)]
             return pltpu.make_async_remote_copy(src, dst, device_id=(1 - tower, batch), **sems), None, None
         count = counts[unit]
@@ -404,7 +404,7 @@
             copy.wait_recv()
             if step == 0:
                 own = pl.ds(pl.multiple_of(unit * unit_rows + tower * half, 8), half)
-                acc[place_in, pl.ds(base, half)] = part[lax.rem(job, 2), own] + mate_in[turn, pl.ds(base, half)]
+                acc[place_in, pl.ds(base, half)] = part[lax.rem(job, 3), own] + mate_in[turn, pl.ds(base, half)]
             elif step <= counts[unit]:
                 item = add[step - 1]
                 rows = pl.ds(pl.multiple_of(base + item["keep"], 8), item["rows"])
@@ -459,7 +459,8 @@
             small_copy(turn - 1).wait()
             total = small_own[turn - 1] + small_in[turn - 1]
             if turn == len(turns):
-                small_out[...] = total
+                small_out[0:8] = total[0:8]
+                small_out[8:, 0:16] = exact_dot(offset_onehot(table.shape[1]), total[8:24, : 4 * tile], 1, 1)
             else:
                 small_own[turn] = total
         if turn < len(turns):
@@ -578,40 +579,54 @@
     load(0)
     heads_load(0, True)
     token_load(0, True)
-    spread_bias(bias_ref, near_ref, heads)
-    near_sums[...] = jnp.zeros_like(near_sums)
-    far_sums[...] = jnp.zeros_like(far_sums)
     small_own[0, 0:8, :] = small[...]
+    compute(jnp.int32(0))
     pl.semaphore_wait(barrier, len(mates))
 
     last_attend = jobs - 3 * (width // job_rows) - 1
+    first_token = last_attend + 1
+    first_attend = 5
     first_small = slots - 1 - len(turns)
-    first_token = first_small - 1 - seqs
+
+    def prepare():
+        spread_bias(bias_ref, near_ref, heads)
+        near_sums[...] = jnp.zeros_like(near_sums)
+        far_sums[...] = jnp.zeros_like(far_sums)
+
+    def products(time):
+        pl.when(time < jobs)(functools.partial(compute, time))
+        pl.when(time == 2)(prepare)
+
+    def attention(time):
+        past = jnp.maximum(time - first_attend, 0)
+        span = last_attend - first_attend
+        begin = jnp.minimum(past * tasks // span, tasks)
+        end = jnp.where(time < first_attend, 0, jnp.minimum((past + 1) * tasks // span, tasks))
+        lax.fori_loop(begin, end, attend, 0)
+
+    def token_part(time):
+        seq = time - first_token
+        pl.when(jnp.logical_and(seq >= 0, seq < seqs))(functools.partial(token_task, seq))
+        pl.when(time == first_token + seqs)(close)
+        for turn in range(len(turns) + 1):
+            pl.when(time == first_small + turn)(functools.partial(small_turn, turn))
 
     def slot(time, carry):
-        for unit in range(len(orders)):
+        for unit, work in ((2, products), (0, attention), (1, token_part)):
             for step in range(steps[unit] + 1):
                 job = time - 1 - step
                 pl.when(jnp.logical_and(job >= 0, job < jobs))(functools.partial(advance, unit, step, job))
-        for turn in range(len(turns) + 1):
-            pl.when(time == first_small + turn)(functools.partial(small_turn, turn))
-        begin = jnp.minimum(time * tasks // last_attend, tasks)
-        end = jnp.minimum((time + 1) * tasks // last_attend, tasks)
-        pl.when(time < jobs)(functools.partial(compute, time))
-        lax.fori_loop(begin, end, attend, 0)
-        seq = time - first_token
-        pl.when(jnp.logical_and(seq >= 0, seq < seqs))(functools.partial(token_task, seq))
-        pl.when(time == first_small - 1)(close)
+            work(time)
         return carry
 
-    lax.fori_loop(0, slots, slot, 0)
+    lax.fori_loop(1, slots, slot, 0)
 
 
 def sum_weights(batch_size, collective, lengths, bucket_bias, streamed, small, resident):
     hidden, normed = streamed[0], streamed[3]
     tokens, width = normed.shape
     seqs = lengths.shape[0]
-    heads = bucket_bias.shape[1]
+    heads = bucket_bias.shape[0]
     slot_len = tokens // seqs
     pair = 2 * width // heads
     total = 2 * hidden.shape[1] + 4 * width
@@ -640,14 +655,14 @@
             jax.ShapeDtypeStruct((width, hidden.shape[1]), full),
             jax.ShapeDtypeStruct((4 * width, width), full),
             jax.ShapeDtypeStruct((tokens, width), low),
-            jax.ShapeDtypeStruct((lines, width), full),
+            jax.ShapeDtypeStruct((8 + bucket_bias.shape[1], width), full),
         ),
         in_specs=[in_smem] * 2 + [anywhere] * len(streamed) + [in_vmem] * (1 + len(resident)),
         out_specs=(anywhere, anywhere, anywhere, anywhere, in_vmem),
         scratch_shapes=[
             pltpu.VMEM((2, tokens, job_rows), low),
             pltpu.VMEM((2, tokens, width), low),
-            pltpu.VMEM((2, job_rows, width), full),
+            pltpu.VMEM((3, job_rows, width), full),
             pltpu.VMEM((steps // 2, 3 * half, width), full),
             pltpu.VMEM((steps, 3 * half, width), full),
             pltpu.VMEM((4, 3 * half, width), full),
@@ -696,18 +711,15 @@
 
 
 def spread_bias(bias_ref, near_ref, heads):
-    lines = lax.dot_general(
-        bias_ref[...], offset_onehot(bias_ref.shape[0]), (((0,), (0,)), ((), ())),
-        precision=highest, preferred_element_type=jnp.float32,
-    )
+    lines = exact_dot(bias_ref[...], offset_onehot(bias_ref.shape[1]), 1, 0)
     for head in range(heads):
         line = jnp.broadcast_to(lines[head : head + 1, :], (tile, 4 * tile))
         near_ref[head] = pltpu.roll(line, 0, 1, stride=1, stride_axis=0)[:, :near]
 
 
 def far_bias(table, head):
-    buckets = table.shape[0]
-    return table[buckets // 2 - 1, head], table[buckets - 1, head]
+    buckets = table.shape[1]
+    return table[head, buckets // 2 - 1], table[head, buckets - 1]
 
 
 def bias_tile(near_ref, head, row_block, column_block, low_far, high_far):
@@ -736,7 +748,7 @@
     near_ref, widen, narrow, weight_sem, slots, block_ref, send_sem, recv_sem, mate_sem,
 ):
     seq = pl.program_id(0)
-    heads = table.shape[1]
+    heads = table.shape[0]
     slot_len, width = x_ref.shape
     blocks = slot_len // tile
     pair = 2 * width // heads
@@ -828,7 +840,7 @@
     rows, width = tokens.shape
     seqs = lengths.shape[0]
     slot_len = rows // seqs
-    heads = bucket_bias.shape[1]
+    heads = bucket_bias.shape[0]
     wq, wk, wv, wo, widen, narrow = weights
     gain_a, gain_f, gain_z = gains
     ff = widen.shape[1]
@@ -1031,10 +1043,6 @@
     )
 
 
-def bucket_sums(offset_sums, shape):
-    return jnp.dot(offset_onehot(shape[0]), offset_sums[: shape[1]].T, precision=highest)
-
-
 def local(
     batch_size,
     tokens,
@@ -1057,7 +1065,7 @@
     gains = (gain_attention, gain_feedforward, gain_final)
     weights = (query_weight, key_weight, value_weight, output_weight, widen_weight, narrow_weight)
     normed, query, key, value, totals, context, mixed, ffn_in, hidden, output, pooled, units = run_forward(
-        batch_size, 0, tokens[0], lengths[0], prefixes[0], bucket_bias, gains, weights
+        batch_size, 0, tokens[0], lengths[0], prefixes[0], bucket_bias.T, gains, weights
     )
     branch, pre, attn, context_grad, mixed_grad, feed_gains, loss, my_rows = run_feed_back(
         lengths[0], prefixes[0], gains[1:], weights[3:], mixed, hidden, output, pooled, units, positives
@@ -1065,9 +1073,9 @@
     streamed = (
         hidden, ffn_in, context, normed, branch, pre, attn, query, key, value, context_grad, tokens[0], mixed_grad
     )
-    resident = (totals, bucket_bias, gain_attention, *weights[:3])
-    sum_narrow, sum_widen, squares, token_gradient, sums = sum_weights(batch_size, 1, lengths[0], bucket_bias, streamed, feed_gains, resident)
-    sum_bucket = bucket_sums(sums[8:, : 4 * tile], bucket_bias.shape)
+    resident = (totals, bucket_bias.T, gain_attention, *weights[:3])
+    sum_narrow, sum_widen, squares, token_gradient, sums = sum_weights(batch_size, 1, lengths[0], bucket_bias.T, streamed, feed_gains, resident)
+    sum_bucket = sums[8:, : bucket_bias.shape[1]]
     sum_output, sum_query, sum_key, sum_value = (squares[n * width : (n + 1) * width] for n in range(4))
     return (
         loss[0, 0],

time: 388 us -> 378 us (0.974)
  Pallas kernels: 360 us -> 351 us
    pallas_call x1, Pallas kernels: 239 us -> 229 us  [sum_weights(): pl.pallas_call(functools.partial(sums_kernel, dims, jobs), out_shape=(jax...]
    unnamed x16 -> x14, local copies, waits for them, and re-layouts: 13.5 us -> 15.4 us
where the time goes in v7:
time: 378 us; the launch traced here: 377 us
  Pallas kernels  351 us (93%)
  local copies, waits for them, and re-layouts  26.1 us (7%)
    pallas_call x1, Pallas kernels, sum_weights(): pl.pallas_call(functools.partial(sums_kernel, dims, jobs), out_shape=(jax...  229 us
    pallas_call x1, Pallas kernels, run_forward(): pl.pallas_call(functools.partial(forward_kernel, groups), grid_spec=pltpu...  80.6 us
    pallas_call x1, Pallas kernels, run_feed_back(): pl.pallas_call(feed_back_kernel, grid_spec=pltpu.PrefetchScalarGridSpec(n...  40.5 us
    unnamed x14, local copies, waits for them, and re-layouts  15.4 us
    slice x1, local copies, waits for them, and re-layouts, local(): squares[n * width:(n + 1) * width]  7.73 us

profile of v7, /device:TPU:0, one launch (start us, length us, event | category | flops | bytes accessed | tf_op | source)
XLA Modules:
  0.0 377.3 jit_solution(8549133976051064520)
XLA Ops:
  0.6 0.0 copy-start.1
  0.7 80.6 %forward.1 = (bf16[2048,768]{1,0:T(8,128)(2,1)}, bf16[2048,768]{1,0:T(8,128)(2,1)}, bf16[2048,768]{1,0:T(8,128)(2,1)}, bf16[2048,768]{1,0:T(8,128)(2,1)}, f32[4,...) custom-call(s32[4]{0:T(128)} %bitcast.16, ...), custom_call_target="tpu_custom_call" | custom-call | tf_op jit(solution)/shard_map/forward/pallas_call | solution.py:862
  81.3 0.0 copy-done.1
  81.3 0.7 copy.27.positives_ref
  82.0 40.5 %feed_back.1 = (bf16[2048,768]{1,0:T(8,128)(2,1)}, bf16[2048,3072]{1,0:T(8,128)(2,1)}, bf16[2048,768]{1,0:T(8,128)(2,1)}, bf16[2048,768]{1,0:T(8,128)(2,1)}, f32...) custom-call(s32[4]{0:T(128)} %bitcast.17, s32[4]{0:T(128)} %bitcast.20, ...), custom_call_target="tpu_custom_call" | custom-call | tf_op jit(solution)/shard_map/feed_back/pallas_call | solution.py:1014
  122.5 229.5 %sum_weights.1 = (f32[3072,768]{1,0:T(8,128)}, f32[768,3072]{1,0:T(8,128)}, f32[3072,768]{1,0:T(8,128)}, bf16[2048,768]{1,0:T(8,128)(2,1)}, f32[40,768]{1,0:T(8,128)}) custom-call(s32[4]{0:T(128)} %bitcast.18, f32[12,32]{1,0:T(8,128)} %bitcast.14, bf16[2048,3072]{1,0:T(8,128)(2,1)} %get-tuple-element.39.hidden_ref.refs_2_, ...), custom_call_target="tpu_custom_call" | custom-call | tf_op jit(solution)/shard_map/sum_weights/pallas_call | solution.py:651
  352.0 1.5 slice_reduce_fusion
  353.4 0.0 copy-start
  353.4 7.7 %fusion = (f32[768,768]{1,0:T(8,128)}, f32[768,768]{1,0:T(8,128)}, f32[768,768]{1,0:T(8,128)}, f32[768,768]{1,0:T(8,128)}) fusion(f32[3072,768]{1,0:T(8,128)} %get-tuple-element.60), kind=kLoop, calls=%fused_computation.3 | loop fusion | bytes 18874368 | tf_op jit(solution)/shard_map/slice | solution.py:1079
  361.2 0.7 slice.29
  361.9 0.7 copy.28
  362.6 0.0 copy-done
  362.6 0.0 slice-start
  362.6 1.7 copy.32
  364.2 0.0 slice-start.1
  364.2 0.0 slice-start.2
  364.2 9.3 %copy.33 = f32[768,3072]{1,0:T(8,128)} copy(f32[768,3072]{1,0:T(8,128)} %get-tuple-element.106) | data formatting | bytes 18874368
  373.6 0.0 slice-done
  373.6 0.0 slice-done.1
  373.6 0.0 slice-done.2
  373.6 3.7 copy.34
  (1 shorter events, 0.0 us)
Async XLA Ops:
  0.6 80.6 %copy-start.1 = (s32[64]{0:T(128)S(1)}, s32[64]{0:T(128)}, u32[]{:S(2)}) copy-start(s32[64]{0:T(128)} %param.17) | copy-start | bytes 772
  353.4 9.1 %copy-start = (bf16[2048,768]{1,0:T(8,128)(2,1)S(1)}, bf16[2048,768]{1,0:T(8,128)(2,1)}, u32[]{:S(2)}) copy-start(bf16[2048,768]{1,0:T(8,128)(2,1)} %get-tuple-element.58) | copy-start | bytes 9437188
  362.6 11.0 %slice-start = ((s8[9437184]{0:T(1024)(128)(4,1)}), s8[4194304]{0:T(1024)(128)(4,1)S(1)}, s32[]{:S(2)}) async-start(s8[9437184]{0:T(1024)(128)(4,1)} %bitcast.9), calls=%async_computation | async-start | bytes 8388608
  364.2 9.3 %slice-start.1 = ((s8[9437184]{0:T(1024)(128)(4,1)}), s8[4194304]{0:T(1024)(128)(4,1)S(1)}, s32[]{:S(2)}) async-start(s8[9437184]{0:T(1024)(128)(4,1)} %bitcast.9), calls=%async_computation.1 | async-start | bytes 8388608
  364.2 9.3 %slice-start.2 = ((s8[9437184]{0:T(1024)(128)(4,1)}), s8[1048576]{0:T(1024)(128)(4,1)S(1)}, s32[]{:S(2)}) async-start(s8[9437184]{0:T(1024)(128)(4,1)} %bitcast.9), calls=%async_computation.2 | async-start | bytes 2097152

commit v8 on v7

--- a/solution.py
+++ b/solution.py
@@ -460,7 +460,7 @@
             total = small_own[turn - 1] + small_in[turn - 1]
             if turn == len(turns):
                 small_out[0:8] = total[0:8]
-                small_out[8:, 0:16] = exact_dot(offset_onehot(table.shape[1]), total[8:24, : 4 * tile], 1, 1)
+                small_out[8:, 0 : table.shape[1]] = exact_dot(total[8:24, : 4 * tile], offset_onehot(table.shape[1]), 1, 1)
             else:
                 small_own[turn] = total
         if turn < len(turns):
@@ -655,7 +655,7 @@
             jax.ShapeDtypeStruct((width, hidden.shape[1]), full),
             jax.ShapeDtypeStruct((4 * width, width), full),
             jax.ShapeDtypeStruct((tokens, width), low),
-            jax.ShapeDtypeStruct((8 + bucket_bias.shape[1], width), full),
+            jax.ShapeDtypeStruct((24, width), full),
         ),
         in_specs=[in_smem] * 2 + [anywhere] * len(streamed) + [in_vmem] * (1 + len(resident)),
         out_specs=(anywhere, anywhere, anywhere, anywhere, in_vmem),
@@ -1043,6 +1043,52 @@
     )
 
 
+def settle_kernel(count, sums, *refs):
+    for source, target in zip(refs[:count], refs[count : 2 * count]):
+        target[...] = source[...]
+    *gains, bucket = refs[2 * count :]
+
+    def small():
+        for index, gain in enumerate(gains):
+            gain[...] = sums[index, :]
+        heads, buckets = bucket.shape
+        bucket[...] = sums[8 : 8 + heads, 0:buckets]
+
+    pl.when(pl.program_id(0) == 0)(small)
+
+
+def settle(narrow, widen, squares, token, sums, table):
+    width = widen.shape[0]
+    steps = 8
+
+    def rows(array, parts=1, first=0):
+        block = array.shape[0] // parts // steps
+        return pl.BlockSpec((block, array.shape[1]), lambda n: (first * steps + n, 0))
+
+    square = jax.ShapeDtypeStruct((width, width), squares.dtype)
+    return pl.pallas_call(
+        functools.partial(settle_kernel, 7),
+        grid=(steps,),
+        in_specs=[
+            pl.BlockSpec(sums.shape, lambda n: (0, 0)), rows(narrow), rows(widen), *(rows(squares, 4, n) for n in range(4)), rows(token),
+        ],
+        out_specs=[
+            rows(narrow), rows(widen), *(rows(squares, 4) for n in range(4)), rows(token),
+            *(pl.BlockSpec((width,), lambda n: (0,)) for _ in range(3)), pl.BlockSpec(table, lambda n: (0, 0)),
+        ],
+        out_shape=(
+            jax.ShapeDtypeStruct(narrow.shape, narrow.dtype),
+            jax.ShapeDtypeStruct(widen.shape, widen.dtype),
+            square, square, square, square,
+            jax.ShapeDtypeStruct(token.shape, token.dtype),
+            *(jax.ShapeDtypeStruct((width,), sums.dtype) for _ in range(3)),
+            jax.ShapeDtypeStruct(table, sums.dtype),
+        ),
+        compiler_params=pltpu.CompilerParams(vmem_limit_bytes=66500000),
+        name="settle",
+    )(sums, narrow, widen, squares, squares, squares, squares, token)
+
+
 def local(
     batch_size,
     tokens,
@@ -1075,22 +1121,24 @@
     )
     resident = (totals, bucket_bias.T, gain_attention, *weights[:3])
     sum_narrow, sum_widen, squares, token_gradient, sums = sum_weights(batch_size, 1, lengths[0], bucket_bias.T, streamed, feed_gains, resident)
-    sum_bucket = sums[8:, : bucket_bias.shape[1]]
-    sum_output, sum_query, sum_key, sum_value = (squares[n * width : (n + 1) * width] for n in range(4))
+    (
+        sum_narrow, sum_widen, sum_output, sum_query, sum_key, sum_value, token_gradient,
+        sum_attention, sum_feedforward, sum_final, sum_bucket,
+    ) = settle(sum_narrow, sum_widen, squares, token_gradient, sums, bucket_bias.shape[::-1])
     return (
         loss[0, 0],
         my_rows,
         token_gradient[None],
-        sums[0],
+        sum_attention,
         sum_query,
         sum_key,
         sum_value,
         sum_output,
-        sum_bucket,
-        sums[1],
+        sum_bucket.T,
+        sum_feedforward,
         sum_widen,
         sum_narrow,
-        sums[2],
+        sum_final,
     )
 
 

time: 378 us -> 374 us (0.989)
  local copies, waits for them, and re-layouts: 26.1 us -> 0.71 us
  Pallas kernels: 351 us -> 373 us
    pallas_call x0 -> x1, Pallas kernels: none -> 22 us  [settle(): pl.pallas_call(functools.partial(settle_kernel, 7), grid=(steps,), in_spe...]
    unnamed x14 -> x2, local copies, waits for them, and re-layouts: 15.4 us -> 0.01 us
    slice x3 -> x0, local copies, waits for them, and re-layouts: 9.93 us -> none  [the longest x1 7.73 us: local(): squares[n * width:(n + 1) * width]]
where the time goes in v8:
time: 374 us
  Pallas kernels  373 us (100%)
    pallas_call x1, Pallas kernels, sum_weights(): pl.pallas_call(functools.partial(sums_kernel, dims, jobs), out_shape=(jax...  229 us
    pallas_call x1, Pallas kernels, run_forward(): pl.pallas_call(functools.partial(forward_kernel, groups), grid_spec=pltpu...  80.6 us
    pallas_call x1, Pallas kernels, run_feed_back(): pl.pallas_call(feed_back_kernel, grid_spec=pltpu.PrefetchScalarGridSpec(n...  40.5 us
    pallas_call x1, Pallas kernels, settle(): pl.pallas_call(functools.partial(settle_kernel, 7), grid=(steps,), in_spe...  22 us

profile of v8, /device:TPU:0, one launch (start us, length us, event | category | flops | bytes accessed | tf_op | source)
XLA Modules:
  0.0 374.1 jit_solution(6063112359132235127)
XLA Ops:
  0.6 0.0 copy-start
  0.7 80.6 %forward.1 = (bf16[2048,768]{1,0:T(8,128)(2,1)}, bf16[2048,768]{1,0:T(8,128)(2,1)}, bf16[2048,768]{1,0:T(8,128)(2,1)}, bf16[2048,768]{1,0:T(8,128)(2,1)}, f32[4,...) custom-call(s32[4]{0:T(128)} %bitcast.14, ...), custom_call_target="tpu_custom_call" | custom-call | tf_op jit(solution)/shard_map/forward/pallas_call | solution.py:862
  81.3 0.0 copy-done
  81.3 0.7 copy.27.positives_ref
  82.0 40.5 %feed_back.1 = (bf16[2048,768]{1,0:T(8,128)(2,1)}, bf16[2048,3072]{1,0:T(8,128)(2,1)}, bf16[2048,768]{1,0:T(8,128)(2,1)}, bf16[2048,768]{1,0:T(8,128)(2,1)}, f32...) custom-call(s32[4]{0:T(128)} %bitcast.15, s32[4]{0:T(128)} %bitcast.18, ...), custom_call_target="tpu_custom_call" | custom-call | tf_op jit(solution)/shard_map/feed_back/pallas_call | solution.py:1014
  122.5 229.4 %sum_weights.1 = (f32[3072,768]{1,0:T(8,128)}, f32[768,3072]{1,0:T(8,128)}, f32[3072,768]{1,0:T(8,128)}, bf16[2048,768]{1,0:T(8,128)(2,1)}, f32[24,768]{1,0:T(8,128)}) custom-call(s32[4]{0:T(128)} %bitcast.16, f32[12,32]{1,0:T(8,128)} %bitcast.12, bf16[2048,3072]{1,0:T(8,128)(2,1)} %get-tuple-element.50.hidden_ref.refs_2_, ...), custom_call_target="tpu_custom_call" | custom-call | tf_op jit(solution)/shard_map/sum_weights/pallas_call | solution.py:651
  351.9 22.0 %settle.1 = (f32[3072,768]{1,0:T(8,128)}, f32[768,3072]{1,0:T(8,128)}, f32[768,768]{1,0:T(8,128)}, f32[768,768]{1,0:T(8,128)}, f32[768,768]{1,0:T(8,128)}, /*ind...) custom-call(f32[24,768]{1,0:T(8,128)} %get-tuple-element.69.sums, ...), custom_call_target="tpu_custom_call" | custom-call | tf_op jit(solution)/shard_map/settle/pallas_call | solution.py:1069
Async XLA Ops:
  0.6 80.6 %copy-start = (s32[64]{0:T(128)S(1)}, s32[64]{0:T(128)}, u32[]{:S(2)}) copy-start(s32[64]{0:T(128)} %param.17) | copy-start | bytes 772

commit v9 on v8

--- a/solution.py
+++ b/solution.py
@@ -1059,7 +1059,7 @@
 
 def settle(narrow, widen, squares, token, sums, table):
     width = widen.shape[0]
-    steps = 8
+    steps = 16
 
     def rows(array, parts=1, first=0):
         block = array.shape[0] // parts // steps

time: 374 us -> 378 us (1.011)
  no operation moved by 1% of the time
where the time goes in v9:
time: 378 us
  Pallas kernels  376 us (99%)
    pallas_call x1, Pallas kernels, sum_weights(): pl.pallas_call(functools.partial(sums_kernel, dims, jobs), out_shape=(jax...  229 us
    pallas_call x1, Pallas kernels, run_forward(): pl.pallas_call(functools.partial(forward_kernel, groups), grid_spec=pltpu...  80.6 us
    pallas_call x1, Pallas kernels, run_feed_back(): pl.pallas_call(feed_back_kernel, grid_spec=pltpu.PrefetchScalarGridSpec(n...  40.5 us
    pallas_call x1, Pallas kernels, settle(): pl.pallas_call(functools.partial(settle_kernel, 7), grid=(steps,), in_spe...  25.8 us

profile of v9, /device:TPU:0, one launch (start us, length us, event | category | flops | bytes accessed | tf_op | source)
XLA Modules:
  0.0 377.8 jit_solution(7953383129302636193)
XLA Ops:
  0.6 0.0 copy-start
  0.7 80.6 %forward.1 = (bf16[2048,768]{1,0:T(8,128)(2,1)}, bf16[2048,768]{1,0:T(8,128)(2,1)}, bf16[2048,768]{1,0:T(8,128)(2,1)}, bf16[2048,768]{1,0:T(8,128)(2,1)}, f32[4,...) custom-call(s32[4]{0:T(128)} %bitcast.14, ...), custom_call_target="tpu_custom_call" | custom-call | tf_op jit(solution)/shard_map/forward/pallas_call | solution.py:862
  81.3 0.0 copy-done
  81.3 0.7 copy.27.positives_ref
  82.0 40.5 %feed_back.1 = (bf16[2048,768]{1,0:T(8,128)(2,1)}, bf16[2048,3072]{1,0:T(8,128)(2,1)}, bf16[2048,768]{1,0:T(8,128)(2,1)}, bf16[2048,768]{1,0:T(8,128)(2,1)}, f32...) custom-call(s32[4]{0:T(128)} %bitcast.15, s32[4]{0:T(128)} %bitcast.18, ...), custom_call_target="tpu_custom_call" | custom-call | tf_op jit(solution)/shard_map/feed_back/pallas_call | solution.py:1014
  122.5 229.4 %sum_weights.1 = (f32[3072,768]{1,0:T(8,128)}, f32[768,3072]{1,0:T(8,128)}, f32[3072,768]{1,0:T(8,128)}, bf16[2048,768]{1,0:T(8,128)(2,1)}, f32[24,768]{1,0:T(8,128)}) custom-call(s32[4]{0:T(128)} %bitcast.16, f32[12,32]{1,0:T(8,128)} %bitcast.12, bf16[2048,3072]{1,0:T(8,128)(2,1)} %get-tuple-element.50.hidden_ref.refs_2_, ...), custom_call_target="tpu_custom_call" | custom-call | tf_op jit(solution)/shard_map/sum_weights/pallas_call | solution.py:651
  351.9 25.8 %settle.1 = (f32[3072,768]{1,0:T(8,128)}, f32[768,3072]{1,0:T(8,128)}, f32[768,768]{1,0:T(8,128)}, f32[768,768]{1,0:T(8,128)}, f32[768,768]{1,0:T(8,128)}, /*ind...) custom-call(f32[24,768]{1,0:T(8,128)} %get-tuple-element.69.sums, ...), custom_call_target="tpu_custom_call" | custom-call | tf_op jit(solution)/shard_map/settle/pallas_call | solution.py:1069
Async XLA Ops:
  0.6 80.6 %copy-start = (s32[64]{0:T(128)S(1)}, s32[64]{0:T(128)}, u32[]{:S(2)}) copy-start(s32[64]{0:T(128)} %param.17) | copy-start | bytes 772
